TPU v7x, 32 devices: a whole 2x2x4 slice. The times are simulated.
32 devices in a mesh: ctx: 4 (over x, core), head: 4 (over z), seq: 2 (over y).
Axes of the slice: x: 2, y: 2, z: 4, core: 2. Of those that a mesh axis runs over, the one named last changes fastest.
Arguments:
- attn_query: bfloat16 [4096, 5120], P(('seq', 'ctx'), 'head'), parts along dimension 0, may hold values from -7.5 to 7.5
- attn_key: bfloat16 [4096, 5120], P(('seq', 'ctx'), 'head'), parts along dimension 0, may hold values from -7.5 to 7.5
- attn_value: bfloat16 [4096, 5120], P(('seq', 'ctx'), 'head'), parts along dimension 0, may hold values from -6 to 6
- fw_query: bfloat16 [4096, 5120], P(('seq', 'ctx'), 'head'), parts along dimension 0, may hold values from -6 to 6
- fw_key: bfloat16 [4096, 5120], P(('seq', 'ctx'), 'head'), parts along dimension 0, may hold values from -6 to 6
- fw_value: bfloat16 [4096, 5120], P(('seq', 'ctx'), 'head'), parts along dimension 0, may hold values from -6 to 6
- fw_rate: float32 [4096, 8], P(('seq', 'ctx'), 'head'), parts along dimension 0, may hold values from 0.005 to 0.05
- fast_weights: float32 [1280, 15360], P(('seq', 'ctx'), 'head'), parts along dimension 0, may hold values from -50 to 50
- momentum: float32 [1280, 15360], P(('seq', 'ctx'), 'head'), parts along dimension 0, may hold values from -6 to 6
Outputs:
- attn_out: bfloat16 [4096, 5120], P(('seq', 'ctx'), 'head'), parts along dimension 0
- fw_out: bfloat16 [4096, 5120], P(('seq', 'ctx'), 'head'), parts along dimension 0
- new_weights: float32 [1280, 15360], P(('seq', 'ctx'), 'head'), parts along dimension 0
- new_momentum: float32 [1280, 15360], P(('seq', 'ctx'), 'head'), parts along dimension 0
There are 2 independent parts, one for each index of `seq`. A program takes and returns all parts, laid end to end along the dimension named above; each array names one. Nothing has to cross between parts.
All inputs are finite; a program needn't handle non-finite values.
Results may differ from a plain program's by a relative error of at most 0.014.
Values may be sent and summed in bfloat16 or wider, within the bound.
No kernel may reach another device: no remote copies, remote signals or barrier semaphores. Data moves between devices by JAX's collectives and lax.ppermute only.
A program may use at most 128 MiB of HBM per device.

v0:
```python
import jax
import jax.numpy as jnp
from jax import lax
from jax.sharding import PartitionSpec as P

HD = 128
FD = 640
WINDOW = 1024


EPSILON = 1e-06
DECAY = 0.9


def from_behind(shard, axis, by):
    devices = lax.axis_size(axis)
    pairs = [(i, i + by) for i in range(devices) if 0 <= i + by < devices]
    return lax.ppermute(shard, axis, pairs)


def local_attention(query_rows, key_rows, value_rows, first_token):
    row_count, width_all = query_rows.shape
    head_count = width_all // HD
    block_rows = min(512, row_count)
    query_all = query_rows.reshape(row_count, head_count, HD)
    key_all = key_rows.reshape(-1, head_count, HD)
    value_all = value_rows.reshape(-1, head_count, HD)
    score_scale = HD ** (-0.5)
    scores = (
        jnp.einsum("qhd,khd->hqk", query_all, key_all, preferred_element_type=jnp.float32)
        * score_scale
    )
    row_index = jnp.arange(block_rows, dtype=jnp.int32)[:, None]
    key_index = jnp.arange(WINDOW + block_rows, dtype=jnp.int32)[None, :]
    allowed = (
        (key_index > row_index)
        & (key_index <= row_index + WINDOW)
        & (first_token + 0 - WINDOW + key_index >= 0)
    )
    scores = jnp.where(allowed[None], scores, -jnp.inf)
    highest = jnp.max(scores, axis=2, keepdims=True)
    exponent = jnp.exp(scores - highest)
    denominator = jnp.sum(exponent, axis=2)
    prob_low = exponent.astype(jnp.bfloat16)
    mixed = jnp.einsum("hqk,khd->qhd", prob_low, value_all, preferred_element_type=jnp.float32)
    outputs = (mixed / jnp.transpose(denominator)[:, :, None]).astype(jnp.bfloat16)
    return outputs.reshape(row_count, width_all)


def local_grads(gate_pre, up_pre, back_hidden):
    sigmoid_gate = jax.nn.sigmoid(gate_pre)
    gate_silu = gate_pre * sigmoid_gate
    hidden = (gate_silu * up_pre).astype(jnp.bfloat16)
    gate_grad = (
        back_hidden * up_pre * sigmoid_gate * (1.0 + gate_pre * (1.0 - sigmoid_gate))
    ).astype(jnp.bfloat16)
    up_grad = (back_hidden * gate_silu).astype(jnp.bfloat16)
    return (hidden, gate_grad, up_grad)


def renormalize(weights, moved):
    shape_split = (weights.shape[0], -1, FD)
    before_sq = jnp.mean(jnp.square(weights.reshape(shape_split)), axis=2, keepdims=True)
    after_sq = jnp.mean(jnp.square(moved.reshape(shape_split)), axis=2, keepdims=True)
    factor = jnp.sqrt(before_sq + EPSILON) * lax.rsqrt(after_sq + EPSILON)
    return (moved.reshape(shape_split) * factor).reshape(moved.shape)


def apply_query(weights_low, queries):
    inv_root = FD ** (-0.5)
    query_gate = (
        jnp.einsum("td,hd->th", queries, weights_low[:, :FD], preferred_element_type=jnp.float32)
        * inv_root
    )
    query_up = (
        jnp.einsum(
            "td,hd->th", queries, weights_low[:, FD : 2 * FD], preferred_element_type=jnp.float32
        )
        * inv_root
    )
    query_hidden = (query_gate * jax.nn.sigmoid(query_gate) * query_up).astype(jnp.bfloat16)
    result = (
        jnp.einsum(
            "th,rh->tr", query_hidden, weights_low[:, 2 * FD :], preferred_element_type=jnp.float32
        )
        * inv_root
    )
    return result.astype(jnp.bfloat16)


def per_device(
    attn_query, attn_key, attn_value, fw_query, fw_key, fw_value, fw_rate, fast_weights, momentum
):
    row_count = attn_query.shape[0]
    reach_shards = WINDOW // row_count
    earlier = [
        from_behind((attn_key, attn_value), "ctx", reach_shards - offset)
        for offset in range(reach_shards)
    ]
    key_rows = jnp.concatenate([shifted[0] for shifted in earlier] + [attn_key], axis=0)
    value_rows = jnp.concatenate([shifted[1] for shifted in earlier] + [attn_value], axis=0)
    attn_out = local_attention(attn_query, key_rows, value_rows, lax.axis_index("ctx") * row_count)
    inv_root = FD ** (-0.5)
    span = 3 * FD
    head_local = fw_rate.shape[1]
    key_heads = [
        fw_key[:, head_index * FD : (head_index + 1) * FD] for head_index in range(head_local)
    ]
    scaled_heads = [
        (
            fw_rate[:, head_index : head_index + 1]
            * fw_value[:, head_index * FD : (head_index + 1) * FD].astype(jnp.float32)
        ).astype(jnp.bfloat16)
        for head_index in range(head_local)
    ]
    shard_rows = lax.all_gather(fast_weights.astype(jnp.bfloat16), "ctx", axis=0, tiled=True)
    result = []
    for add_head_index in range(head_local):
        block_low = shard_rows[:, add_head_index * span : (add_head_index + 1) * span]
        gate_part = (
            jnp.einsum(
                "td,cd->tc",
                key_heads[add_head_index],
                block_low[:, :FD],
                preferred_element_type=jnp.float32,
            )
            * inv_root
        )
        up_part = (
            jnp.einsum(
                "td,cd->tc",
                key_heads[add_head_index],
                block_low[:, FD : 2 * FD],
                preferred_element_type=jnp.float32,
            )
            * inv_root
        )
        scaled_part = scaled_heads[add_head_index]
        back_part = (
            jnp.dot(scaled_part, block_low[:, 2 * FD :], preferred_element_type=jnp.float32)
            * inv_root
        )
        result.append(gate_part)
        result.append(up_part)
        result.append(back_part)
    running = tuple(result)
    grad_heads = [
        local_grads(
            running[3 * head_index], running[3 * head_index + 1], running[3 * head_index + 2]
        )
        for head_index in range(head_local)
    ]
    pieces = []
    for row_head_index in range(head_local):
        hidden, gate_grad, up_grad = grad_heads[row_head_index]
        pieces.append(
            jnp.einsum(
                "th,td->hd",
                gate_grad,
                key_heads[row_head_index],
                preferred_element_type=jnp.float32,
            )
        )
        pieces.append(
            jnp.einsum(
                "th,td->hd", up_grad, key_heads[row_head_index], preferred_element_type=jnp.float32
            )
        )
        pieces.append(
            jnp.einsum(
                "tr,th->rh",
                scaled_heads[row_head_index],
                hidden,
                preferred_element_type=jnp.float32,
            )
        )
    own_update = lax.psum_scatter(
        jnp.concatenate(pieces, axis=1), "ctx", scatter_dimension=0, tiled=True
    )
    new_momentum = DECAY * momentum + own_update
    new_weights = renormalize(fast_weights, fast_weights + new_momentum)
    new_low = lax.all_gather(new_weights.astype(jnp.bfloat16), "ctx", axis=0, tiled=True)
    outputs = [
        apply_query(
            new_low[:, head_index * span : (head_index + 1) * span],
            fw_query[:, head_index * FD : (head_index + 1) * FD],
        )
        for head_index in range(head_local)
    ]
    fw_out = jnp.concatenate(outputs, axis=1)
    return (attn_out, fw_out, new_weights, new_momentum)


def solution(mesh):
    in_specs = (
        P(("seq", "ctx"), "head"),
        P(("seq", "ctx"), "head"),
        P(("seq", "ctx"), "head"),
        P(("seq", "ctx"), "head"),
        P(("seq", "ctx"), "head"),
        P(("seq", "ctx"), "head"),
        P(("seq", "ctx"), "head"),
        P(("seq", "ctx"), "head"),
        P(("seq", "ctx"), "head"),
    )
    out_specs = (
        P(("seq", "ctx"), "head"),
        P(("seq", "ctx"), "head"),
        P(("seq", "ctx"), "head"),
        P(("seq", "ctx"), "head"),
    )
    return jax.shard_map(
        per_device, mesh=mesh, in_specs=in_specs, out_specs=out_specs, check_vma=False
    )
```

profile of v0, /device:TPU:7, one launch (start us, length us, event | category | flops | bytes accessed | tf_op | source)
XLA Modules:
  0.0 330.4 jit_solution(17139259832476738827)
XLA Ops:
  7.2 0.0 copy-start.4
  7.2 0.0 all-gather.3.cloned.1.call-start
  7.2 4.6 %fusion.75 = (bf16[160,3840]{1,0:T(8,128)(2,1)}, f32[160,3840]{1,0:T(8,128)}) fusion(f32[160,3840]{1,0:T(8,128)} %param.16), kind=kLoop, calls=%fused_computation.105 | loop fusion | flops 1228800 | bytes 6144000 | tf_op jit(solution)/shard_map/convert_element_type | solution.py:116
  11.9 0.0 all-gather.3.cloned.1.call-update
  11.9 0.0 reduce-scatter.4.cloned.1.call-start
  12.0 0.0 copy-done.4
  12.0 39.3 %all-gather.3.cloned.1.call-done = bf16[640,3840]{1,0:T(8,128)(2,1)} async-done(((bf16[160,3840]{1,0:T(8,128)(2,1)}), bf16[640,3840]{1,0:T(8,128)(2,1)}) %all-gather.3.cloned.1.call-update) | async-done | bytes 4915216 | tf_op jit(solution)/shard_map/all_gather | solution.py:116
  51.3 2.1 convolution_multiply_fusion.9
  53.4 1.9 convolution_multiply_fusion.10
  55.3 0.0 copy-done.7
  55.3 0.0 copy-done.5
  55.3 0.8 convolution_multiply_fusion.11
  56.2 2.1 convolution_dynamic-update-slice_fusion.5
  58.3 2.0 convolution_dynamic-update-slice_fusion.4
  60.3 2.1 convolution_dynamic-update-slice_fusion.3
  62.4 0.8 convolution_multiply_fusion.6
  63.2 0.8 convolution_multiply_fusion.7
  63.9 0.8 convolution_multiply_fusion.8
  64.8 2.1 convolution_dynamic-update-slice_fusion.2
  66.9 2.0 convolution_dynamic-update-slice_fusion.1
  68.9 2.1 convolution_dynamic-update-slice_fusion
  70.9 11.1 %copy.105 = f32[640,3840]{1,0:T(8,128)} copy(f32[640,3840]{0,1:T(8,128)} %convolution_dynamic-update-slice_fusion) | data formatting | bytes 19660800
  82.0 0.0 reduce-scatter.4.cloned.1.call-update
  82.0 0.0 copy-start
  82.0 0.0 all-gather.5.cloned.1.call-start
  82.1 1.4 collective-permute-start.1
  83.5 1.3 collective-permute-start
  84.8 2.4 copy.80
  87.3 1.3 collective-permute-start.3
  88.5 1.5 collective-permute-start.2
  90.0 0.0 copy-done
  90.0 3.1 copy.88
  93.1 2.8 copy.83
  95.9 0.1 copy-done.3
  96.0 3.1 copy.87
  99.0 2.7 square.13
  101.7 0.3 reduce_sum.28
  102.0 0.1 copy.89
  102.1 1.3 fusion.7
  103.4 0.0 collective-permute-done.1
  103.4 68.9 %collective-permute-done = bf16[512,1280]{1,0:T(8,128)(2,1)} collective-permute-done((bf16[512,1280]{1,0:T(8,128)(2,1)}, bf16[512,1280]{1,0:T(8,128)(2,1)}, u32[]{:S(2)}, u32[]{:S(2)}) %collective-permute-start) | collective-permute-done | bytes 1310752 | tf_op jit(solution)/shard_map/ppermute | solution.py:18
  172.2 3.6 %pad_maximum_fusion = bf16[1536,1280]{1,0:T(8,128)(2,1)} fusion(bf16[512,1280]{1,0:T(8,128)(2,1)} %param.11, bf16[512,1280]{1,0:T(8,128)(2,1)} %collective-permute-done.1, bf16[512,1280]{1,0:T(8,128)(2,1)} %collective-permute-done), kind=kLoop, calls=%fused_computation.7 | loop fusion | flops 11796480 | bytes 7864320 | tf_op jit(solution)/shard_map/concatenate | solution.py:101
  175.8 6.4 %copy.79 = bf16[1536,1280]{0,1:T(8,128)(2,1)} copy(bf16[1536,1280]{1,0:T(8,128)(2,1)} %pad_maximum_fusion) | data formatting | bytes 7864320 | tf_op jit(solution)/shard_map/concatenate | solution.py:101
  182.2 0.0 collective-permute-done.3
  182.2 41.7 %collective-permute-done.2 = bf16[512,1280]{0,1:T(8,128)(2,1)} collective-permute-done((bf16[512,1280]{0,1:T(8,128)(2,1)}, bf16[512,1280]{0,1:T(8,128)(2,1)}, u32[]{:S(2)}, u32[]{:S(2)}) %collective-permute-start.2) | collective-permute-done | bytes 1310752 | tf_op jit(solution)/shard_map/ppermute | solution.py:18
  223.9 0.0 copy-done.2
  223.9 3.3 %pad_maximum_fusion.1 = bf16[1536,1280]{0,1:T(8,128)(2,1)} fusion(bf16[512,1280]{0,1:T(8,128)(2,1)S(1)} %copy-done.2, bf16[512,1280]{0,1:T(8,128)(2,1)} %collective-permute-done.3, bf16[512,1280]{0,1:T(8,128)(2,1)} %collective-permute-done.2), kind=kLoop, calls=%fused_computation.8 | loop fusion | flops 11796480 | bytes 7864320 | tf_op jit(solution)/shard_map/concatenate | solution.py:100
  227.3 4.8 %copy.106 = f32[160,3840]{0,1:T(8,128)} copy(f32[160,3840]{1,0:T(8,128)} %reduce-scatter.4.cloned.1.call-done) | data formatting | bytes 4915200
  232.0 9.9 %fusion.74 = (f32[160,3840]{0,1:T(8,128)}, f32[160,3840]{0,1:T(8,128)}, f32[160,3840]{0,1:T(8,128)}) fusion(f32[160,3840]{0,1:T(8,128)} %copy.88, f32[160,3840]{0,1:T(8,128)} %copy.106, f32[160,3840]{0,1:T(8,128)} %copy.87), kind=kLoop, calls=%fused_computation.104 | loop fusion | flops 2457600 | bytes 14745600 | tf_op jit(solution)/shard_map/square | solution.py:64
  241.9 2.4 reduce_sum.29
  244.3 5.1 %fusion.73 = (bf16[160,3840]{0,1:T(8,128)(2,1)}, f32[160,3840]{0,1:T(8,128)}) fusion(f32[160,3840]{0,1:T(8,128)} %get-tuple-element.27, f32[160,6]{0,1:T(8,128)S(1)} %rsqrt_multiply_fusion), kind=kLoop, calls=%fused_computation.103 | loop fusion | flops 1228800 | bytes 6147840 | tf_op jit(solution)/shard_map/convert_element_type | solution.py:182
  249.4 3.8 %copy.90 = bf16[160,3840]{1,0:T(8,128)(2,1)} copy(bf16[160,3840]{0,1:T(8,128)(2,1)} %get-tuple-element.24) | data formatting | bytes 2457600 | tf_op jit(solution)/shard_map/convert_element_type | solution.py:182
  253.1 0.0 all-gather.5.cloned.1.call-update
  253.2 16.6 %fusion.2 = (f32[10,512]{1,0:T(8,128)S(1)}, f32[10,1536,512]{2,1,0:T(8,128)}) fusion(pred[512,1536]{0,1:T(8,128)(4,1)S(1)} %fusion.7, bf16[1536,10,128]{0,2,1:T(8,128)(2,1)} %bitcast.50, bf16[512,10,128]{0,2,1:T(8,128)(2,1)S(1)} %bitcast.52), kind=kOutput, calls=%fused_computation.4 | convolution fusion | flops 2036853760 | bytes 37507072 | tf_op jit(solution)/shard_map/qhd,khd->hqk/dot_general | solution.py:30
  269.7 13.9 %fusion = f32[10,512]{1,0:T(8,128)S(1)} fusion(f32[10,1536,512]{2,1,0:T(8,128)} %get-tuple-element.34, f32[10,512]{1,0:T(8,128)S(1)} %get-tuple-element.33, pred[512,1536]{0,1:T(8,128)(4,1)S(1)} %fusion.7), kind=kLoop, calls=%fused_computation.2 | loop fusion | flops 31452160 | bytes 32284672 | tf_op jit(solution)/shard_map/reduce_sum | solution.py:43
  283.6 15.5 %fusion.8 = bf16[512,10,128]{0,2,1:T(8,128)(2,1)S(1)} fusion(bf16[1536,10,128]{0,2,1:T(8,128)(2,1)} %bitcast.53, f32[10,1536,512]{2,1,0:T(8,128)} %get-tuple-element.34, f32[10,512]{1,0:T(8,128)S(1)} %get-tuple-element.33, pred[512,1536]{0,1:T(8,128)(4,1)S(1)} %fusion.7, f32[512,10]{0,1:T(8,128)S(1)} %bitcast.55), kind=kOutput, calls=%fused_computation.16 | convolution fusion | flops 2046033920 | bytes 37527552 | tf_op jit(solution)/shard_map/hqk,khd->qhd/dot_general | solution.py:45
  299.0 1.4 copy.95
  300.5 4.9 %copy.96 = f32[160,3840]{1,0:T(8,128)} copy(f32[160,3840]{0,1:T(8,128)} %get-tuple-element.25) | data formatting | bytes 4915200
  305.4 5.0 %copy.97 = f32[160,3840]{1,0:T(8,128)} copy(f32[160,3840]{0,1:T(8,128)} %get-tuple-element.28) | data formatting | bytes 4915200
  310.3 3.0 fusion.14
  313.3 3.0 fusion.11
  316.3 3.2 fusion.20
  319.5 3.2 fusion.19
  322.7 1.2 pad_maximum_fusion.2
  (16 shorter events, 0.1 us)
Async XLA Ops:
  7.2 4.8 %copy-start.4 = (f32[512,2]{0,1:T(2,128)S(1)}, f32[512,2]{0,1:T(2,128)}, u32[]{:S(2)}) copy-start(f32[512,2]{0,1:T(2,128)} %param.15) | copy-start | bytes 12292
  7.2 44.1 %copy-start.6 = (bf16[512,1280]{1,0:T(8,128)(2,1)S(1)}, bf16[512,1280]{1,0:T(8,128)(2,1)}, u32[]{:S(2)}) copy-start(bf16[512,1280]{1,0:T(8,128)(2,1)} %param.13) | copy-start | bytes 3932164
  7.2 44.1 %all-gather.3.cloned.1.call-start = ((), (), s32[]{:S(2)}) async-start(), calls=%async_computation.1 | async-start | bytes 6144000 | tf_op jit(solution)/shard_map/all_gather | solution.py:116
  11.9 43.4 %copy-start.7 = (bf16[512,1280]{1,0:T(8,128)(2,1)S(1)}, bf16[512,1280]{1,0:T(8,128)(2,1)}, u32[]{:S(2)}) copy-start(bf16[512,1280]{1,0:T(8,128)(2,1)} %param.14) | copy-start | bytes 3932164
  11.9 215.4 %reduce-scatter.4.cloned.1.call-start = ((), (), s32[]{:S(2)}) async-start(), calls=%async_computation.3 | async-start | bytes 12288000
  51.3 4.0 %copy-start.5 = (bf16[640,3840]{1,0:T(8,128)(2,1)S(1)}, bf16[640,3840]{1,0:T(8,128)(2,1)}, u32[]{:S(2)}) copy-start(bf16[640,3840]{1,0:T(8,128)(2,1)} %all-gather.3.cloned.1.call-done) | copy-start | bytes 14745604
  82.0 8.0 %copy-start = (f32[160,3840]{1,0:T(8,128)S(1)}, f32[160,3840]{1,0:T(8,128)}, u32[]{:S(2)}) copy-start(f32[160,3840]{1,0:T(8,128)} %param.16) | copy-start | bytes 7372804
  82.0 228.3 %all-gather.5.cloned.1.call-start = ((), (), s32[]{:S(2)}) async-start(), calls=%async_computation.2 | async-start | bytes 6144000 | tf_op jit(solution)/shard_map/all_gather | solution.py:182
  82.1 21.3 %collective-permute-start.1 = (bf16[512,1280]{1,0:T(8,128)(2,1)}, bf16[512,1280]{1,0:T(8,128)(2,1)}, u32[]{:S(2)}, u32[]{:S(2)}) collective-permute-start(bf16[512,1280]{1,0:T(8,128)(2,1)} %param.11), channel_id=1, source_target_pairs={{0,8},{8,16},{16,24},{1,9},{9,17},{17,25},{2,10},{10,18},{18,26},{... | collective-permute-start | bytes 3932168 | tf_op jit(solution)/shard_map/ppermute | solution.py:18
  83.5 88.7 %collective-permute-start = (bf16[512,1280]{1,0:T(8,128)(2,1)}, bf16[512,1280]{1,0:T(8,128)(2,1)}, u32[]{:S(2)}, u32[]{:S(2)}) collective-permute-start(bf16[512,1280]{1,0:T(8,128)(2,1)} %param.11), channel_id=1, source_target_pairs={{0,16},{8,24},{1,17},{9,25},{2,18},{10,26},{3,19},{11,27},{4,20},{... | collective-permute-start | bytes 3932168 | tf_op jit(solution)/shard_map/ppermute | solution.py:18
  87.3 95.0 %collective-permute-start.3 = (bf16[512,1280]{0,1:T(8,128)(2,1)}, bf16[512,1280]{0,1:T(8,128)(2,1)}, u32[]{:S(2)}, u32[]{:S(2)}) collective-permute-start(bf16[512,1280]{0,1:T(8,128)(2,1)} %copy.80), channel_id=1, source_target_pairs={{0,8},{8,16},{16,24},{1,9},{9,17},{17,25},{2,10},{10,18},{18,26},{... | collective-permute-start | bytes 3932168 | tf_op jit(solution)/shard_map/ppermute | solution.py:18
  88.5 135.4 %collective-permute-start.2 = (bf16[512,1280]{0,1:T(8,128)(2,1)}, bf16[512,1280]{0,1:T(8,128)(2,1)}, u32[]{:S(2)}, u32[]{:S(2)}) collective-permute-start(bf16[512,1280]{0,1:T(8,128)(2,1)} %copy.80), channel_id=1, source_target_pairs={{0,16},{8,24},{1,17},{9,25},{2,18},{10,26},{3,19},{11,27},{4,20},{... | collective-permute-start | bytes 3932168 | tf_op jit(solution)/shard_map/ppermute | solution.py:18
  93.1 2.8 copy-start.3
  175.8 48.1 %copy-start.2 = (bf16[512,1280]{0,1:T(8,128)(2,1)S(1)}, bf16[512,1280]{0,1:T(8,128)(2,1)}, u32[]{:S(2)}) copy-start(bf16[512,1280]{0,1:T(8,128)(2,1)} %copy.80) | copy-start | bytes 3932164
  249.4 3.8 %copy-start.1 = (bf16[512,1280]{0,1:T(8,128)(2,1)S(1)}, bf16[512,1280]{0,1:T(8,128)(2,1)}, u32[]{:S(2)}) copy-start(bf16[512,1280]{0,1:T(8,128)(2,1)} %copy.83) | copy-start | bytes 3932164
  305.4 5.0 %copy-start.8 = (bf16[512,1280]{1,0:T(8,128)(2,1)S(1)}, bf16[512,1280]{1,0:T(8,128)(2,1)}, u32[]{:S(2)}) copy-start(bf16[512,1280]{1,0:T(8,128)(2,1)} %param.12) | copy-start | bytes 3932164
Sparse Core Ops, SparseCore 0:
  12.0 39.2 all-gather.2
  82.1 125.8 reduce-scatter.3
  253.3 38.4 all-gather.4
where the time goes:
time: 332 us; the launch traced here: 330 us
  waiting for transfers between devices  150 us (45%)
  matrix products  63.9 us (19%)
  local copies, waits for them, and re-layouts  51.5 us (16%)
  other arithmetic  45.5 us (14%)
  between operations  14 us (4%)
  starting transfers between devices  5.59 us (2%)
    ppermute x4, waiting for transfers between devices, from_behind(): return lax.ppermute(shard, axis, pairs)  111 us
    all_gather x1, waiting for transfers between devices, per_device(): lax.all_gather(fast_weights.astype(jnp.bfloat16), 'ctx', axis=0, tiled=True)  39.3 us
    unnamed x27, local copies, waits for them, and re-layouts  38.6 us
    dot_general x1, matrix products, local_attention(): jnp.einsum('qhd,khd->hqk', query_all, key_all, preferred_element_type=jnp...  16.6 us
    dot_general x1, matrix products, local_attention(): jnp.einsum('hqk,khd->qhd', prob_low, value_all, preferred_element_type=jn...  15.5 us
    reduce_sum x1, other arithmetic, local_attention(): denominator = jnp.sum(exponent, axis=2)  13.9 us
    square x1, other arithmetic, renormalize(): jnp.square(moved.reshape(shape_split))  9.87 us
  transfers between devices with their start and end apart: 7, of which 3 were waited for; matrix products, arithmetic and copies ran while one was open for 26% of the time, Pallas kernels for 0%

commit v1 on v0

v1 whole, which is shorter than its diff:
```python
import functools
import math

import jax
import jax.numpy as jnp
from jax import lax
from jax.experimental import pallas as pl
from jax.experimental.pallas import tpu as pltpu
from jax.sharding import PartitionSpec as P

HD = 128
FD = 640
WINDOW = 1024
EPSILON = 1e-06
DECAY = 0.9
SPAN = 3 * FD
INV_ROOT = FD ** (-0.5)
EXP2_SCALE = HD ** (-0.5) * math.log2(math.e)
LOWEST = -1e30
F32 = jnp.float32
BF16 = jnp.bfloat16
ANY = pl.BlockSpec(memory_space=pl.ANY)


def dot(a, b, a_dim, b_dim):
    return lax.dot_general(a, b, (((a_dim,), (b_dim,)), ((), ())), preferred_element_type=F32)


def cost(flops, bytes_accessed, transcendentals=0):
    return pl.CostEstimate(
        flops=int(flops), bytes_accessed=int(bytes_accessed), transcendentals=int(transcendentals)
    )


def attention_kernel(shape_kind, has_state, last, offset, *refs):
    if has_state:
        q_ref, k_ref, v_ref, o_in_ref, st_in_ref = refs[:5]
        outs = refs[5:]
    else:
        q_ref, k_ref, v_ref = refs[:3]
        outs = refs[3:]
    head = pl.program_id(0)
    heads = pl.num_programs(0)
    scores = dot(k_ref[...], q_ref[...], 1, 1)
    if shape_kind != "full":
        key_row = lax.broadcasted_iota(jnp.int32, scores.shape, 0)
        query_row = lax.broadcasted_iota(jnp.int32, scores.shape, 1)
        allowed = key_row <= query_row if shape_kind == "causal" else key_row > query_row
        scores = jnp.where(allowed, scores, LOWEST)
    highest = jnp.max(scores, axis=0, keepdims=True)
    if has_state:
        valid = lax.axis_index("ctx") >= offset
        before = jnp.where(valid, st_in_ref[pl.ds(head, 1), :], LOWEST)
        highest = jnp.maximum(highest, before)
    weights = jnp.exp2((scores - highest) * EXP2_SCALE)
    total = jnp.sum(weights, axis=0, keepdims=True)
    mixed = dot(v_ref[...], weights.astype(BF16), 0, 0)
    if has_state:
        keep = jnp.exp2((before - highest) * EXP2_SCALE)
        total = total + keep * st_in_ref[pl.ds(heads + head, 1), :]
        mixed = mixed + keep * o_in_ref[...].astype(F32)
    if last:
        outs[0][...] = (mixed / total).T.astype(BF16)
    else:
        outs[0][...] = mixed.astype(BF16)
        outs[1][pl.ds(head, 1), :] = highest
        outs[1][pl.ds(heads + head, 1), :] = total


def attention_step(shape_kind, queries, keys, values, state, last, offset):
    rows, width = queries.shape
    heads = width // HD
    column = pl.BlockSpec((rows, HD), lambda h: (0, h))
    turned = pl.BlockSpec((HD, rows), lambda h: (h, 0))
    stats = pl.BlockSpec((2 * heads, rows), lambda h: (0, 0))
    in_specs = [column, column, column]
    args = [queries, keys, values]
    if state is not None:
        in_specs += [turned, stats]
        args += list(state)
    if last:
        out_shape = jax.ShapeDtypeStruct((rows, width), BF16)
        out_specs = column
    else:
        out_shape = (
            jax.ShapeDtypeStruct((width, rows), BF16),
            jax.ShapeDtypeStruct((2 * heads, rows), F32),
        )
        out_specs = (turned, stats)
    return pl.pallas_call(
        functools.partial(attention_kernel, shape_kind, state is not None, last, offset),
        grid=(heads,),
        in_specs=in_specs,
        out_specs=out_specs,
        out_shape=out_shape,
        cost_estimate=cost(4 * rows * rows * width, 5 * rows * width * 2, rows * rows * heads),
        name="attend_" + shape_kind,
    )(*args)


def shifted(arrays, by, low, high):
    pairs = [(i, i + by) for i in range(low, high)]
    return [lax.ppermute(array, "ctx", pairs) for array in arrays]


def fetch_rows(parts, masks, target, sems):
    index = lax.axis_index("ctx")
    copies = []
    for number, (part, mask) in enumerate(zip(parts, masks)):
        rows = part.shape[0]
        if mask is None:
            place = target
        else:
            place = target.at[pl.ds(pl.multiple_of((index ^ mask) * rows, 32), rows)]
        copy = pltpu.make_async_copy(part, place, sems.at[number])
        copy.start()
        copies.append(copy)
    return copies


def grads_kernel(masks, split, head, *refs):
    count = len(masks)
    key_ref, value_ref, rate_ref = refs[:3]
    parts = refs[3 : 3 + count]
    outs = refs[3 + count : -7]
    low, scaled, hidden, gate_grad, up_grad, update, sems = refs[-7:]
    copies = fetch_rows(parts, masks, low, sems)
    rate = rate_ref[:, head : head + 1]
    scaled[...] = (rate * value_ref[...].astype(F32)).astype(BF16)
    for copy in copies:
        copy.wait()
    tokens = key_ref.shape[0]
    block = min(256, tokens)

    def forward(step, carry):
        rows = pl.ds(pl.multiple_of(step * block, block), block)
        keys = key_ref[rows, :]
        gate = dot(keys, low[:, :FD], 1, 1) * INV_ROOT
        up = dot(keys, low[:, FD : 2 * FD], 1, 1) * INV_ROOT
        back = dot(scaled[rows, :], low[:, 2 * FD :], 1, 0) * INV_ROOT
        sigmoid = 1.0 / (1.0 + jnp.exp(-gate))
        silu = gate * sigmoid
        hidden[rows, :] = (silu * up).astype(BF16)
        gate_grad[rows, :] = (back * up * sigmoid * (1.0 + gate * (1.0 - sigmoid))).astype(BF16)
        up_grad[rows, :] = (back * silu).astype(BF16)
        return carry

    lax.fori_loop(0, tokens // block, forward, 0)

    def backward(step, carry):
        rows = pl.ds(pl.multiple_of(step * 128, 128), 128)
        update[rows, :FD] = dot(gate_grad[:, rows], key_ref[...], 0, 0)
        update[rows, FD : 2 * FD] = dot(up_grad[:, rows], key_ref[...], 0, 0)
        update[rows, 2 * FD :] = dot(scaled[:, rows], hidden[...], 0, 0)
        return carry

    lax.fori_loop(0, FD // 128, backward, 0)
    if split:
        index = lax.axis_index("ctx")
        for out, mask in zip(outs, (3, 1, 2, 0)):
            rows = out.shape[0]
            out[...] = update[pl.ds(pl.multiple_of((index ^ mask) * rows, 32), rows), :].astype(out.dtype)
    else:
        outs[0][...] = update[...]


def head_grads(fw_key, fw_value, fw_rate, gathered, head, split):
    tokens = fw_key.shape[0]
    parts = [part for part, _ in gathered]
    masks = [mask for _, mask in gathered]
    column = pl.BlockSpec((tokens, FD), lambda i: (0, head))
    if split:
        rows = parts[0].shape[0]
        out_shape = tuple(jax.ShapeDtypeStruct((rows, SPAN), kind) for kind in (BF16, BF16, F32, F32))
    else:
        out_shape = (jax.ShapeDtypeStruct((FD, SPAN), F32),)
    out_specs = tuple(pl.BlockSpec(out.shape, lambda i: (0, 0)) for out in out_shape)
    return pl.pallas_call(
        functools.partial(grads_kernel, masks, split, head),
        grid=(1,),
        in_specs=[column, column, pl.BlockSpec(fw_rate.shape, lambda i: (0, 0))] + [ANY] * len(parts),
        out_specs=out_specs,
        out_shape=out_shape,
        scratch_shapes=[
            pltpu.VMEM((FD, SPAN), BF16),
            pltpu.VMEM((tokens, FD), BF16),
            pltpu.VMEM((tokens, FD), BF16),
            pltpu.VMEM((tokens, FD), BF16),
            pltpu.VMEM((tokens, FD), BF16),
            pltpu.VMEM((FD, SPAN), F32),
            pltpu.SemaphoreType.DMA((len(parts),)),
        ],
        cost_estimate=cost(12 * tokens * FD * FD, 8e6, tokens * FD),
        name="head_grads",
    )(fw_key, fw_value, fw_rate, *parts)


def move_kernel(sums, aliased, w_ref, m_ref, *refs):
    addends = refs[:sums]
    nw_ref, nm_ref, low_ref = refs[-3:]
    update = addends[0][...]
    for addend in addends[1:]:
        update = update + addend[...].astype(F32)
    weights = w_ref[...]
    momentum = DECAY * m_ref[...] + update
    moved = weights + momentum
    nm_ref[...] = momentum
    for part in range(3):
        cols = slice(part * FD, (part + 1) * FD)
        before = jnp.mean(jnp.square(weights[:, cols]), axis=1, keepdims=True)
        after = jnp.mean(jnp.square(moved[:, cols]), axis=1, keepdims=True)
        fresh = moved[:, cols] * (jnp.sqrt(before + EPSILON) * lax.rsqrt(after + EPSILON))
        nw_ref[:, cols] = fresh
        low_ref[:, cols] = fresh.astype(BF16)


def move_weights(fast_weights, momentum, addends, head, previous):
    rows = fast_weights.shape[0]
    block = 32 if rows % 32 == 0 else rows
    wide = pl.BlockSpec((block, SPAN), lambda i: (i, head))
    own = pl.BlockSpec((block, SPAN), lambda i: (i, 0))
    in_specs = [wide, wide] + [own] * len(addends)
    args = [fast_weights, momentum] + list(addends)
    aliases = {}
    if previous is not None:
        aliases = {len(args): 0, len(args) + 1: 1}
        in_specs += [ANY, ANY]
        args += list(previous)
    full = jax.ShapeDtypeStruct(fast_weights.shape, F32)
    return pl.pallas_call(
        functools.partial(move_kernel, len(addends), previous is not None),
        grid=(rows // block,),
        in_specs=in_specs,
        out_specs=(wide, wide, own),
        out_shape=(full, full, jax.ShapeDtypeStruct((rows, SPAN), BF16)),
        input_output_aliases=aliases,
        cost_estimate=cost(20 * rows * SPAN, 26 * rows * SPAN),
        name="move_weights",
    )(*args)


def query_kernel(masks, aliased, q_ref, *refs):
    count = len(masks)
    parts = refs[:count]
    out_ref, low, sems = refs[-3:]
    for copy in fetch_rows(parts, masks, low, sems):
        copy.wait()
    tokens = q_ref.shape[0]
    block = min(256, tokens)

    def one(step, carry):
        rows = pl.ds(pl.multiple_of(step * block, block), block)
        queries = q_ref[rows, :]
        gate = dot(queries, low[:, :FD], 1, 1) * INV_ROOT
        up = dot(queries, low[:, FD : 2 * FD], 1, 1) * INV_ROOT
        hidden = (gate * (1.0 / (1.0 + jnp.exp(-gate))) * up).astype(BF16)
        out_ref[rows, :] = (dot(hidden, low[:, 2 * FD :], 1, 1) * INV_ROOT).astype(BF16)
        return carry

    lax.fori_loop(0, tokens // block, one, 0)


def head_query(fw_query, gathered, head, previous):
    tokens = fw_query.shape[0]
    parts = [part for part, _ in gathered]
    masks = [mask for _, mask in gathered]
    column = pl.BlockSpec((tokens, FD), lambda i: (0, head))
    in_specs = [column] + [ANY] * len(parts)
    args = [fw_query] + parts
    aliases = {}
    if previous is not None:
        aliases = {len(args): 0}
        in_specs.append(ANY)
        args.append(previous)
    return pl.pallas_call(
        functools.partial(query_kernel, masks, previous is not None),
        grid=(1,),
        in_specs=in_specs,
        out_specs=column,
        out_shape=jax.ShapeDtypeStruct(fw_query.shape, BF16),
        scratch_shapes=[pltpu.VMEM((FD, SPAN), BF16), pltpu.SemaphoreType.DMA((len(parts),))],
        input_output_aliases=aliases,
        cost_estimate=cost(6 * tokens * FD * FD, 4e6, tokens * FD),
        name="head_query",
    )(*args)


def swapped(array, mask):
    devices = lax.axis_size("ctx")
    return lax.ppermute(array, "ctx", [(i, i ^ mask) for i in range(devices)])


def gather_rows(shard, paired):
    if not paired:
        return [(lax.all_gather(shard, "ctx", axis=0, tiled=True), None)]
    across = swapped(shard, 2)
    beside = swapped(shard, 1)
    return [(shard, 0), (beside, 1), (across, 2), (swapped(across, 1), 3)]


def sum_rows(pieces, paired):
    if not paired:
        return [lax.psum_scatter(pieces[0], "ctx", scatter_dimension=0, tiled=True)]
    far, near, across, own = pieces
    far = swapped(far, 1)
    near = swapped(near, 1)
    total = (across + far.astype(F32)).astype(BF16)
    return [own, near, swapped(total, 2)]


def per_device(
    attn_query, attn_key, attn_value, fw_query, fw_key, fw_value, fw_rate, fast_weights, momentum
):
    devices = lax.axis_size("ctx")
    rows = attn_query.shape[0]
    reach = WINDOW // rows
    head_local = fw_rate.shape[1]
    paired = devices == 4

    lows = [
        fast_weights[:, head * SPAN : (head + 1) * SPAN].astype(BF16) for head in range(head_local)
    ]
    gathered = [gather_rows(low, paired) for low in lows]

    travelling = [attn_query]
    for step in range(1, reach + 1):
        travelling.append(shifted([travelling[-1]], -1, 1, devices - step + 1)[0])

    pieces = [
        head_grads(fw_key, fw_value, fw_rate, gathered[head], head, paired)
        for head in range(head_local)
    ]
    sums = [sum_rows(piece, paired) for piece in pieces]

    state = None
    for step in range(reach, -1, -1):
        shape_kind = "causal" if step == 0 else "before" if step == reach else "full"
        state = attention_step(
            shape_kind, travelling[step], attn_key, attn_value, state, step == 0, 1
        )
        if step > 0:
            state = shifted(state, 1, 0, devices - step)
    attn_out = state

    new = None
    new_lows = []
    for head in range(head_local):
        new_weights, new_momentum, low = move_weights(
            fast_weights, momentum, sums[head], head, new
        )
        new = (new_weights, new_momentum)
        new_lows.append(low)
    new_gathered = [gather_rows(low, paired) for low in new_lows]
    fw_out = None
    for head in range(head_local):
        fw_out = head_query(fw_query, new_gathered[head], head, fw_out)
    return (attn_out, fw_out, new_weights, new_momentum)


def solution(mesh):
    spec = P(("seq", "ctx"), "head")
    return jax.shard_map(
        per_device, mesh=mesh, in_specs=(spec,) * 9, out_specs=(spec,) * 4, check_vma=False
    )
```

time: 332 us -> 191 us (0.58)
  the two profiles are of different devices: /device:TPU:7 before, /device:TPU:0 now
where the time goes in v1:
time: 191 us; the launch traced here: 189 us
  Pallas kernels  74.7 us (39%)
  waiting for transfers between devices  57.7 us (30%)
  starting transfers between devices  45.7 us (24%)
  local copies, waits for them, and re-layouts  6.12 us (3%)
  other arithmetic  4.24 us (2%)
    ppermute x18, waiting for transfers between devices, swapped(): return lax.ppermute(array, 'ctx', [(i, i ^ mask) for i in range(devices)])  57.7 us
    ppermute x6, starting transfers between devices, shifted(): return [lax.ppermute(array, 'ctx', pairs) for array in arrays]  34.9 us
    pallas_call x3, Pallas kernels, attention_step(): pl.pallas_call(functools.partial(attention_kernel, shape_kind, state is n...  31.1 us
    pallas_call x2, Pallas kernels, head_grads(): pl.pallas_call(functools.partial(grads_kernel, masks, split, head), grid=...  20.5 us
    pallas_call x2, Pallas kernels, head_query(): pl.pallas_call(functools.partial(query_kernel, masks, previous is not Non...  11.7 us
    pallas_call x2, Pallas kernels, move_weights(): pl.pallas_call(functools.partial(move_kernel, len(addends), previous is n...  11.4 us
    ppermute x18, starting transfers between devices, swapped(): return lax.ppermute(array, 'ctx', [(i, i ^ mask) for i in range(devices)])  10.8 us
    unnamed x39, local copies, waits for them, and re-layouts  6.03 us
  transfers between devices with their start and end apart: 24, of which 6 were waited for; matrix products, arithmetic and copies ran while one was open for 3% of the time, Pallas kernels for 34%

profile of v1, /device:TPU:0, one launch (start us, length us, event | category | flops | bytes accessed | tf_op | source)
XLA Modules:
  0.0 189.5 jit_solution(14888531719957766621)
XLA Ops:
  0.6 1.3 collective-permute-start
  1.9 1.8 convert.4
  3.8 0.0 copy-start.15
  3.8 0.1 fusion
  3.9 0.0 copy-start.10
  3.9 0.0 copy-start.8
  3.9 3.7 %collective-permute-start.13 = (bf16[160,1920]{1,0:T(8,128)(2,1)S(1)}, bf16[160,1920]{1,0:T(8,128)(2,1)}, u32[]{:S(2)}, u32[]{:S(2)}) collective-permute-start(bf16[160,1920]{1,0:T(8,128)(2,1)S(1)} %get-tuple-element.40.refs_3_), channel_id=1, source_target_pairs={{0,16},{8,24},{16,0},{24,8},{1,17},{9,25},{17,1},{25,9},{2,18},{10... | collective-permute-start | bytes 1843208 | tf_op jit(solution)/shard_map/ppermute | solution.py:290
  7.6 0.1 collective-permute-start.7
  7.6 0.3 collective-permute-start.12
  7.9 33.2 %collective-permute-done.13.refs_5_ = bf16[160,1920]{1,0:T(8,128)(2,1)} collective-permute-done((bf16[160,1920]{1,0:T(8,128)(2,1)S(1)}, bf16[160,1920]{1,0:T(8,128)(2,1)}, u32[]{:S(2)}, u32[]{:S(2)}) %collective-permute-start.13) | collective-permute-done | bytes 614432 | tf_op jit(solution)/shard_map/ppermute | solution.py:290
  41.2 0.0 collective-permute-start.14
  41.2 0.0 collective-permute-done.refs_0_
  41.2 1.3 collective-permute-start.1
  42.5 1.2 collective-permute-start.6
  43.7 4.0 %collective-permute-done.7.refs_5_ = bf16[160,1920]{1,0:T(8,128)(2,1)S(1)} collective-permute-done((bf16[160,1920]{1,0:T(8,128)(2,1)S(1)}, bf16[160,1920]{1,0:T(8,128)(2,1)S(1)}, u32[]{:S(2)}, u32[]{:S(2)}) %collective-permute-start.7) | collective-permute-done | bytes 614432 | tf_op jit(solution)/shard_map/ppermute | solution.py:290
  47.6 0.0 collective-permute-start.8
  47.6 0.9 copy.16.refs_2_
  48.6 0.0 collective-permute-done.12.refs_4_
  48.6 0.0 collective-permute-done.14.refs_6_
  48.6 10.3 %head_grads.3 = (bf16[160,1920]{1,0:T(8,128)(2,1)}, bf16[160,1920]{1,0:T(8,128)(2,1)}, f32[160,1920]{1,0:T(8,128)}, f32[160,1920]{1,0:T(8,128)}) custom-call(bf16[512,1280]{1,0:T(8,128)(2,1)} %refs_0_.5, bf16[512,1280]{1,0:T(8,128)(2,1)} %refs_1_.9, f32[512,2]{1,0:T(8,128)} %copy.16.refs_2_, bf16[160,1920]{1,0:T(8,128)(2,1)} %copy-done.10, ...), custom_call_target="tpu_custom_call" | custom-call | flops 2516582400 | bytes 8000000 | tf_op jit(solution)/shard_map/head_grads/pallas_call | solution.py:178
  58.9 0.5 collective-permute-start.16
  59.4 0.1 collective-permute-start.15
  59.5 0.0 collective-permute-done.6.refs_4_
  59.5 0.0 collective-permute-done.8.refs_6_
  59.5 10.2 %head_grads.2 = (bf16[160,1920]{1,0:T(8,128)(2,1)}, bf16[160,1920]{1,0:T(8,128)(2,1)}, f32[160,1920]{1,0:T(8,128)}, f32[160,1920]{1,0:T(8,128)}) custom-call(bf16[512,1280]{1,0:T(8,128)(2,1)} %refs_0_.5, bf16[512,1280]{1,0:T(8,128)(2,1)} %refs_1_.9, f32[512,2]{1,0:T(8,128)} %copy.16.refs_2_, bf16[160,1920]{1,0:T(8,128)(2,1)} %copy-done.8, ...), custom_call_target="tpu_custom_call" | custom-call | flops 2516582400 | bytes 8000000 | tf_op jit(solution)/shard_map/head_grads/pallas_call | solution.py:178
  69.8 0.5 collective-permute-start.10
  70.3 0.1 collective-permute-start.9
  70.4 10.1 %attend_before.1 = (bf16[1280,512]{1,0:T(8,128)(2,1)}, f32[20,512]{1,0:T(8,128)}) custom-call(bf16[512,1280]{1,0:T(8,128)(2,1)} %collective-permute-done.1.refs_0_, bf16[512,1280]{1,0:T(8,128)(2,1)} %refs_1_.7, bf16[512,1280]{1,0:T(8,128)(2,1)} %refs_2_.7), custom_call_target="tpu_custom_call" | custom-call | flops 1342177280 | bytes 6553600 | tf_op jit(solution)/shard_map/attend_before/pallas_call | solution.py:90
  80.4 2.4 %collective-permute-start.2 = (bf16[1280,512]{1,0:T(8,128)(2,1)}, bf16[1280,512]{1,0:T(8,128)(2,1)S(1)}, u32[]{:S(2)}, u32[]{:S(2)}) collective-permute-start(bf16[1280,512]{1,0:T(8,128)(2,1)} %get-tuple-element.22), channel_id=1, source_target_pairs={{0,8},{8,16},{1,9},{9,17},{2,10},{10,18},{3,11},{11,19},{4,12},{12... | collective-permute-start | bytes 3932168 | tf_op jit(solution)/shard_map/ppermute | solution.py:103
  82.9 1.2 add_convert_fusion
  84.1 0.1 collective-permute-start.17
  84.2 0.0 collective-permute-done.10
  84.2 1.2 add_convert_fusion.1
  85.4 2.1 %collective-permute-start.11 = (bf16[160,1920]{1,0:T(8,128)(2,1)S(1)}, bf16[160,1920]{1,0:T(8,128)(2,1)}, u32[]{:S(2)}, u32[]{:S(2)}) collective-permute-start(bf16[160,1920]{1,0:T(8,128)(2,1)S(1)} %add_convert_fusion.1), channel_id=1, source_target_pairs={{0,16},{8,24},{16,0},{24,8},{1,17},{9,25},{17,1},{25,9},{2,18},{10... | collective-permute-start | bytes 1843208 | tf_op jit(solution)/shard_map/ppermute | solution.py:290
  87.5 1.3 collective-permute-start.3
  88.8 12.1 %collective-permute-done.17.refs_2_ = bf16[160,1920]{1,0:T(8,128)(2,1)S(1)} collective-permute-done((bf16[160,1920]{1,0:T(8,128)(2,1)S(1)}, bf16[160,1920]{1,0:T(8,128)(2,1)S(1)}, u32[]{:S(2)}, u32[]{:S(2)}) %collective-permute-start.17) | collective-permute-done | bytes 614432 | tf_op jit(solution)/shard_map/ppermute | solution.py:290
  100.9 0.8 copy-done.11
  101.8 5.7 %move_weights.2 = (f32[160,3840]{1,0:T(8,128)}, f32[160,3840]{1,0:T(8,128)}, bf16[160,1920]{1,0:T(8,128)(2,1)}) custom-call(f32[160,3840]{1,0:T(8,128)} %w_ref.3, f32[160,3840]{1,0:T(8,128)} %m_ref.3, f32[160,1920]{1,0:T(8,128)} %get-tuple-element.30.refs_0_, bf16[160,1920]{1,0:T(8,128)(2,1)} %copy-done.6, bf16[160,1920]{1,0:T(8,128)(2,1)} %copy-done.11), custom_call_target="tpu_custom_call" | custom-call | flops 6144000 | bytes 7987200 | tf_op jit(solution)/shard_map/move_weights/pallas_call | solution.py:230
  107.5 0.0 collective-permute-start.22
  107.5 5.7 %collective-permute-done.11.refs_2_ = bf16[160,1920]{1,0:T(8,128)(2,1)} collective-permute-done((bf16[160,1920]{1,0:T(8,128)(2,1)S(1)}, bf16[160,1920]{1,0:T(8,128)(2,1)}, u32[]{:S(2)}, u32[]{:S(2)}) %collective-permute-start.11) | collective-permute-done | bytes 614432 | tf_op jit(solution)/shard_map/ppermute | solution.py:290
  113.2 5.7 %move_weights.3 = (f32[160,3840]{1,0:T(8,128)}, f32[160,3840]{1,0:T(8,128)}, bf16[160,1920]{1,0:T(8,128)(2,1)}) custom-call(f32[160,3840]{1,0:T(8,128)} %w_ref.3, f32[160,3840]{1,0:T(8,128)} %m_ref.3, f32[160,1920]{1,0:T(8,128)} %get-tuple-element.26.refs_0_, ...), custom_call_target="tpu_custom_call", output_to_operand_aliasing={{0}: (5, {}), {1}: (6, {})} | custom-call | flops 6144000 | bytes 7987200 | tf_op jit(solution)/shard_map/move_weights/pallas_call | solution.py:230
  118.9 1.1 collective-permute-start.19
  120.0 0.6 copy-done.13
  120.6 1.1 copy-done.1
  121.7 10.7 %attend_full.1 = (bf16[1280,512]{1,0:T(8,128)(2,1)}, f32[20,512]{1,0:T(8,128)}) custom-call(bf16[512,1280]{1,0:T(8,128)(2,1)} %copy-done, bf16[512,1280]{1,0:T(8,128)(2,1)} %refs_1_.7, bf16[512,1280]{1,0:T(8,128)(2,1)} %refs_2_.7, bf16[1280,512]{1,0:T(8,128)(2,1)} %copy-done.1, f32[20,512]{1,0:T(8,128)} %copy-done.13), custom_call_target="tpu_custom_call" | custom-call | flops 1342177280 | bytes 6553600 | tf_op jit(solution)/shard_map/attend_full/pallas_call | solution.py:90
  132.4 26.3 %collective-permute-start.4 = (bf16[1280,512]{1,0:T(8,128)(2,1)}, bf16[1280,512]{1,0:T(8,128)(2,1)S(1)}, u32[]{:S(2)}, u32[]{:S(2)}) collective-permute-start(bf16[1280,512]{1,0:T(8,128)(2,1)} %get-tuple-element.24), channel_id=1, source_target_pairs={{0,8},{8,16},{16,24},{1,9},{9,17},{17,25},{2,10},{10,18},{18,26},{... | collective-permute-start | bytes 3932168 | tf_op jit(solution)/shard_map/ppermute | solution.py:103
  158.7 0.1 collective-permute-start.21
  158.8 0.0 collective-permute-done.22.refs_2_
  158.8 0.5 collective-permute-start.23
  159.3 0.1 collective-permute-start.18
  159.4 0.0 collective-permute-done.19.refs_2_
  159.4 0.4 collective-permute-start.20
  159.8 2.5 %collective-permute-done.21.refs_1_ = bf16[160,1920]{1,0:T(8,128)(2,1)S(1)} collective-permute-done((bf16[160,1920]{1,0:T(8,128)(2,1)S(1)}, bf16[160,1920]{1,0:T(8,128)(2,1)S(1)}, u32[]{:S(2)}, u32[]{:S(2)}) %collective-permute-start.21) | collective-permute-done | bytes 614432 | tf_op jit(solution)/shard_map/ppermute | solution.py:290
  162.3 0.8 copy-done.12
  163.2 0.2 collective-permute-done.23.refs_3_
  163.4 5.8 %head_query.2.refs_4_ = bf16[512,1280]{1,0:T(8,128)(2,1)} custom-call(bf16[512,1280]{1,0:T(8,128)(2,1)} %q_ref.3, bf16[160,1920]{1,0:T(8,128)(2,1)} %get-tuple-element.37.refs_0_, bf16[160,1920]{1,0:T(8,128)(2,1)} %copy-done.12, bf16[160,1920]{1,0:T(8,128)(2,1)} %copy-done.9, bf16[160,1920]{1,0:T(8,128)(2,1)} %collective-permute-done.23.refs_3_), custom_call_target="tpu_custom_call" | custom-call | flops 1258291200 | bytes 4000000 | tf_op jit(solution)/shard_map/head_query/pallas_call | solution.py:275
  169.2 2.3 %collective-permute-start.5 = (f32[20,512]{1,0:T(8,128)S(1)}, f32[20,512]{1,0:T(8,128)S(1)}, u32[]{:S(2)}, u32[]{:S(2)}) collective-permute-start(f32[20,512]{1,0:T(8,128)S(1)} %copy-done.18), channel_id=1, source_target_pairs={{0,8},{8,16},{16,24},{1,9},{9,17},{17,25},{2,10},{10,18},{18,26},{... | collective-permute-start | bytes 122888 | tf_op jit(solution)/shard_map/ppermute | solution.py:103
  171.5 0.0 collective-permute-done.18.refs_1_
  171.5 0.0 collective-permute-done.20.refs_3_
  171.5 5.8 %head_query.3 = bf16[512,1280]{1,0:T(8,128)(2,1)} custom-call(bf16[512,1280]{1,0:T(8,128)(2,1)} %q_ref.3, bf16[160,1920]{1,0:T(8,128)(2,1)} %get-tuple-element.36.refs_0_, bf16[160,1920]{1,0:T(8,128)(2,1)} %collective-permute-done.18.refs_1_, bf16[160,1920]{1,0:T(8,128)(2,1)} %collective-permute-done.19.refs_2_, ...), custom_call_target="tpu_custom_call", output_to_operand_aliasing={{}: (5, {})} | custom-call | flops 1258291200 | bytes 4000000 | tf_op jit(solution)/shard_map/head_query/pallas_call | solution.py:275
  177.4 0.0 collective-permute-done.4.refs_3_
  177.4 0.6 copy-done.14
  178.0 1.1 copy-done.2
  179.1 10.3 %attend_causal.1 = bf16[512,1280]{1,0:T(8,128)(2,1)} custom-call(bf16[512,1280]{1,0:T(8,128)(2,1)} %refs_0_.3, bf16[512,1280]{1,0:T(8,128)(2,1)} %refs_1_.7, bf16[512,1280]{1,0:T(8,128)(2,1)} %refs_2_.7, bf16[1280,512]{1,0:T(8,128)(2,1)} %copy-done.2, f32[20,512]{1,0:T(8,128)} %copy-done.14), custom_call_target="tpu_custom_call" | custom-call | flops 1342177280 | bytes 6553600 | tf_op jit(solution)/shard_map/attend_causal/pallas_call | solution.py:90
  (36 shorter events, 0.1 us)
Async XLA Ops:
  0.6 40.5 %collective-permute-start = (bf16[512,1280]{1,0:T(8,128)(2,1)}, bf16[512,1280]{1,0:T(8,128)(2,1)S(1)}, u32[]{:S(2)}, u32[]{:S(2)}) collective-permute-start(bf16[512,1280]{1,0:T(8,128)(2,1)} %refs_0_.3), channel_id=1, source_target_pairs={{8,0},{16,8},{24,16},{9,1},{17,9},{25,17},{10,2},{18,10},{26,18},{... | collective-permute-start | bytes 3932168 | tf_op jit(solution)/shard_map/ppermute | solution.py:103
  3.8 43.9 %copy-start.15 = (f32[512,2]{0,1:T(2,128)S(1)}, f32[512,2]{0,1:T(2,128)}, u32[]{:S(2)}) copy-start(f32[512,2]{0,1:T(2,128)} %param.15) | copy-start | bytes 12292
  3.9 44.7 %copy-start.10 = (bf16[160,1920]{1,0:T(8,128)(2,1)}, bf16[160,1920]{1,0:T(8,128)(2,1)S(1)}, u32[]{:S(2)}) copy-start(bf16[160,1920]{1,0:T(8,128)(2,1)S(1)} %get-tuple-element.40.refs_3_) | copy-start | bytes 1843204
  3.9 55.0 %copy-start.8 = (bf16[160,1920]{1,0:T(8,128)(2,1)}, bf16[160,1920]{1,0:T(8,128)(2,1)S(1)}, u32[]{:S(2)}) copy-start(bf16[160,1920]{1,0:T(8,128)(2,1)S(1)} %get-tuple-element.41.refs_3_) | copy-start | bytes 1843204
  3.9 37.3 %collective-permute-start.13 = (bf16[160,1920]{1,0:T(8,128)(2,1)S(1)}, bf16[160,1920]{1,0:T(8,128)(2,1)}, u32[]{:S(2)}, u32[]{:S(2)}) collective-permute-start(bf16[160,1920]{1,0:T(8,128)(2,1)S(1)} %get-tuple-element.40.refs_3_), channel_id=1, source_target_pairs={{0,16},{8,24},{16,0},{24,8},{1,17},{9,25},{17,1},{25,9},{2,18},{10... | collective-permute-start | bytes 1843208 | tf_op jit(solution)/shard_map/ppermute | solution.py:290
  7.6 40.1 %collective-permute-start.7 = (bf16[160,1920]{1,0:T(8,128)(2,1)S(1)}, bf16[160,1920]{1,0:T(8,128)(2,1)S(1)}, u32[]{:S(2)}, u32[]{:S(2)}) collective-permute-start(bf16[160,1920]{1,0:T(8,128)(2,1)S(1)} %get-tuple-element.41.refs_3_), channel_id=1, source_target_pairs={{0,16},{8,24},{16,0},{24,8},{1,17},{9,25},{17,1},{25,9},{2,18},{10... | collective-permute-start | bytes 1843208 | tf_op jit(solution)/shard_map/ppermute | solution.py:290
  7.6 40.9 %collective-permute-start.12 = (bf16[160,1920]{1,0:T(8,128)(2,1)S(1)}, bf16[160,1920]{1,0:T(8,128)(2,1)}, u32[]{:S(2)}, u32[]{:S(2)}) collective-permute-start(bf16[160,1920]{1,0:T(8,128)(2,1)S(1)} %get-tuple-element.40.refs_3_), channel_id=1, source_target_pairs={{0,8},{8,0},{16,24},{24,16},{1,9},{9,1},{17,25},{25,17},{2,10},{10... | collective-permute-start | bytes 1843208 | tf_op jit(solution)/shard_map/ppermute | solution.py:290
  41.2 7.4 %collective-permute-start.14 = (bf16[160,1920]{1,0:T(8,128)(2,1)}, bf16[160,1920]{1,0:T(8,128)(2,1)}, u32[]{:S(2)}, u32[]{:S(2)}) collective-permute-start(bf16[160,1920]{1,0:T(8,128)(2,1)} %collective-permute-done.13.refs_5_), channel_id=1, source_target_pairs={{0,8},{8,0},{16,24},{24,16},{1,9},{9,1},{17,25},{25,17},{2,10},{10... | collective-permute-start | bytes 1843208 | tf_op jit(solution)/shard_map/ppermute | solution.py:290
  41.2 17.7 %copy-start = (bf16[512,1280]{1,0:T(8,128)(2,1)}, bf16[512,1280]{1,0:T(8,128)(2,1)S(1)}, u32[]{:S(2)}) copy-start(bf16[512,1280]{1,0:T(8,128)(2,1)S(1)} %collective-permute-done.refs_0_) | copy-start | bytes 3932164
  41.2 29.2 %collective-permute-start.1 = (bf16[512,1280]{1,0:T(8,128)(2,1)S(1)}, bf16[512,1280]{1,0:T(8,128)(2,1)}, u32[]{:S(2)}, u32[]{:S(2)}) collective-permute-start(bf16[512,1280]{1,0:T(8,128)(2,1)S(1)} %collective-permute-done.refs_0_), channel_id=1, source_target_pairs={{8,0},{16,8},{9,1},{17,9},{10,2},{18,10},{11,3},{19,11},{12,4},{20... | collective-permute-start | bytes 3932168 | tf_op jit(solution)/shard_map/ppermute | solution.py:103
  42.5 17.0 %collective-permute-start.6 = (bf16[160,1920]{1,0:T(8,128)(2,1)S(1)}, bf16[160,1920]{1,0:T(8,128)(2,1)}, u32[]{:S(2)}, u32[]{:S(2)}) collective-permute-start(bf16[160,1920]{1,0:T(8,128)(2,1)S(1)} %get-tuple-element.41.refs_3_), channel_id=1, source_target_pairs={{0,8},{8,0},{16,24},{24,16},{1,9},{9,1},{17,25},{25,17},{2,10},{10... | collective-permute-start | bytes 1843208 | tf_op jit(solution)/shard_map/ppermute | solution.py:290
  47.6 11.2 %copy-start.16 = (bf16[160,1920]{1,0:T(8,128)(2,1)}, bf16[160,1920]{1,0:T(8,128)(2,1)S(1)}, u32[]{:S(2)}) copy-start(bf16[160,1920]{1,0:T(8,128)(2,1)S(1)} %collective-permute-done.7.refs_5_) | copy-start | bytes 1843204
  47.6 11.9 %collective-permute-start.8 = (bf16[160,1920]{1,0:T(8,128)(2,1)S(1)}, bf16[160,1920]{1,0:T(8,128)(2,1)}, u32[]{:S(2)}, u32[]{:S(2)}) collective-permute-start(bf16[160,1920]{1,0:T(8,128)(2,1)S(1)} %collective-permute-done.7.refs_5_), channel_id=1, source_target_pairs={{0,8},{8,0},{16,24},{24,16},{1,9},{9,1},{17,25},{25,17},{2,10},{10... | collective-permute-start | bytes 1843208 | tf_op jit(solution)/shard_map/ppermute | solution.py:290
  58.9 24.0 %collective-permute-start.16 = (bf16[160,1920]{1,0:T(8,128)(2,1)}, bf16[160,1920]{1,0:T(8,128)(2,1)}, u32[]{:S(2)}, u32[]{:S(2)}) collective-permute-start(bf16[160,1920]{1,0:T(8,128)(2,1)} %get-tuple-element.33), channel_id=1, source_target_pairs={{0,8},{8,0},{16,24},{24,16},{1,9},{9,1},{17,25},{25,17},{2,10},{10... | collective-permute-start | bytes 1843208 | tf_op jit(solution)/shard_map/ppermute | solution.py:290
  59.4 28.1 %collective-permute-start.15 = (bf16[160,1920]{1,0:T(8,128)(2,1)}, bf16[160,1920]{1,0:T(8,128)(2,1)S(1)}, u32[]{:S(2)}, u32[]{:S(2)}) collective-permute-start(bf16[160,1920]{1,0:T(8,128)(2,1)} %get-tuple-element.31), channel_id=1, source_target_pairs={{0,8},{8,0},{16,24},{24,16},{1,9},{9,1},{17,25},{25,17},{2,10},{10... | collective-permute-start | bytes 1843208 | tf_op jit(solution)/shard_map/ppermute | solution.py:290
  69.8 14.4 %collective-permute-start.10 = (bf16[160,1920]{1,0:T(8,128)(2,1)}, bf16[160,1920]{1,0:T(8,128)(2,1)}, u32[]{:S(2)}, u32[]{:S(2)}) collective-permute-start(bf16[160,1920]{1,0:T(8,128)(2,1)} %get-tuple-element.29), channel_id=1, source_target_pairs={{0,8},{8,0},{16,24},{24,16},{1,9},{9,1},{17,25},{25,17},{2,10},{10... | collective-permute-start | bytes 1843208 | tf_op jit(solution)/shard_map/ppermute | solution.py:290
  70.3 12.6 %copy-start.3 = (f32[160,1920]{1,0:T(8,128)S(1)}, f32[160,1920]{1,0:T(8,128)}, u32[]{:S(2)}) copy-start(f32[160,1920]{1,0:T(8,128)} %get-tuple-element.32) | copy-start | bytes 3686404
  70.3 37.2 %collective-permute-start.9 = (bf16[160,1920]{1,0:T(8,128)(2,1)}, bf16[160,1920]{1,0:T(8,128)(2,1)}, u32[]{:S(2)}, u32[]{:S(2)}) collective-permute-start(bf16[160,1920]{1,0:T(8,128)(2,1)} %get-tuple-element.27), channel_id=1, source_target_pairs={{0,8},{8,0},{16,24},{24,16},{1,9},{9,1},{17,25},{25,17},{2,10},{10... | collective-permute-start | bytes 1843208 | tf_op jit(solution)/shard_map/ppermute | solution.py:290
  80.4 3.8 %copy-start.4 = (f32[160,1920]{1,0:T(8,128)S(1)}, f32[160,1920]{1,0:T(8,128)}, u32[]{:S(2)}) copy-start(f32[160,1920]{1,0:T(8,128)} %get-tuple-element.28) | copy-start | bytes 3686404
  80.4 39.6 %collective-permute-start.2 = (bf16[1280,512]{1,0:T(8,128)(2,1)}, bf16[1280,512]{1,0:T(8,128)(2,1)S(1)}, u32[]{:S(2)}, u32[]{:S(2)}) collective-permute-start(bf16[1280,512]{1,0:T(8,128)(2,1)} %get-tuple-element.22), channel_id=1, source_target_pairs={{0,8},{8,16},{1,9},{9,17},{2,10},{10,18},{3,11},{11,19},{4,12},{12... | collective-permute-start | bytes 3932168 | tf_op jit(solution)/shard_map/ppermute | solution.py:103
  84.1 3.4 %copy-start.17 = (f32[20,512]{1,0:T(8,128)S(1)}, f32[20,512]{1,0:T(8,128)}, u32[]{:S(2)}) copy-start(f32[20,512]{1,0:T(8,128)} %get-tuple-element.23) | copy-start | bytes 122884
  84.1 16.8 %collective-permute-start.17 = (bf16[160,1920]{1,0:T(8,128)(2,1)S(1)}, bf16[160,1920]{1,0:T(8,128)(2,1)S(1)}, u32[]{:S(2)}, u32[]{:S(2)}) collective-permute-start(bf16[160,1920]{1,0:T(8,128)(2,1)S(1)} %add_convert_fusion), channel_id=1, source_target_pairs={{0,16},{8,24},{16,0},{24,8},{1,17},{9,25},{17,1},{25,9},{2,18},{10... | collective-permute-start | bytes 1843208 | tf_op jit(solution)/shard_map/ppermute | solution.py:290
  85.4 27.7 %collective-permute-start.11 = (bf16[160,1920]{1,0:T(8,128)(2,1)S(1)}, bf16[160,1920]{1,0:T(8,128)(2,1)}, u32[]{:S(2)}, u32[]{:S(2)}) collective-permute-start(bf16[160,1920]{1,0:T(8,128)(2,1)S(1)} %add_convert_fusion.1), channel_id=1, source_target_pairs={{0,16},{8,24},{16,0},{24,8},{1,17},{9,25},{17,1},{25,9},{2,18},{10... | collective-permute-start | bytes 1843208 | tf_op jit(solution)/shard_map/ppermute | solution.py:290
  87.5 13.4 %copy-start.6 = (bf16[160,1920]{1,0:T(8,128)(2,1)}, bf16[160,1920]{1,0:T(8,128)(2,1)S(1)}, u32[]{:S(2)}) copy-start(bf16[160,1920]{1,0:T(8,128)(2,1)S(1)} %collective-permute-done.15.refs_1_) | copy-start | bytes 1843204
  87.5 32.5 %collective-permute-start.3 = (f32[20,512]{1,0:T(8,128)S(1)}, f32[20,512]{1,0:T(8,128)S(1)}, u32[]{:S(2)}, u32[]{:S(2)}) collective-permute-start(f32[20,512]{1,0:T(8,128)S(1)} %copy-done.17), channel_id=1, source_target_pairs={{0,8},{8,16},{1,9},{9,17},{2,10},{10,18},{3,11},{11,19},{4,12},{12... | collective-permute-start | bytes 122888 | tf_op jit(solution)/shard_map/ppermute | solution.py:103
  100.9 0.8 copy-start.11
  107.5 51.3 %collective-permute-start.22 = (bf16[160,1920]{1,0:T(8,128)(2,1)}, bf16[160,1920]{1,0:T(8,128)(2,1)S(1)}, u32[]{:S(2)}, u32[]{:S(2)}) collective-permute-start(bf16[160,1920]{1,0:T(8,128)(2,1)} %get-tuple-element.37.refs_0_), channel_id=1, source_target_pairs={{0,16},{8,24},{16,0},{24,8},{1,17},{9,25},{17,1},{25,9},{2,18},{10... | collective-permute-start | bytes 1843208 | tf_op jit(solution)/shard_map/ppermute | solution.py:290
  118.9 39.8 %copy-start.5 = (bf16[160,1920]{1,0:T(8,128)(2,1)S(1)}, bf16[160,1920]{1,0:T(8,128)(2,1)}, u32[]{:S(2)}) copy-start(bf16[160,1920]{1,0:T(8,128)(2,1)} %get-tuple-element.37.refs_0_) | copy-start | bytes 1843204
  118.9 40.4 %copy-start.7 = (bf16[160,1920]{1,0:T(8,128)(2,1)S(1)}, bf16[160,1920]{1,0:T(8,128)(2,1)}, u32[]{:S(2)}) copy-start(bf16[160,1920]{1,0:T(8,128)(2,1)} %get-tuple-element.36.refs_0_) | copy-start | bytes 1843204
  118.9 40.5 %collective-permute-start.19 = (bf16[160,1920]{1,0:T(8,128)(2,1)}, bf16[160,1920]{1,0:T(8,128)(2,1)}, u32[]{:S(2)}, u32[]{:S(2)}) collective-permute-start(bf16[160,1920]{1,0:T(8,128)(2,1)} %get-tuple-element.36.refs_0_), channel_id=1, source_target_pairs={{0,16},{8,24},{16,0},{24,8},{1,17},{9,25},{17,1},{25,9},{2,18},{10... | collective-permute-start | bytes 1843208 | tf_op jit(solution)/shard_map/ppermute | solution.py:290
  120.0 0.6 copy-start.13
  120.6 1.1 copy-start.1
  132.4 36.8 %copy-start.18 = (f32[20,512]{1,0:T(8,128)S(1)}, f32[20,512]{1,0:T(8,128)}, u32[]{:S(2)}) copy-start(f32[20,512]{1,0:T(8,128)} %get-tuple-element.25) | copy-start | bytes 122884
  132.4 45.0 %collective-permute-start.4 = (bf16[1280,512]{1,0:T(8,128)(2,1)}, bf16[1280,512]{1,0:T(8,128)(2,1)S(1)}, u32[]{:S(2)}, u32[]{:S(2)}) collective-permute-start(bf16[1280,512]{1,0:T(8,128)(2,1)} %get-tuple-element.24), channel_id=1, source_target_pairs={{0,8},{8,16},{16,24},{1,9},{9,17},{17,25},{2,10},{10,18},{18,26},{... | collective-permute-start | bytes 3932168 | tf_op jit(solution)/shard_map/ppermute | solution.py:103
  158.7 3.6 %collective-permute-start.21 = (bf16[160,1920]{1,0:T(8,128)(2,1)S(1)}, bf16[160,1920]{1,0:T(8,128)(2,1)S(1)}, u32[]{:S(2)}, u32[]{:S(2)}) collective-permute-start(bf16[160,1920]{1,0:T(8,128)(2,1)S(1)} %copy-done.5), channel_id=1, source_target_pairs={{0,8},{8,0},{16,24},{24,16},{1,9},{9,1},{17,25},{25,17},{2,10},{10... | collective-permute-start | bytes 1843208 | tf_op jit(solution)/shard_map/ppermute | solution.py:290
  158.8 4.6 %copy-start.9 = (bf16[160,1920]{1,0:T(8,128)(2,1)}, bf16[160,1920]{1,0:T(8,128)(2,1)S(1)}, u32[]{:S(2)}) copy-start(bf16[160,1920]{1,0:T(8,128)(2,1)S(1)} %collective-permute-done.22.refs_2_) | copy-start | bytes 1843204
  158.8 4.6 %collective-permute-start.23 = (bf16[160,1920]{1,0:T(8,128)(2,1)S(1)}, bf16[160,1920]{1,0:T(8,128)(2,1)}, u32[]{:S(2)}, u32[]{:S(2)}) collective-permute-start(bf16[160,1920]{1,0:T(8,128)(2,1)S(1)} %collective-permute-done.22.refs_2_), channel_id=1, source_target_pairs={{0,8},{8,0},{16,24},{24,16},{1,9},{9,1},{17,25},{25,17},{2,10},{10... | collective-permute-start | bytes 1843208 | tf_op jit(solution)/shard_map/ppermute | solution.py:290
  159.3 12.2 %collective-permute-start.18 = (bf16[160,1920]{1,0:T(8,128)(2,1)S(1)}, bf16[160,1920]{1,0:T(8,128)(2,1)}, u32[]{:S(2)}, u32[]{:S(2)}) collective-permute-start(bf16[160,1920]{1,0:T(8,128)(2,1)S(1)} %copy-done.7), channel_id=1, source_target_pairs={{0,8},{8,0},{16,24},{24,16},{1,9},{9,1},{17,25},{25,17},{2,10},{10... | collective-permute-start | bytes 1843208 | tf_op jit(solution)/shard_map/ppermute | solution.py:290
  159.4 12.1 %collective-permute-start.20 = (bf16[160,1920]{1,0:T(8,128)(2,1)}, bf16[160,1920]{1,0:T(8,128)(2,1)}, u32[]{:S(2)}, u32[]{:S(2)}) collective-permute-start(bf16[160,1920]{1,0:T(8,128)(2,1)} %collective-permute-done.19.refs_2_), channel_id=1, source_target_pairs={{0,8},{8,0},{16,24},{24,16},{1,9},{9,1},{17,25},{25,17},{2,10},{10... | collective-permute-start | bytes 1843208 | tf_op jit(solution)/shard_map/ppermute | solution.py:290
  162.3 0.8 copy-start.12
  169.2 8.2 %collective-permute-start.5 = (f32[20,512]{1,0:T(8,128)S(1)}, f32[20,512]{1,0:T(8,128)S(1)}, u32[]{:S(2)}, u32[]{:S(2)}) collective-permute-start(f32[20,512]{1,0:T(8,128)S(1)} %copy-done.18), channel_id=1, source_target_pairs={{0,8},{8,16},{16,24},{1,9},{9,17},{17,25},{2,10},{10,18},{18,26},{... | collective-permute-start | bytes 122888 | tf_op jit(solution)/shard_map/ppermute | solution.py:103
  177.4 0.6 copy-start.14
  178.0 1.1 copy-start.2

commit v2 on v1

v2 whole, which is shorter than its diff:
```python
import functools
import math

import jax
import jax.numpy as jnp
from jax import lax
from jax.experimental import pallas as pl
from jax.experimental.pallas import tpu as pltpu
from jax.sharding import PartitionSpec as P


HD = 128
FD = 640
EPSILON = 1e-06
DECAY = 0.9
SPAN = 3 * FD
INV_ROOT = FD ** (-0.5)
EXP2_SCALE = HD ** (-0.5) * math.log2(math.e)
LOWEST = -1e30
F32 = jnp.float32
BF16 = jnp.bfloat16
ANY = pl.BlockSpec(memory_space=pl.ANY)


def dot(a, b, a_dim, b_dim):
    return lax.dot_general(a, b, (((a_dim,), (b_dim,)), ((), ())), preferred_element_type=F32)


def cost(flops, bytes_accessed, transcendentals=0):
    return pl.CostEstimate(
        flops=int(flops), bytes_accessed=int(bytes_accessed), transcendentals=int(transcendentals)
    )


CHUNK = 128


def soft(scores, values):
    highest = jnp.max(scores, axis=0, keepdims=True)
    weights = jnp.exp2((scores - highest) * EXP2_SCALE)
    total = jnp.sum(weights, axis=0, keepdims=True)
    return dot(values, weights.astype(BF16), 0, 0), highest, total


def masked(scores, causal, first_key, first_query):
    key_row = lax.broadcasted_iota(jnp.int32, scores.shape, 0) + first_key
    query_row = lax.broadcasted_iota(jnp.int32, scores.shape, 1) + first_query
    allowed = key_row <= query_row if causal else key_row > query_row
    return jnp.where(allowed, scores, LOWEST)


def scaled_to(before, after):
    return jnp.exp2((before - after) * EXP2_SCALE)


def own_kernel(per_step, q_ref, k_ref, v_ref, o_ref, st_ref):
    for g in range(per_step):
        cols = slice(g * HD, (g + 1) * HD)
        for first in range(0, q_ref.shape[0], CHUNK):
            rows = slice(first, first + CHUNK)
            upto = first + CHUNK
            scores = masked(dot(k_ref[:upto, cols], q_ref[rows, cols], 1, 1), True, 0, first)
            mixed, highest, total = soft(scores, v_ref[:upto, cols])
            o_ref[cols, rows] = mixed.astype(BF16)
            st_ref[g : g + 1, rows] = highest
            st_ref[8 + g : 9 + g, rows] = total


def group_kernel(
    per_step, q_ref, far_ref, k_ref, v_ref, pk_ref, pv_ref, o_ref, st_ref, fo_ref, fst_ref, lo_ref, lst_ref
):
    leading = lax.axis_index("ctx") % 2 == 0
    for g in range(per_step):
        cols = slice(g * HD, (g + 1) * HD)
        top, bottom = slice(g, g + 1), slice(8 + g, 9 + g)
        for first in range(0, q_ref.shape[0], CHUNK):
            rows = slice(first, first + CHUNK)
            far = far_ref[rows, cols]
            scores = masked(dot(k_ref[first:, cols], far, 1, 1), False, first, first)
            far_o, far_m, far_l = soft(scores, v_ref[first:, cols])
            guest = jnp.where(leading, far, q_ref[rows, cols])
            mixed, highest, total = soft(dot(pk_ref[:, cols], guest, 1, 1), pv_ref[:, cols])
            far_top = jnp.where(leading, jnp.maximum(far_m, highest), far_m)
            far_keep = scaled_to(far_m, far_top)
            far_add = jnp.where(leading, scaled_to(highest, far_top), 0.0)
            fo_ref[cols, rows] = (far_o * far_keep + mixed * far_add).astype(BF16)
            fst_ref[top, rows] = far_top
            fst_ref[bottom, rows] = far_l * far_keep + total * far_add
            own_m = st_ref[top, rows]
            own_top = jnp.where(leading, own_m, jnp.maximum(own_m, highest))
            own_keep = scaled_to(own_m, own_top)
            own_add = jnp.where(leading, 0.0, scaled_to(highest, own_top))
            lo_ref[cols, rows] = (o_ref[cols, rows].astype(F32) * own_keep + mixed * own_add).astype(BF16)
            lst_ref[top, rows] = own_top
            lst_ref[bottom, rows] = st_ref[bottom, rows] * own_keep + total * own_add


def merge_kernel(per_step, o_ref, st_ref, fo_ref, fst_ref, out_ref):
    valid = lax.axis_index("ctx") >= 2
    for g in range(per_step):
        cols = slice(g * HD, (g + 1) * HD)
        top, bottom = slice(g, g + 1), slice(8 + g, 9 + g)
        own_m = st_ref[top, :]
        far_m = jnp.where(valid, fst_ref[top, :], LOWEST)
        highest = jnp.maximum(own_m, far_m)
        own_keep = scaled_to(own_m, highest)
        far_keep = scaled_to(far_m, highest)
        total = st_ref[bottom, :] * own_keep + fst_ref[bottom, :] * far_keep
        mixed = o_ref[cols, :].astype(F32) * own_keep + fo_ref[cols, :].astype(F32) * far_keep
        out_ref[:, cols] = (mixed / total).T.astype(BF16)


def whole_kernel(
    per_step, q_ref, k_ref, v_ref, pk_ref, pv_ref, fk_ref, fv_ref, fpk_ref, fpv_ref, out_ref
):
    index = lax.axis_index("ctx")
    leading = index % 2 == 0
    valid = index >= 2
    beside = jnp.logical_or(valid, jnp.logical_not(leading))
    for g in range(per_step):
        cols = slice(g * HD, (g + 1) * HD)
        other_k = jnp.where(leading, fpk_ref[:, cols], pk_ref[:, cols])
        other_v = jnp.where(leading, fpv_ref[:, cols], pv_ref[:, cols])
        for first in range(0, q_ref.shape[0], CHUNK):
            rows = slice(first, first + CHUNK)
            upto = first + CHUNK
            queries = q_ref[rows, cols]
            own = masked(dot(k_ref[:upto, cols], queries, 1, 1), True, 0, first)
            far = masked(dot(fk_ref[first:, cols], queries, 1, 1), False, first, first)
            own_o, own_m, own_l = soft(own, v_ref[:upto, cols])
            far_o, far_m, far_l = soft(far, fv_ref[first:, cols])
            other_o, other_m, other_l = soft(dot(other_k, queries, 1, 1), other_v)
            far_m = jnp.where(valid, far_m, LOWEST)
            other_m = jnp.where(beside, other_m, LOWEST)
            highest = jnp.maximum(jnp.maximum(own_m, far_m), other_m)
            own_f = scaled_to(own_m, highest)
            far_f = scaled_to(far_m, highest)
            other_f = scaled_to(other_m, highest)
            total = own_l * own_f + far_l * far_f + other_l * other_f
            mixed = own_o * own_f + far_o * far_f + other_o * other_f
            out_ref[rows, cols] = (mixed / total).T.astype(BF16)


def attention_call(kernel, heads, arrays, firsts, outs, units, into=None):
    rows = arrays[0].shape[0] if isinstance(firsts[0], int) else arrays[0].shape[1]
    per_step = max(
        size
        for size in range(1, 6)
        if heads % size == 0 and all(f % size == 0 for f in firsts + outs if isinstance(f, int))
    )

    def spec(first):
        if first == "t":
            return pl.BlockSpec((per_step * HD, rows), lambda i: (i, 0))
        if first == "s":
            return pl.BlockSpec((16, rows), lambda i: (i, 0))
        return pl.BlockSpec((rows, per_step * HD), lambda i: (0, i + first // per_step))

    def shape(first):
        if first == "t":
            return jax.ShapeDtypeStruct((heads * HD, rows), BF16)
        if first == "s":
            return jax.ShapeDtypeStruct((16 * (heads // per_step), rows), F32)
        return jax.ShapeDtypeStruct(into[0], BF16)

    aliases = {}
    in_specs = [spec(first) for first in firsts]
    body = functools.partial(kernel, per_step)
    if into is not None and into[1] is not None:
        aliases = {len(arrays): 0}
        count = len(arrays)
        arrays = list(arrays) + [into[1]]
        in_specs.append(ANY)
        inner = body
        body = lambda *refs: inner(*refs[:count], *refs[count + 1 :])
    return pl.pallas_call(
        body,
        grid=(heads // per_step,),
        in_specs=in_specs,
        out_specs=[spec(first) for first in outs],
        out_shape=[shape(first) for first in outs],
        input_output_aliases=aliases,
        cost_estimate=cost(
            4 * units * rows * rows * heads * HD,
            len(firsts + outs) * rows * heads * HD * 2,
            units * rows * rows * heads,
        ),
    )(*arrays)


def fetch_rows(parts, masks, target, sems):
    index = lax.axis_index("ctx")
    copies = []
    for number, (part, mask) in enumerate(zip(parts, masks)):
        rows = part.shape[0]
        if mask is None:
            place = target
        else:
            place = target.at[pl.ds(pl.multiple_of((index ^ mask) * rows, 32), rows)]
        copy = pltpu.make_async_copy(part, place, sems.at[number])
        copy.start()
        copies.append(copy)
    return copies


def grads_kernel(masks, split, head, *refs):
    count = len(masks)
    key_ref, value_ref, rate_ref = refs[:3]
    parts = refs[3 : 3 + count]
    outs = refs[3 + count : -7]
    low, scaled, hidden, gate_grad, up_grad, update, sems = refs[-7:]
    copies = fetch_rows(parts, masks, low, sems)
    rate = rate_ref[:, head : head + 1]
    scaled[...] = (rate * value_ref[...].astype(F32)).astype(BF16)
    for copy in copies:
        copy.wait()
    tokens = key_ref.shape[0]
    block = min(256, tokens)

    for first in range(0, tokens, block):
        rows = slice(first, first + block)
        keys = key_ref[rows, :]
        gate = dot(keys, low[:, :FD], 1, 1) * INV_ROOT
        up = dot(keys, low[:, FD : 2 * FD], 1, 1) * INV_ROOT
        back = dot(scaled[rows, :], low[:, 2 * FD :], 1, 0) * INV_ROOT
        sigmoid = 1.0 / (1.0 + jnp.exp(-gate))
        silu = gate * sigmoid
        hidden[rows, :] = (silu * up).astype(BF16)
        gate_grad[rows, :] = (back * up * sigmoid * (1.0 + gate * (1.0 - sigmoid))).astype(BF16)
        up_grad[rows, :] = (back * silu).astype(BF16)
    for first in range(0, FD, 128):
        rows = slice(first, first + 128)
        update[rows, :FD] = dot(gate_grad[:, rows], key_ref[...], 0, 0)
        update[rows, FD : 2 * FD] = dot(up_grad[:, rows], key_ref[...], 0, 0)
        update[rows, 2 * FD :] = dot(scaled[:, rows], hidden[...], 0, 0)
    if split:
        index = lax.axis_index("ctx")
        for out, mask in zip(outs, (3, 1, 2, 0)):
            rows = out.shape[0]
            out[...] = update[pl.ds(pl.multiple_of((index ^ mask) * rows, 32), rows), :].astype(out.dtype)
    else:
        outs[0][...] = update[...]


def head_grads(fw_key, fw_value, fw_rate, gathered, head, split):
    tokens = fw_key.shape[0]
    parts = [part for part, _ in gathered]
    masks = [mask for _, mask in gathered]
    column = pl.BlockSpec((tokens, FD), lambda i: (0, head))
    if split:
        rows = parts[0].shape[0]
        out_shape = tuple(jax.ShapeDtypeStruct((rows, SPAN), kind) for kind in (BF16, BF16, F32, F32))
    else:
        out_shape = (jax.ShapeDtypeStruct((FD, SPAN), F32),)
    out_specs = tuple(pl.BlockSpec(out.shape, lambda i: (0, 0)) for out in out_shape)
    return pl.pallas_call(
        functools.partial(grads_kernel, masks, split, head),
        grid=(1,),
        in_specs=[column, column, pl.BlockSpec(fw_rate.shape, lambda i: (0, 0))] + [ANY] * len(parts),
        out_specs=out_specs,
        out_shape=out_shape,
        scratch_shapes=[
            pltpu.VMEM((FD, SPAN), BF16),
            pltpu.VMEM((tokens, FD), BF16),
            pltpu.VMEM((tokens, FD), BF16),
            pltpu.VMEM((tokens, FD), BF16),
            pltpu.VMEM((tokens, FD), BF16),
            pltpu.VMEM((FD, SPAN), F32),
            pltpu.SemaphoreType.DMA((len(parts),)),
        ],
        cost_estimate=cost(12 * tokens * FD * FD, 8e6, tokens * FD),
        name="head_grads",
    )(fw_key, fw_value, fw_rate, *parts)


def move_kernel(sums, w_ref, m_ref, *refs):
    addends = refs[:sums]
    nw_ref, nm_ref, low_ref = refs[-3:]
    update = addends[0][...]
    for addend in addends[1:]:
        update = update + addend[...].astype(F32)
    weights = w_ref[...]
    momentum = DECAY * m_ref[...] + update
    moved = weights + momentum
    nm_ref[...] = momentum
    for part in range(3):
        cols = slice(part * FD, (part + 1) * FD)
        before = jnp.mean(jnp.square(weights[:, cols]), axis=1, keepdims=True)
        after = jnp.mean(jnp.square(moved[:, cols]), axis=1, keepdims=True)
        fresh = moved[:, cols] * (jnp.sqrt(before + EPSILON) * lax.rsqrt(after + EPSILON))
        nw_ref[:, cols] = fresh
        low_ref[:, cols] = fresh.astype(BF16)


def move_weights(fast_weights, momentum, addends, head, previous):
    rows = fast_weights.shape[0]
    block = 32 if rows % 32 == 0 else rows
    wide = pl.BlockSpec((block, SPAN), lambda i: (i, head))
    own = pl.BlockSpec((block, SPAN), lambda i: (i, 0))
    in_specs = [wide, wide] + [own] * len(addends)
    args = [fast_weights, momentum] + list(addends)
    aliases = {}
    if previous is not None:
        aliases = {len(args): 0, len(args) + 1: 1}
        in_specs += [ANY, ANY]
        args += list(previous)
    full = jax.ShapeDtypeStruct(fast_weights.shape, F32)
    return pl.pallas_call(
        functools.partial(move_kernel, len(addends)),
        grid=(rows // block,),
        in_specs=in_specs,
        out_specs=(wide, wide, own),
        out_shape=(full, full, jax.ShapeDtypeStruct((rows, SPAN), BF16)),
        input_output_aliases=aliases,
        cost_estimate=cost(20 * rows * SPAN, 26 * rows * SPAN),
        name="move_weights",
    )(*args)


def query_kernel(masks, q_ref, *refs):
    count = len(masks)
    parts = refs[:count]
    out_ref, low, sems = refs[-3:]
    for copy in fetch_rows(parts, masks, low, sems):
        copy.wait()
    tokens = q_ref.shape[0]
    block = min(256, tokens)

    for first in range(0, tokens, block):
        rows = slice(first, first + block)
        queries = q_ref[rows, :]
        gate = dot(queries, low[:, :FD], 1, 1) * INV_ROOT
        up = dot(queries, low[:, FD : 2 * FD], 1, 1) * INV_ROOT
        hidden = (gate * (1.0 / (1.0 + jnp.exp(-gate))) * up).astype(BF16)
        out_ref[rows, :] = (dot(hidden, low[:, 2 * FD :], 1, 1) * INV_ROOT).astype(BF16)


def head_query(fw_query, gathered, head, previous):
    tokens = fw_query.shape[0]
    parts = [part for part, _ in gathered]
    masks = [mask for _, mask in gathered]
    column = pl.BlockSpec((tokens, FD), lambda i: (0, head))
    in_specs = [column] + [ANY] * len(parts)
    args = [fw_query] + parts
    aliases = {}
    if previous is not None:
        aliases = {len(args): 0}
        in_specs.append(ANY)
        args.append(previous)
    return pl.pallas_call(
        functools.partial(query_kernel, masks),
        grid=(1,),
        in_specs=in_specs,
        out_specs=column,
        out_shape=jax.ShapeDtypeStruct(fw_query.shape, BF16),
        scratch_shapes=[pltpu.VMEM((FD, SPAN), BF16), pltpu.SemaphoreType.DMA((len(parts),))],
        input_output_aliases=aliases,
        cost_estimate=cost(6 * tokens * FD * FD, 4e6, tokens * FD),
        name="head_query",
    )(*args)


def swapped(array, mask):
    devices = lax.axis_size("ctx")
    return lax.ppermute(array, "ctx", [(i, i ^ mask) for i in range(devices)])


def shifted(array, by):
    devices = lax.axis_size("ctx")
    pairs = [(i, i + by) for i in range(devices) if 0 <= i + by < devices]
    return lax.ppermute(array, "ctx", pairs)


def after(array, *others):
    return lax.optimization_barrier((array,) + others)[0]


class Lane:
    def __init__(self):
        self.ended = None

    def cross(self, array):
        if self.ended is not None:
            array = after(array, self.ended)
        self.ended = swapped(array, 2)
        return self.ended


def gather_rows(lane, shard, paired):
    if not paired:
        return [(lax.all_gather(shard, "ctx", axis=0, tiled=True), None)]
    across = lane.cross(shard)
    beside = swapped(shard, 1)
    return [(shard, 0), (beside, 1), (across, 2), (swapped(across, 1), 3)]


def sum_rows(lane, pieces, paired):
    if not paired:
        return [lax.psum_scatter(pieces[0], "ctx", scatter_dimension=0, tiled=True)]
    far, near, across, own = pieces
    far = swapped(far, 1)
    near = swapped(near, 1)
    total = (across + far.astype(F32)).astype(BF16)
    return [own, near, lane.cross(total)]


def per_device(
    attn_query, attn_key, attn_value, fw_query, fw_key, fw_value, fw_rate, fast_weights, momentum
):
    devices = lax.axis_size("ctx")
    head_local = fw_rate.shape[1]
    paired = devices == 4
    lane = Lane()
    heads = range(head_local)
    all_heads = attn_query.shape[1] // HD
    moved = 2 * all_heads // 5
    stay = all_heads - moved

    low = fast_weights[:, :SPAN].astype(BF16)
    gathered = [gather_rows(lane, low, paired)]
    started = gathered[0][2 if paired else 0][0]
    source = after(fast_weights, low)
    for head in heads[1:]:
        low = source[:, head * SPAN : (head + 1) * SPAN].astype(BF16)
        gathered.append(gather_rows(lane, low, paired))

    pair_key = swapped(attn_key, 1)
    pair_value = swapped(attn_value, 1)
    queries = attn_query[:, moved * HD :]
    pairs = jnp.concatenate([attn_key[:, : moved * HD], attn_value[:, : moved * HD]], axis=1)
    far_query = shifted(after(queries, started), -2)
    far_pairs = shifted(after(pairs, started), 2)
    far_pairs_other = swapped(far_pairs, 1)

    own = attention_call(
        own_kernel, stay, [queries, attn_key, attn_value], [0, moved, moved], ["t", "s"], 0.6
    )
    before = own[1]
    sums = []
    for head in heads:
        pieces = head_grads(after(fw_key, before), fw_value, fw_rate, gathered[head], head, paired)
        before = pieces[-1]
        sums.append(sum_rows(lane, pieces, paired))
    far_o, far_st, own_o, own_st = attention_call(
        group_kernel,
        stay,
        [queries, after(far_query, before), attn_key, attn_value, pair_key, pair_value, *own],
        [0, 0, moved, moved, moved, moved, "t", "s"],
        ["t", "s", "t", "s"],
        1.6,
    )
    far_o = shifted(far_o, 2)
    far_st = shifted(far_st, 2)

    new = None
    new_gathered = []
    for head in heads:
        new_weights, new_momentum, low = move_weights(fast_weights, momentum, sums[head], head, new)
        new = (new_weights, new_momentum)
        new_gathered.append(gather_rows(lane, low, paired))
    attn_out = attention_call(
        whole_kernel,
        moved,
        [attn_query, attn_key, attn_value, pair_key, pair_value, far_pairs, far_pairs, far_pairs_other, far_pairs_other],
        [0, 0, 0, 0, 0, 0, moved, 0, moved],
        [0],
        2.2,
        (attn_query.shape, None),
    )[0]
    fw_out = None
    for head in heads:
        fw_out = head_query(fw_query, new_gathered[head], head, fw_out)
    attn_out = attention_call(
        merge_kernel,
        stay,
        [own_o, own_st, far_o, far_st],
        ["t", "s", "t", "s"],
        [moved],
        0.01,
        (attn_query.shape, attn_out),
    )[0]
    return (attn_out, fw_out, new_weights, new_momentum)


def solution(mesh):
    spec = P(("seq", "ctx"), "head")

    return jax.shard_map(
        per_device, mesh=mesh, in_specs=(spec,) * 9, out_specs=(spec,) * 4, check_vma=False
    )
```

time: 191 us -> 196 us (1.026)
  the two profiles are of different devices: /device:TPU:0 before, /device:TPU:7 now
where the time goes in v2:
time: 196 us
  waiting for transfers between devices  87.9 us (45%)
  Pallas kernels  69.3 us (35%)
  starting transfers between devices  25.3 us (13%)
  local copies, waits for them, and re-layouts  9.88 us (5%)
  other arithmetic  2.17 us (1%)
    ppermute x21, waiting for transfers between devices, swapped(): return lax.ppermute(array, 'ctx', [(i, i ^ mask) for i in range(devices)])  57.4 us
    ppermute x4, waiting for transfers between devices, shifted(): return lax.ppermute(array, 'ctx', pairs)  30.5 us
    pallas_call x4, Pallas kernels, attention_call(): pl.pallas_call(body, grid=(heads // per_step,), in_specs=in_specs, out_sp...  28.5 us
    pallas_call x2, Pallas kernels, head_grads(): pl.pallas_call(functools.partial(grads_kernel, masks, split, head), grid=...  17.9 us
    ppermute x21, starting transfers between devices, swapped(): return lax.ppermute(array, 'ctx', [(i, i ^ mask) for i in range(devices)])  17.1 us
    pallas_call x2, Pallas kernels, move_weights(): pl.pallas_call(functools.partial(move_kernel, len(addends)), grid=(rows /...  11.4 us
    pallas_call x2, Pallas kernels, head_query(): pl.pallas_call(functools.partial(query_kernel, masks), grid=(1,), in_spec...  11.4 us
    ppermute x4, starting transfers between devices, shifted(): return lax.ppermute(array, 'ctx', pairs)  8.26 us
  transfers between devices with their start and end apart: 25, of which 7 were waited for; matrix products, arithmetic and copies ran while one was open for 3% of the time, Pallas kernels for 32%

profile of v2, /device:TPU:7, one launch (start us, length us, event | category | flops | bytes accessed | tf_op | source)
XLA Modules:
  0.0 195.6 jit_solution(13667800235550928249)
XLA Ops:
  0.6 0.0 copy-start.2
  0.7 1.5 slice.27.refs_3_
  2.1 0.0 copy-start.9
  2.1 0.3 collective-permute-start
  2.4 2.2 %slice.26.refs_3_ = bf16[160,1920]{1,0:T(8,128)(2,1)} slice(f32[160,3840]{1,0:T(8,128)} %w_ref.3), slice={[0:160], [1920:3840]} | slice | bytes 1228800 | tf_op jit(solution)/shard_map/slice | solution.py:424
  4.6 12.3 %collective-permute-done.refs_5_ = bf16[160,1920]{1,0:T(8,128)(2,1)S(1)} collective-permute-done((bf16[160,1920]{1,0:T(8,128)(2,1)S(1)}, bf16[160,1920]{1,0:T(8,128)(2,1)S(1)}, u32[]{:S(2)}, u32[]{:S(2)}) %collective-permute-start) | collective-permute-done | bytes 614432 | tf_op jit(solution)/shard_map/ppermute | solution.py:365
  16.9 0.3 collective-permute-start.5
  17.2 1.8 collective-permute-start.2
  19.0 0.5 collective-permute-start.4
  19.5 0.9 copy.17.refs_2_
  20.4 0.9 slice.17.q_ref
  21.3 6.0 %shard_map.120 = (bf16[768,512]{1,0:T(8,128)(2,1)}, f32[48,512]{1,0:T(8,128)}) custom-call(bf16[512,768]{1,0:T(8,128)(2,1)} %slice.17.q_ref, bf16[512,1280]{1,0:T(8,128)(2,1)} %k_ref.5, bf16[512,1280]{1,0:T(8,128)(2,1)} %v_ref.5), custom_call_target="tpu_custom_call" | custom-call | flops 483183808 | bytes 3932160 | tf_op jit(solution)/shard_map/pallas_call | solution.py:176
  27.3 3.8 %collective-permute-done.5.refs_5_ = bf16[160,1920]{1,0:T(8,128)(2,1)} collective-permute-done((bf16[160,1920]{1,0:T(8,128)(2,1)}, bf16[160,1920]{1,0:T(8,128)(2,1)}, u32[]{:S(2)}, u32[]{:S(2)}) %collective-permute-start.5) | collective-permute-done | bytes 614432 | tf_op jit(solution)/shard_map/ppermute | solution.py:365
  31.1 2.4 %collective-permute-start.6 = (bf16[160,1920]{1,0:T(8,128)(2,1)}, bf16[160,1920]{1,0:T(8,128)(2,1)}, u32[]{:S(2)}, u32[]{:S(2)}) collective-permute-start(bf16[160,1920]{1,0:T(8,128)(2,1)} %collective-permute-done.5.refs_5_), channel_id=1, source_target_pairs={{0,8},{8,0},{16,24},{24,16},{1,9},{9,1},{17,25},{25,17},{2,10},{10... | collective-permute-start | bytes 1843208 | tf_op jit(solution)/shard_map/ppermute | solution.py:365
  33.5 0.0 collective-permute-done.2.refs_4_
  33.5 0.0 collective-permute-done.3.refs_6_
  33.5 0.8 copy-done.17
  34.3 9.0 %head_grads.2 = (bf16[160,1920]{1,0:T(8,128)(2,1)}, bf16[160,1920]{1,0:T(8,128)(2,1)}, f32[160,1920]{1,0:T(8,128)}, f32[160,1920]{1,0:T(8,128)}) custom-call(bf16[512,1280]{1,0:T(8,128)(2,1)} %refs_0_.1, bf16[512,1280]{1,0:T(8,128)(2,1)} %refs_1_.3, f32[512,2]{1,0:T(8,128)} %copy.17.refs_2_, bf16[160,1920]{1,0:T(8,128)(2,1)} %copy-done.9, ...), custom_call_target="tpu_custom_call" | custom-call | flops 2516582400 | bytes 8000000 | tf_op jit(solution)/shard_map/head_grads/pallas_call | solution.py:256
  43.3 0.1 collective-permute-start.15
  43.4 0.0 copy-start.4
  43.4 0.0 collective-permute-done.4.refs_4_
  43.4 9.0 %head_grads.3 = (bf16[160,1920]{1,0:T(8,128)(2,1)}, bf16[160,1920]{1,0:T(8,128)(2,1)}, f32[160,1920]{1,0:T(8,128)}, f32[160,1920]{1,0:T(8,128)}) custom-call(bf16[512,1280]{1,0:T(8,128)(2,1)} %refs_0_.1, bf16[512,1280]{1,0:T(8,128)(2,1)} %refs_1_.3, f32[512,2]{1,0:T(8,128)} %copy.17.refs_2_, bf16[160,1920]{1,0:T(8,128)(2,1)} %slice.26.refs_3_, ...), custom_call_target="tpu_custom_call" | custom-call | flops 2516582400 | bytes 8000000 | tf_op jit(solution)/shard_map/head_grads/pallas_call | solution.py:256
  52.4 0.0 slice-start
  52.4 0.0 slice-start.1
  52.4 0.5 collective-permute-start.14
  53.0 0.1 add_convert_fusion
  53.1 0.0 copy-start.3
  53.1 0.3 collective-permute-start.16
  53.4 0.0 slice-done
  53.5 0.2 slice-done.1
  53.6 1.1 pad_maximum_fusion
  54.7 1.4 collective-permute-start.11
  56.2 0.5 collective-permute-start.18
  56.7 1.0 add_convert_fusion.1
  57.7 10.9 %collective-permute-done.16.refs_2_ = bf16[160,1920]{1,0:T(8,128)(2,1)S(1)} collective-permute-done((bf16[160,1920]{1,0:T(8,128)(2,1)S(1)}, bf16[160,1920]{1,0:T(8,128)(2,1)S(1)}, u32[]{:S(2)}, u32[]{:S(2)}) %collective-permute-start.16) | collective-permute-done | bytes 614432 | tf_op jit(solution)/shard_map/ppermute | solution.py:365
  68.6 0.3 collective-permute-start.17
  68.8 1.2 collective-permute-start.7
  70.0 0.1 collective-permute-start.8
  70.1 0.8 copy-done.12
  71.0 0.7 collective-permute-start.13
  71.6 5.7 %move_weights.2 = (f32[160,3840]{1,0:T(8,128)}, f32[160,3840]{1,0:T(8,128)}, bf16[160,1920]{1,0:T(8,128)(2,1)}) custom-call(f32[160,3840]{1,0:T(8,128)} %w_ref.3, f32[160,3840]{1,0:T(8,128)} %m_ref.3, f32[160,1920]{1,0:T(8,128)} %get-tuple-element.38.refs_0_, bf16[160,1920]{1,0:T(8,128)(2,1)} %copy-done.12, bf16[160,1920]{1,0:T(8,128)(2,1)} %copy-done.8), custom_call_target="tpu_custom_call" | custom-call | flops 6144000 | bytes 7987200 | tf_op jit(solution)/shard_map/move_weights/pallas_call | solution.py:308
  77.4 27.0 %collective-permute-done.17.refs_2_ = bf16[160,1920]{1,0:T(8,128)(2,1)} collective-permute-done((bf16[160,1920]{1,0:T(8,128)(2,1)}, bf16[160,1920]{1,0:T(8,128)(2,1)}, u32[]{:S(2)}, u32[]{:S(2)}) %collective-permute-start.17) | collective-permute-done | bytes 614432 | tf_op jit(solution)/shard_map/ppermute | solution.py:365
  104.3 4.3 %collective-permute-start.1 = (bf16[512,768]{1,0:T(8,128)(2,1)}, bf16[512,768]{1,0:T(8,128)(2,1)}, u32[]{:S(2)}, u32[]{:S(2)}) collective-permute-start(bf16[512,768]{1,0:T(8,128)(2,1)} %slice.17.q_ref), channel_id=1, source_target_pairs={{16,0},{24,8},{17,1},{25,9},{18,2},{26,10},{19,3},{27,11},{20,4},{... | collective-permute-start | bytes 2359304 | tf_op jit(solution)/shard_map/ppermute | solution.py:371
  108.6 1.4 collective-permute-start.12
  110.0 5.7 %move_weights.3 = (f32[160,3840]{1,0:T(8,128)}, f32[160,3840]{1,0:T(8,128)}, bf16[160,1920]{1,0:T(8,128)(2,1)}) custom-call(f32[160,3840]{1,0:T(8,128)} %w_ref.3, f32[160,3840]{1,0:T(8,128)} %m_ref.3, f32[160,1920]{1,0:T(8,128)} %get-tuple-element.42.refs_0_, ...), custom_call_target="tpu_custom_call", output_to_operand_aliasing={{0}: (5, {}), {1}: (6, {})} | custom-call | flops 6144000 | bytes 7987200 | tf_op jit(solution)/shard_map/move_weights/pallas_call | solution.py:308
  115.8 3.4 %collective-permute-done.20.refs_2_ = bf16[160,1920]{1,0:T(8,128)(2,1)} collective-permute-done((bf16[160,1920]{1,0:T(8,128)(2,1)}, bf16[160,1920]{1,0:T(8,128)(2,1)}, u32[]{:S(2)}, u32[]{:S(2)}) %collective-permute-start.20) | collective-permute-done | bytes 614432 | tf_op jit(solution)/shard_map/ppermute | solution.py:365
  119.2 0.3 collective-permute-start.21
  119.4 14.7 %collective-permute-done.1.far_ref = bf16[512,768]{1,0:T(8,128)(2,1)} collective-permute-done((bf16[512,768]{1,0:T(8,128)(2,1)}, bf16[512,768]{1,0:T(8,128)(2,1)}, u32[]{:S(2)}, u32[]{:S(2)}) %collective-permute-start.1) | collective-permute-done | bytes 786464 | tf_op jit(solution)/shard_map/ppermute | solution.py:371
  134.1 8.3 %shard_map.121 = (bf16[768,512]{1,0:T(8,128)(2,1)}, f32[48,512]{1,0:T(8,128)}, bf16[768,512]{1,0:T(8,128)(2,1)}, f32[48,512]{1,0:T(8,128)}) custom-call(bf16[512,768]{1,0:T(8,128)(2,1)} %slice.17.q_ref, bf16[512,768]{1,0:T(8,128)(2,1)} %collective-permute-done.1.far_ref, bf16[512,1280]{1,0:T(8,128)(2,1)} %k_ref.5, bf16[512,1280]{1,0:T(8,128)(2,1)} %v_ref.5, ...), custom_call_target="tpu_custom_call" | custom-call | flops 1288490240 | bytes 9437184 | tf_op jit(solution)/shard_map/pallas_call | solution.py:176
  142.4 1.3 collective-permute-start.9
  143.7 1.3 collective-permute-start.10
  145.0 2.6 %collective-permute-start.23 = (bf16[160,1920]{1,0:T(8,128)(2,1)S(1)}, bf16[160,1920]{1,0:T(8,128)(2,1)S(1)}, u32[]{:S(2)}, u32[]{:S(2)}) collective-permute-start(bf16[160,1920]{1,0:T(8,128)(2,1)S(1)} %copy-done.6), channel_id=1, source_target_pairs={{0,8},{8,0},{16,24},{24,16},{1,9},{9,1},{17,25},{25,17},{2,10},{10... | collective-permute-start | bytes 1843208 | tf_op jit(solution)/shard_map/ppermute | solution.py:365
  147.6 15.8 %collective-permute-done.10.refs_3_ = f32[48,512]{1,0:T(8,128)S(1)} collective-permute-done((f32[48,512]{1,0:T(8,128)}, f32[48,512]{1,0:T(8,128)S(1)}, u32[]{:S(2)}, u32[]{:S(2)}) %collective-permute-start.10) | collective-permute-done | bytes 98336 | tf_op jit(solution)/shard_map/ppermute | solution.py:371
  163.5 3.3 %collective-permute-start.24 = (bf16[160,1920]{1,0:T(8,128)(2,1)}, bf16[160,1920]{1,0:T(8,128)(2,1)}, u32[]{:S(2)}, u32[]{:S(2)}) collective-permute-start(bf16[160,1920]{1,0:T(8,128)(2,1)} %collective-permute-done.20.refs_2_), channel_id=1, source_target_pairs={{0,8},{8,0},{16,24},{24,16},{1,9},{9,1},{17,25},{25,17},{2,10},{10... | collective-permute-start | bytes 1843208 | tf_op jit(solution)/shard_map/ppermute | solution.py:365
  166.7 0.1 collective-permute-start.19
  166.8 0.4 collective-permute-start.22
  167.2 10.8 %shard_map.122.refs_4_ = bf16[512,1280]{1,0:T(8,128)(2,1)} custom-call(bf16[512,1280]{1,0:T(8,128)(2,1)} %q_ref.3, bf16[512,1280]{1,0:T(8,128)(2,1)} %k_ref.5, bf16[512,1280]{1,0:T(8,128)(2,1)} %v_ref.5, bf16[512,1280]{1,0:T(8,128)(2,1)} %collective-permute-done.7.pk_ref, bf16[512,1280]{1,0:T(8,128)(2,1)} %collective-permute-done.8.pv_ref, ...), custom_call_target="tpu_custom_call" | custom-call | flops 1181116032 | bytes 5242880 | tf_op jit(solution)/shard_map/pallas_call | solution.py:176
  178.0 0.0 copy-start.5
  178.0 0.9 copy-done.5
  178.9 3.4 %shard_map.123 = bf16[512,1280]{1,0:T(8,128)(2,1)} custom-call(bf16[768,512]{1,0:T(8,128)(2,1)} %get-tuple-element.45.refs_0_, f32[48,512]{1,0:T(8,128)} %get-tuple-element.46.refs_1_, bf16[768,512]{1,0:T(8,128)(2,1)} %copy-done.5, f32[48,512]{1,0:T(8,128)} %copy-done.13, bf16[512,1280]{1,0:T(8,128)(2,1)} %shard_map.122.refs_4_), custom_call_target="tpu_custom_call", output_to_operand_aliasing={{}: (4, {})} | custom-call | flops 8053063 | bytes 3932160 | tf_op jit(solution)/shard_map/pallas_call | solution.py:176
  182.3 0.8 copy-done.10
  183.1 5.7 %head_query.2.refs_4_ = bf16[512,1280]{1,0:T(8,128)(2,1)} custom-call(bf16[512,1280]{1,0:T(8,128)(2,1)} %q_ref.5, bf16[160,1920]{1,0:T(8,128)(2,1)} %get-tuple-element.62.refs_0_, bf16[160,1920]{1,0:T(8,128)(2,1)} %copy-done.10, bf16[160,1920]{1,0:T(8,128)(2,1)} %collective-permute-done.20.refs_2_, bf16[160,1920]{1,0:T(8,128)(2,1)} %collective-permute-done.24.refs_3_), custom_call_target="tpu_custom_call" | custom-call | flops 1258291200 | bytes 4000000 | tf_op jit(solution)/shard_map/head_query/pallas_call | solution.py:350
  188.9 0.8 copy-done.11
  189.7 5.7 %head_query.3 = bf16[512,1280]{1,0:T(8,128)(2,1)} custom-call(bf16[512,1280]{1,0:T(8,128)(2,1)} %q_ref.5, bf16[160,1920]{1,0:T(8,128)(2,1)} %get-tuple-element.63.refs_0_, bf16[160,1920]{1,0:T(8,128)(2,1)} %copy-done.11, bf16[160,1920]{1,0:T(8,128)(2,1)} %collective-permute-done.21.refs_2_, ...), custom_call_target="tpu_custom_call", output_to_operand_aliasing={{}: (5, {})} | custom-call | flops 1258291200 | bytes 4000000 | tf_op jit(solution)/shard_map/head_query/pallas_call | solution.py:350
  (43 shorter events, 0.1 us)
Async XLA Ops:
  0.6 18.9 %copy-start.14 = (f32[512,2]{0,1:T(2,128)S(1)}, f32[512,2]{0,1:T(2,128)}, u32[]{:S(2)}) copy-start(f32[512,2]{0,1:T(2,128)} %param.15) | copy-start | bytes 12292
  0.6 19.7 %copy-start.2 = (bf16[512,1280]{1,0:T(8,128)(2,1)S(1)}, bf16[512,1280]{1,0:T(8,128)(2,1)}, u32[]{:S(2)}) copy-start(bf16[512,1280]{1,0:T(8,128)(2,1)} %q_ref.3) | copy-start | bytes 3932164
  2.1 19.2 %copy-start.9 = (bf16[160,1920]{1,0:T(8,128)(2,1)}, bf16[160,1920]{1,0:T(8,128)(2,1)S(1)}, u32[]{:S(2)}) copy-start(bf16[160,1920]{1,0:T(8,128)(2,1)S(1)} %slice.27.refs_3_) | copy-start | bytes 1843204
  2.1 14.8 %collective-permute-start = (bf16[160,1920]{1,0:T(8,128)(2,1)S(1)}, bf16[160,1920]{1,0:T(8,128)(2,1)S(1)}, u32[]{:S(2)}, u32[]{:S(2)}) collective-permute-start(bf16[160,1920]{1,0:T(8,128)(2,1)S(1)} %slice.27.refs_3_), channel_id=1, source_target_pairs={{0,16},{8,24},{16,0},{24,8},{1,17},{9,25},{17,1},{25,9},{2,18},{10... | collective-permute-start | bytes 1843208 | tf_op jit(solution)/shard_map/ppermute | solution.py:365
  16.9 10.4 %copy-start.16 = (bf16[160,1920]{1,0:T(8,128)(2,1)}, bf16[160,1920]{1,0:T(8,128)(2,1)S(1)}, u32[]{:S(2)}) copy-start(bf16[160,1920]{1,0:T(8,128)(2,1)S(1)} %collective-permute-done.refs_5_) | copy-start | bytes 1843204
  16.9 14.2 %collective-permute-start.5 = (bf16[160,1920]{1,0:T(8,128)(2,1)}, bf16[160,1920]{1,0:T(8,128)(2,1)}, u32[]{:S(2)}, u32[]{:S(2)}) collective-permute-start(bf16[160,1920]{1,0:T(8,128)(2,1)} %slice.26.refs_3_), channel_id=1, source_target_pairs={{0,16},{8,24},{16,0},{24,8},{1,17},{9,25},{17,1},{25,9},{2,18},{10... | collective-permute-start | bytes 1843208 | tf_op jit(solution)/shard_map/ppermute | solution.py:365
  17.2 16.3 %collective-permute-start.2 = (bf16[160,1920]{1,0:T(8,128)(2,1)S(1)}, bf16[160,1920]{1,0:T(8,128)(2,1)S(1)}, u32[]{:S(2)}, u32[]{:S(2)}) collective-permute-start(bf16[160,1920]{1,0:T(8,128)(2,1)S(1)} %slice.27.refs_3_), channel_id=1, source_target_pairs={{0,8},{8,0},{16,24},{24,16},{1,9},{9,1},{17,25},{25,17},{2,10},{10... | collective-permute-start | bytes 1843208 | tf_op jit(solution)/shard_map/ppermute | solution.py:365
  19.0 14.5 %collective-permute-start.3 = (bf16[160,1920]{1,0:T(8,128)(2,1)S(1)}, bf16[160,1920]{1,0:T(8,128)(2,1)}, u32[]{:S(2)}, u32[]{:S(2)}) collective-permute-start(bf16[160,1920]{1,0:T(8,128)(2,1)S(1)} %collective-permute-done.refs_5_), channel_id=1, source_target_pairs={{0,8},{8,0},{16,24},{24,16},{1,9},{9,1},{17,25},{25,17},{2,10},{10... | collective-permute-start | bytes 1843208 | tf_op jit(solution)/shard_map/ppermute | solution.py:365
  19.0 24.4 %collective-permute-start.4 = (bf16[160,1920]{1,0:T(8,128)(2,1)}, bf16[160,1920]{1,0:T(8,128)(2,1)}, u32[]{:S(2)}, u32[]{:S(2)}) collective-permute-start(bf16[160,1920]{1,0:T(8,128)(2,1)} %slice.26.refs_3_), channel_id=1, source_target_pairs={{0,8},{8,0},{16,24},{24,16},{1,9},{9,1},{17,25},{25,17},{2,10},{10... | collective-permute-start | bytes 1843208 | tf_op jit(solution)/shard_map/ppermute | solution.py:365
  31.1 12.3 %collective-permute-start.6 = (bf16[160,1920]{1,0:T(8,128)(2,1)}, bf16[160,1920]{1,0:T(8,128)(2,1)}, u32[]{:S(2)}, u32[]{:S(2)}) collective-permute-start(bf16[160,1920]{1,0:T(8,128)(2,1)} %collective-permute-done.5.refs_5_), channel_id=1, source_target_pairs={{0,8},{8,0},{16,24},{24,16},{1,9},{9,1},{17,25},{25,17},{2,10},{10... | collective-permute-start | bytes 1843208 | tf_op jit(solution)/shard_map/ppermute | solution.py:365
  33.5 0.8 copy-start.17
  43.3 9.7 %collective-permute-start.15 = (bf16[160,1920]{1,0:T(8,128)(2,1)}, bf16[160,1920]{1,0:T(8,128)(2,1)S(1)}, u32[]{:S(2)}, u32[]{:S(2)}) collective-permute-start(bf16[160,1920]{1,0:T(8,128)(2,1)} %get-tuple-element.54), channel_id=1, source_target_pairs={{0,8},{8,0},{16,24},{24,16},{1,9},{9,1},{17,25},{25,17},{2,10},{10... | collective-permute-start | bytes 1843208 | tf_op jit(solution)/shard_map/ppermute | solution.py:365
  43.4 9.6 %copy-start.4 = (f32[160,1920]{1,0:T(8,128)S(1)}, f32[160,1920]{1,0:T(8,128)}, u32[]{:S(2)}) copy-start(f32[160,1920]{1,0:T(8,128)} %get-tuple-element.53) | copy-start | bytes 3686404
  52.4 1.0 slice-start
  52.4 1.2 slice-start.1
  52.4 4.3 %collective-permute-start.14 = (bf16[160,1920]{1,0:T(8,128)(2,1)}, bf16[160,1920]{1,0:T(8,128)(2,1)S(1)}, u32[]{:S(2)}, u32[]{:S(2)}) collective-permute-start(bf16[160,1920]{1,0:T(8,128)(2,1)} %get-tuple-element.52), channel_id=1, source_target_pairs={{0,8},{8,0},{16,24},{24,16},{1,9},{9,1},{17,25},{25,17},{2,10},{10... | collective-permute-start | bytes 1843208 | tf_op jit(solution)/shard_map/ppermute | solution.py:365
  53.1 3.1 %copy-start.15 = (bf16[160,1920]{1,0:T(8,128)(2,1)S(1)}, bf16[160,1920]{1,0:T(8,128)(2,1)}, u32[]{:S(2)}) copy-start(bf16[160,1920]{1,0:T(8,128)(2,1)} %get-tuple-element.57) | copy-start | bytes 1843204
  53.1 3.6 %copy-start.3 = (f32[160,1920]{1,0:T(8,128)S(1)}, f32[160,1920]{1,0:T(8,128)}, u32[]{:S(2)}) copy-start(f32[160,1920]{1,0:T(8,128)} %get-tuple-element.51) | copy-start | bytes 3686404
  53.1 15.4 %collective-permute-start.16 = (bf16[160,1920]{1,0:T(8,128)(2,1)S(1)}, bf16[160,1920]{1,0:T(8,128)(2,1)S(1)}, u32[]{:S(2)}, u32[]{:S(2)}) collective-permute-start(bf16[160,1920]{1,0:T(8,128)(2,1)S(1)} %add_convert_fusion), channel_id=1, source_target_pairs={{0,16},{8,24},{16,0},{24,8},{1,17},{9,25},{17,1},{25,9},{2,18},{10... | collective-permute-start | bytes 1843208 | tf_op jit(solution)/shard_map/ppermute | solution.py:365
  53.6 16.4 %copy-start.1 = (bf16[512,1280]{1,0:T(8,128)(2,1)S(1)}, bf16[512,1280]{1,0:T(8,128)(2,1)}, u32[]{:S(2)}) copy-start(bf16[512,1280]{1,0:T(8,128)(2,1)} %v_ref.5) | copy-start | bytes 3932164
  54.7 14.1 %copy-start = (bf16[512,1280]{1,0:T(8,128)(2,1)S(1)}, bf16[512,1280]{1,0:T(8,128)(2,1)}, u32[]{:S(2)}) copy-start(bf16[512,1280]{1,0:T(8,128)(2,1)} %k_ref.5) | copy-start | bytes 3932164
  54.7 49.6 %collective-permute-start.11 = (bf16[512,1024]{1,0:T(8,128)(2,1)}, bf16[512,1024]{1,0:T(8,128)(2,1)}, u32[]{:S(2)}, u32[]{:S(2)}) collective-permute-start(bf16[512,1024]{1,0:T(8,128)(2,1)} %pad_maximum_fusion), channel_id=1, source_target_pairs={{0,16},{8,24},{1,17},{9,25},{2,18},{10,26},{3,19},{11,27},{4,20},{... | collective-permute-start | bytes 3145736 | tf_op jit(solution)/shard_map/ppermute | solution.py:371
  56.2 13.9 %collective-permute-start.18 = (bf16[160,1920]{1,0:T(8,128)(2,1)S(1)}, bf16[160,1920]{1,0:T(8,128)(2,1)S(1)}, u32[]{:S(2)}, u32[]{:S(2)}) collective-permute-start(bf16[160,1920]{1,0:T(8,128)(2,1)S(1)} %copy-done.15), channel_id=1, source_target_pairs={{0,8},{8,0},{16,24},{24,16},{1,9},{9,1},{17,25},{25,17},{2,10},{10... | collective-permute-start | bytes 1843208 | tf_op jit(solution)/shard_map/ppermute | solution.py:365
  68.6 1.5 copy-start.8
  68.6 35.7 %collective-permute-start.17 = (bf16[160,1920]{1,0:T(8,128)(2,1)}, bf16[160,1920]{1,0:T(8,128)(2,1)}, u32[]{:S(2)}, u32[]{:S(2)}) collective-permute-start(bf16[160,1920]{1,0:T(8,128)(2,1)} %add_convert_fusion.1), channel_id=1, source_target_pairs={{0,16},{8,24},{16,0},{24,8},{1,17},{9,25},{17,1},{25,9},{2,18},{10... | collective-permute-start | bytes 1843208 | tf_op jit(solution)/shard_map/ppermute | solution.py:365
  68.8 65.3 %collective-permute-start.7 = (bf16[512,1280]{1,0:T(8,128)(2,1)S(1)}, bf16[512,1280]{1,0:T(8,128)(2,1)}, u32[]{:S(2)}, u32[]{:S(2)}) collective-permute-start(bf16[512,1280]{1,0:T(8,128)(2,1)S(1)} %copy-done), channel_id=1, source_target_pairs={{0,8},{8,0},{16,24},{24,16},{1,9},{9,1},{17,25},{25,17},{2,10},{10... | collective-permute-start | bytes 3932168 | tf_op jit(solution)/shard_map/ppermute | solution.py:365
  70.0 64.1 %collective-permute-start.8 = (bf16[512,1280]{1,0:T(8,128)(2,1)S(1)}, bf16[512,1280]{1,0:T(8,128)(2,1)}, u32[]{:S(2)}, u32[]{:S(2)}) collective-permute-start(bf16[512,1280]{1,0:T(8,128)(2,1)S(1)} %copy-done.1), channel_id=1, source_target_pairs={{0,8},{8,0},{16,24},{24,16},{1,9},{9,1},{17,25},{25,17},{2,10},{10... | collective-permute-start | bytes 3932168 | tf_op jit(solution)/shard_map/ppermute | solution.py:365
  70.1 0.8 copy-start.12
  71.0 37.6 %collective-permute-start.13 = (bf16[160,1920]{1,0:T(8,128)(2,1)}, bf16[160,1920]{1,0:T(8,128)(2,1)}, u32[]{:S(2)}, u32[]{:S(2)}) collective-permute-start(bf16[160,1920]{1,0:T(8,128)(2,1)} %get-tuple-element.50), channel_id=1, source_target_pairs={{0,8},{8,0},{16,24},{24,16},{1,9},{9,1},{17,25},{25,17},{2,10},{10... | collective-permute-start | bytes 1843208 | tf_op jit(solution)/shard_map/ppermute | solution.py:365
  104.3 14.8 %collective-permute-start.20 = (bf16[160,1920]{1,0:T(8,128)(2,1)}, bf16[160,1920]{1,0:T(8,128)(2,1)}, u32[]{:S(2)}, u32[]{:S(2)}) collective-permute-start(bf16[160,1920]{1,0:T(8,128)(2,1)} %get-tuple-element.62.refs_0_), channel_id=1, source_target_pairs={{0,16},{8,24},{16,0},{24,8},{1,17},{9,25},{17,1},{25,9},{2,18},{10... | collective-permute-start | bytes 1843208 | tf_op jit(solution)/shard_map/ppermute | solution.py:365
  104.3 29.8 %collective-permute-start.1 = (bf16[512,768]{1,0:T(8,128)(2,1)}, bf16[512,768]{1,0:T(8,128)(2,1)}, u32[]{:S(2)}, u32[]{:S(2)}) collective-permute-start(bf16[512,768]{1,0:T(8,128)(2,1)} %slice.17.q_ref), channel_id=1, source_target_pairs={{16,0},{24,8},{17,1},{25,9},{18,2},{26,10},{19,3},{27,11},{20,4},{... | collective-permute-start | bytes 2359304 | tf_op jit(solution)/shard_map/ppermute | solution.py:371
  108.6 58.1 %collective-permute-start.12 = (bf16[512,1024]{1,0:T(8,128)(2,1)}, bf16[512,1024]{1,0:T(8,128)(2,1)}, u32[]{:S(2)}, u32[]{:S(2)}) collective-permute-start(bf16[512,1024]{1,0:T(8,128)(2,1)} %collective-permute-done.11.fk_ref.fv_ref), channel_id=1, source_target_pairs={{0,8},{8,0},{16,24},{24,16},{1,9},{9,1},{17,25},{25,17},{2,10},{10... | collective-permute-start | bytes 3145736 | tf_op jit(solution)/shard_map/ppermute | solution.py:365
  119.2 47.7 %collective-permute-start.21 = (bf16[160,1920]{1,0:T(8,128)(2,1)}, bf16[160,1920]{1,0:T(8,128)(2,1)}, u32[]{:S(2)}, u32[]{:S(2)}) collective-permute-start(bf16[160,1920]{1,0:T(8,128)(2,1)} %get-tuple-element.63.refs_0_), channel_id=1, source_target_pairs={{0,16},{8,24},{16,0},{24,8},{1,17},{9,25},{17,1},{25,9},{2,18},{10... | collective-permute-start | bytes 1843208 | tf_op jit(solution)/shard_map/ppermute | solution.py:365
  134.1 10.9 %copy-start.6 = (bf16[160,1920]{1,0:T(8,128)(2,1)S(1)}, bf16[160,1920]{1,0:T(8,128)(2,1)}, u32[]{:S(2)}) copy-start(bf16[160,1920]{1,0:T(8,128)(2,1)} %get-tuple-element.62.refs_0_) | copy-start | bytes 1843204
  134.1 32.6 %copy-start.7 = (bf16[160,1920]{1,0:T(8,128)(2,1)S(1)}, bf16[160,1920]{1,0:T(8,128)(2,1)}, u32[]{:S(2)}) copy-start(bf16[160,1920]{1,0:T(8,128)(2,1)} %get-tuple-element.63.refs_0_) | copy-start | bytes 1843204
  142.4 35.6 %collective-permute-start.9 = (bf16[768,512]{1,0:T(8,128)(2,1)}, bf16[768,512]{1,0:T(8,128)(2,1)S(1)}, u32[]{:S(2)}, u32[]{:S(2)}) collective-permute-start(bf16[768,512]{1,0:T(8,128)(2,1)} %get-tuple-element.47), channel_id=1, source_target_pairs={{0,16},{8,24},{1,17},{9,25},{2,18},{10,26},{3,19},{11,27},{4,20},{... | collective-permute-start | bytes 2359304 | tf_op jit(solution)/shard_map/ppermute | solution.py:371
  143.7 19.7 %collective-permute-start.10 = (f32[48,512]{1,0:T(8,128)}, f32[48,512]{1,0:T(8,128)S(1)}, u32[]{:S(2)}, u32[]{:S(2)}) collective-permute-start(f32[48,512]{1,0:T(8,128)} %get-tuple-element.48), channel_id=1, source_target_pairs={{0,16},{8,24},{1,17},{9,25},{2,18},{10,26},{3,19},{11,27},{4,20},{... | collective-permute-start | bytes 294920 | tf_op jit(solution)/shard_map/ppermute | solution.py:371
  145.0 37.3 %collective-permute-start.23 = (bf16[160,1920]{1,0:T(8,128)(2,1)S(1)}, bf16[160,1920]{1,0:T(8,128)(2,1)S(1)}, u32[]{:S(2)}, u32[]{:S(2)}) collective-permute-start(bf16[160,1920]{1,0:T(8,128)(2,1)S(1)} %copy-done.6), channel_id=1, source_target_pairs={{0,8},{8,0},{16,24},{24,16},{1,9},{9,1},{17,25},{25,17},{2,10},{10... | collective-permute-start | bytes 1843208 | tf_op jit(solution)/shard_map/ppermute | solution.py:365
  163.5 14.6 %copy-start.13 = (f32[48,512]{1,0:T(8,128)}, f32[48,512]{1,0:T(8,128)S(1)}, u32[]{:S(2)}) copy-start(f32[48,512]{1,0:T(8,128)S(1)} %collective-permute-done.10.refs_3_) | copy-start | bytes 294916
  163.5 18.8 %collective-permute-start.24 = (bf16[160,1920]{1,0:T(8,128)(2,1)}, bf16[160,1920]{1,0:T(8,128)(2,1)}, u32[]{:S(2)}, u32[]{:S(2)}) collective-permute-start(bf16[160,1920]{1,0:T(8,128)(2,1)} %collective-permute-done.20.refs_2_), channel_id=1, source_target_pairs={{0,8},{8,0},{16,24},{24,16},{1,9},{9,1},{17,25},{25,17},{2,10},{10... | collective-permute-start | bytes 1843208 | tf_op jit(solution)/shard_map/ppermute | solution.py:365
  166.7 22.1 %collective-permute-start.19 = (bf16[160,1920]{1,0:T(8,128)(2,1)S(1)}, bf16[160,1920]{1,0:T(8,128)(2,1)S(1)}, u32[]{:S(2)}, u32[]{:S(2)}) collective-permute-start(bf16[160,1920]{1,0:T(8,128)(2,1)S(1)} %copy-done.7), channel_id=1, source_target_pairs={{0,8},{8,0},{16,24},{24,16},{1,9},{9,1},{17,25},{25,17},{2,10},{10... | collective-permute-start | bytes 1843208 | tf_op jit(solution)/shard_map/ppermute | solution.py:365
  166.8 22.1 %collective-permute-start.22 = (bf16[160,1920]{1,0:T(8,128)(2,1)}, bf16[160,1920]{1,0:T(8,128)(2,1)}, u32[]{:S(2)}, u32[]{:S(2)}) collective-permute-start(bf16[160,1920]{1,0:T(8,128)(2,1)} %collective-permute-done.21.refs_2_), channel_id=1, source_target_pairs={{0,8},{8,0},{16,24},{24,16},{1,9},{9,1},{17,25},{25,17},{2,10},{10... | collective-permute-start | bytes 1843208 | tf_op jit(solution)/shard_map/ppermute | solution.py:365
  178.0 0.9 copy-start.5
  182.3 0.8 copy-start.10
  188.9 0.9 copy-start.11

commit v3 on v2

--- a/solution.py
+++ b/solution.py
@@ -19,7 +19,8 @@
 LOWEST = -1e30
 F32 = jnp.float32
 BF16 = jnp.bfloat16
-ANY = pl.BlockSpec(memory_space=pl.ANY)
+ANY = pl.BlockSpec(memory_space=pltpu.HBM)
+PARAMS = pltpu.CompilerParams(vmem_limit_bytes=67043328)
 
 
 def dot(a, b, a_dim, b_dim):
@@ -63,7 +64,7 @@
             mixed, highest, total = soft(scores, v_ref[:upto, cols])
             o_ref[cols, rows] = mixed.astype(BF16)
             st_ref[g : g + 1, rows] = highest
-            st_ref[8 + g : 9 + g, rows] = total
+            st_ref[per_step + g : per_step + g + 1, rows] = total
 
 
 def group_kernel(
@@ -72,7 +73,7 @@
     leading = lax.axis_index("ctx") % 2 == 0
     for g in range(per_step):
         cols = slice(g * HD, (g + 1) * HD)
-        top, bottom = slice(g, g + 1), slice(8 + g, 9 + g)
+        top, bottom = slice(g, g + 1), slice(per_step + g, per_step + g + 1)
         for first in range(0, q_ref.shape[0], CHUNK):
             rows = slice(first, first + CHUNK)
             far = far_ref[rows, cols]
@@ -99,7 +100,7 @@
     valid = lax.axis_index("ctx") >= 2
     for g in range(per_step):
         cols = slice(g * HD, (g + 1) * HD)
-        top, bottom = slice(g, g + 1), slice(8 + g, 9 + g)
+        top, bottom = slice(g, g + 1), slice(per_step + g, per_step + g + 1)
         own_m = st_ref[top, :]
         far_m = jnp.where(valid, fst_ref[top, :], LOWEST)
         highest = jnp.maximum(own_m, far_m)
@@ -141,26 +142,28 @@
             out_ref[rows, cols] = (mixed / total).T.astype(BF16)
 
 
-def attention_call(kernel, heads, arrays, firsts, outs, units, into=None):
+def attention_call(kernel, heads, arrays, firsts, outs, units, into=None, most=5):
     rows = arrays[0].shape[0] if isinstance(firsts[0], int) else arrays[0].shape[1]
     per_step = max(
         size
-        for size in range(1, 6)
+        for size in range(1, most + 1)
         if heads % size == 0 and all(f % size == 0 for f in firsts + outs if isinstance(f, int))
     )
+
+    stat_rows = 8 * pl.cdiv(2 * per_step, 8)
 
     def spec(first):
         if first == "t":
             return pl.BlockSpec((per_step * HD, rows), lambda i: (i, 0))
         if first == "s":
-            return pl.BlockSpec((16, rows), lambda i: (i, 0))
+            return pl.BlockSpec((stat_rows, rows), lambda i: (i, 0))
         return pl.BlockSpec((rows, per_step * HD), lambda i: (0, i + first // per_step))
 
     def shape(first):
         if first == "t":
             return jax.ShapeDtypeStruct((heads * HD, rows), BF16)
         if first == "s":
-            return jax.ShapeDtypeStruct((16 * (heads // per_step), rows), F32)
+            return jax.ShapeDtypeStruct((stat_rows * (heads // per_step), rows), F32)
         return jax.ShapeDtypeStruct(into[0], BF16)
 
     aliases = {}
@@ -180,6 +183,7 @@
         out_specs=[spec(first) for first in outs],
         out_shape=[shape(first) for first in outs],
         input_output_aliases=aliases,
+        compiler_params=PARAMS,
         cost_estimate=cost(
             4 * units * rows * rows * heads * HD,
             len(firsts + outs) * rows * heads * HD * 2,
@@ -188,89 +192,171 @@
     )(*arrays)
 
 
-def fetch_rows(parts, masks, target, sems):
-    index = lax.axis_index("ctx")
-    copies = []
-    for number, (part, mask) in enumerate(zip(parts, masks)):
-        rows = part.shape[0]
-        if mask is None:
-            place = target
-        else:
-            place = target.at[pl.ds(pl.multiple_of((index ^ mask) * rows, 32), rows)]
-        copy = pltpu.make_async_copy(part, place, sems.at[number])
+def rows_of(mask, rows):
+    return pl.ds(pl.multiple_of((lax.axis_index("ctx") ^ mask) * rows, 32), rows)
+
+
+class Copies:
+    def __init__(self, sems):
+        self.sems = sems
+        self.used = 0
+
+    def start(self, source, target):
+        copy = pltpu.make_async_copy(source, target, self.sems.at[self.used])
+        self.used += 1
         copy.start()
-        copies.append(copy)
-    return copies
+        return copy
+
+    def part(self, parts, masks, low, third):
+        cols = slice(third * FD, (third + 1) * FD)
+        copies = []
+        for part, mask in zip(parts, masks):
+            rows = part.shape[0]
+            place = slice(None) if mask is None else rows_of(mask, rows)
+            copies.append(self.start(part.at[:, cols], low.at[place, cols]))
+        return copies
+
+
+def wait(copies):
+    for copy in copies:
+        copy.wait()
 
 
 def grads_kernel(masks, split, head, *refs):
     count = len(masks)
-    key_ref, value_ref, rate_ref = refs[:3]
+    rate_ref, key_hbm, value_hbm = refs[:3]
     parts = refs[3 : 3 + count]
-    outs = refs[3 + count : -7]
-    low, scaled, hidden, gate_grad, up_grad, update, sems = refs[-7:]
-    copies = fetch_rows(parts, masks, low, sems)
-    rate = rate_ref[:, head : head + 1]
-    scaled[...] = (rate * value_ref[...].astype(F32)).astype(BF16)
-    for copy in copies:
-        copy.wait()
+    outs = refs[3 + count : -10]
+    key_ref, value_ref, low, scaled, hidden, gate_grad, up_grad, update, stage, sems = refs[-10:]
+    mine = slice(head * FD, (head + 1) * FD)
+    copies = Copies(sems)
+    key_copy = copies.start(key_hbm.at[:, mine], key_ref)
+    gate_copies = copies.part(parts, masks, low, 0)
+    up_copies = copies.part(parts, masks, low, 1)
+    value_copy = copies.start(value_hbm.at[:, mine], value_ref)
+    back_copies = copies.part(parts, masks, low, 2)
     tokens = key_ref.shape[0]
+    rate = jnp.broadcast_to(rate_ref[head : head + 1, :], (8, tokens)).T[:, :1]
     block = min(256, tokens)
-
     for first in range(0, tokens, block):
         rows = slice(first, first + block)
+        if first == 0:
+            wait([key_copy] + gate_copies)
         keys = key_ref[rows, :]
         gate = dot(keys, low[:, :FD], 1, 1) * INV_ROOT
+        if first == 0:
+            wait(up_copies)
         up = dot(keys, low[:, FD : 2 * FD], 1, 1) * INV_ROOT
+        if first == 0:
+            wait([value_copy])
+            scaled[...] = (rate * value_ref[...].astype(F32)).astype(BF16)
+            wait(back_copies)
         back = dot(scaled[rows, :], low[:, 2 * FD :], 1, 0) * INV_ROOT
         sigmoid = 1.0 / (1.0 + jnp.exp(-gate))
         silu = gate * sigmoid
         hidden[rows, :] = (silu * up).astype(BF16)
         gate_grad[rows, :] = (back * up * sigmoid * (1.0 + gate * (1.0 - sigmoid))).astype(BF16)
         up_grad[rows, :] = (back * silu).astype(BF16)
-    for first in range(0, FD, 128):
-        rows = slice(first, first + 128)
-        update[rows, :FD] = dot(gate_grad[:, rows], key_ref[...], 0, 0)
-        update[rows, FD : 2 * FD] = dot(up_grad[:, rows], key_ref[...], 0, 0)
-        update[rows, 2 * FD :] = dot(scaled[:, rows], hidden[...], 0, 0)
-    if split:
-        index = lax.axis_index("ctx")
-        for out, mask in zip(outs, (3, 1, 2, 0)):
-            rows = out.shape[0]
-            out[...] = update[pl.ds(pl.multiple_of((index ^ mask) * rows, 32), rows), :].astype(out.dtype)
-    else:
-        outs[0][...] = update[...]
+    sent = []
+    for third, (left, right) in enumerate(((gate_grad, key_ref), (up_grad, key_ref), (scaled, hidden))):
+        cols = slice(third * FD, (third + 1) * FD)
+        for first in range(0, FD, 128):
+            rows = slice(first, first + 128)
+            update[rows, cols] = dot(left[:, rows], right[...], 0, 0)
+        if split:
+            far, near, across, own = outs
+            rows = far.shape[0]
+            for number, (out, mask) in enumerate(((far, 3), (near, 1), (across, 2))):
+                place = slice(number * rows, (number + 1) * rows)
+                stage[place, cols] = update[rows_of(mask, rows), cols].astype(BF16)
+                sent.append(copies.start(stage.at[place, cols], out.at[:, cols]))
+            sent.append(copies.start(update.at[rows_of(0, rows), cols], own.at[:, cols]))
+        else:
+            sent.append(copies.start(update.at[:, cols], outs[0].at[:, cols]))
+    wait(sent)
 
 
 def head_grads(fw_key, fw_value, fw_rate, gathered, head, split):
     tokens = fw_key.shape[0]
     parts = [part for part, _ in gathered]
     masks = [mask for _, mask in gathered]
-    column = pl.BlockSpec((tokens, FD), lambda i: (0, head))
     if split:
         rows = parts[0].shape[0]
-        out_shape = tuple(jax.ShapeDtypeStruct((rows, SPAN), kind) for kind in (BF16, BF16, F32, F32))
+        out_shape = tuple(jax.ShapeDtypeStruct((rows, SPAN), kind) for kind in (BF16, BF16, BF16, F32))
     else:
         out_shape = (jax.ShapeDtypeStruct((FD, SPAN), F32),)
-    out_specs = tuple(pl.BlockSpec(out.shape, lambda i: (0, 0)) for out in out_shape)
+    by_token = pltpu.VMEM((tokens, FD), BF16)
     return pl.pallas_call(
         functools.partial(grads_kernel, masks, split, head),
-        grid=(1,),
-        in_specs=[column, column, pl.BlockSpec(fw_rate.shape, lambda i: (0, 0))] + [ANY] * len(parts),
-        out_specs=out_specs,
+        in_specs=[pl.BlockSpec(memory_space=pltpu.VMEM)] + [ANY] * (2 + len(parts)),
+        out_specs=tuple(ANY for _ in out_shape),
         out_shape=out_shape,
         scratch_shapes=[
+            by_token,
+            by_token,
             pltpu.VMEM((FD, SPAN), BF16),
-            pltpu.VMEM((tokens, FD), BF16),
-            pltpu.VMEM((tokens, FD), BF16),
-            pltpu.VMEM((tokens, FD), BF16),
-            pltpu.VMEM((tokens, FD), BF16),
+            by_token,
+            by_token,
+            by_token,
+            by_token,
             pltpu.VMEM((FD, SPAN), F32),
-            pltpu.SemaphoreType.DMA((len(parts),)),
+            pltpu.VMEM((3 * parts[0].shape[0] if split else 16, SPAN), BF16),
+            pltpu.SemaphoreType.DMA((2 + 3 * len(parts) + 3 * len(out_shape),)),
         ],
+        compiler_params=PARAMS,
         cost_estimate=cost(12 * tokens * FD * FD, 8e6, tokens * FD),
         name="head_grads",
-    )(fw_key, fw_value, fw_rate, *parts)
+    )(fw_rate.T, fw_key, fw_value, *parts)
+
+
+def round_kernel(w_ref, low_ref):
+    low_ref[...] = w_ref[...].astype(BF16)
+
+
+def row_block(rows, most):
+    return max((size for size in range(16, most + 1, 16) if rows % size == 0), default=rows)
+
+
+def round_head(fast_weights, head):
+    rows = fast_weights.shape[0]
+    block = row_block(rows, 80)
+    return pl.pallas_call(
+        round_kernel,
+        grid=(rows // block,),
+        in_specs=[pl.BlockSpec((block, SPAN), lambda i: (i, head))],
+        out_specs=pl.BlockSpec((block, SPAN), lambda i: (i, 0)),
+        out_shape=jax.ShapeDtypeStruct((rows, SPAN), BF16),
+        compiler_params=PARAMS,
+        cost_estimate=cost(rows * SPAN, 6 * rows * SPAN),
+        name="round_head",
+    )(fast_weights)
+
+
+def pack_kernel(moved, q_ref, k_ref, v_ref, queries_ref, pairs_ref):
+    width = moved * HD
+    queries_ref[...] = q_ref[:, width:]
+    pairs_ref[:, :width] = k_ref[...]
+    pairs_ref[:, width:] = v_ref[...]
+
+
+def pack_travellers(attn_query, attn_key, attn_value, moved):
+    rows, width = attn_query.shape
+    block = row_block(rows, 256)
+
+    def spec(cols):
+        return pl.BlockSpec((block, cols), lambda i: (i, 0))
+
+    widths = (width - moved * HD, 2 * moved * HD)
+    return pl.pallas_call(
+        functools.partial(pack_kernel, moved),
+        grid=(rows // block,),
+        in_specs=[spec(width), spec(moved * HD), spec(moved * HD)],
+        out_specs=[spec(cols) for cols in widths],
+        out_shape=[jax.ShapeDtypeStruct((rows, cols), BF16) for cols in widths],
+        compiler_params=PARAMS,
+        cost_estimate=cost(0, 8 * rows * width),
+        name="pack_travellers",
+    )(attn_query, attn_key, attn_value)
 
 
 def move_kernel(sums, w_ref, m_ref, *refs):
@@ -294,7 +380,7 @@
 
 def move_weights(fast_weights, momentum, addends, head, previous):
     rows = fast_weights.shape[0]
-    block = 32 if rows % 32 == 0 else rows
+    block = row_block(rows, 80)
     wide = pl.BlockSpec((block, SPAN), lambda i: (i, head))
     own = pl.BlockSpec((block, SPAN), lambda i: (i, 0))
     in_specs = [wide, wide] + [own] * len(addends)
@@ -312,49 +398,63 @@
         out_specs=(wide, wide, own),
         out_shape=(full, full, jax.ShapeDtypeStruct((rows, SPAN), BF16)),
         input_output_aliases=aliases,
+        compiler_params=PARAMS,
         cost_estimate=cost(20 * rows * SPAN, 26 * rows * SPAN),
         name="move_weights",
     )(*args)
 
 
-def query_kernel(masks, q_ref, *refs):
+def query_kernel(masks, q_hbm, head, *refs):
     count = len(masks)
     parts = refs[:count]
-    out_ref, low, sems = refs[-3:]
-    for copy in fetch_rows(parts, masks, low, sems):
-        copy.wait()
+    out_hbm, q_ref, low, stage, sems = refs[-5:]
+    mine = slice(head * FD, (head + 1) * FD)
+    copies = Copies(sems)
+    query_copy = copies.start(q_hbm.at[:, mine], q_ref)
+    loads = [copies.part(parts, masks, low, third) for third in range(3)]
     tokens = q_ref.shape[0]
     block = min(256, tokens)
-
+    sent = []
     for first in range(0, tokens, block):
         rows = slice(first, first + block)
+        if first == 0:
+            wait([query_copy] + loads[0])
         queries = q_ref[rows, :]
         gate = dot(queries, low[:, :FD], 1, 1) * INV_ROOT
+        if first == 0:
+            wait(loads[1])
         up = dot(queries, low[:, FD : 2 * FD], 1, 1) * INV_ROOT
         hidden = (gate * (1.0 / (1.0 + jnp.exp(-gate))) * up).astype(BF16)
-        out_ref[rows, :] = (dot(hidden, low[:, 2 * FD :], 1, 1) * INV_ROOT).astype(BF16)
+        if first == 0:
+            wait(loads[2])
+        stage[rows, :] = (dot(hidden, low[:, 2 * FD :], 1, 1) * INV_ROOT).astype(BF16)
+        sent.append(copies.start(stage.at[rows, :], out_hbm.at[rows, mine]))
+    wait(sent)
 
 
 def head_query(fw_query, gathered, head, previous):
     tokens = fw_query.shape[0]
     parts = [part for part, _ in gathered]
     masks = [mask for _, mask in gathered]
-    column = pl.BlockSpec((tokens, FD), lambda i: (0, head))
-    in_specs = [column] + [ANY] * len(parts)
     args = [fw_query] + parts
     aliases = {}
     if previous is not None:
         aliases = {len(args): 0}
-        in_specs.append(ANY)
         args.append(previous)
+    by_token = pltpu.VMEM((tokens, FD), BF16)
     return pl.pallas_call(
-        functools.partial(query_kernel, masks),
-        grid=(1,),
-        in_specs=in_specs,
-        out_specs=column,
+        lambda q_hbm, *refs: query_kernel(masks, q_hbm, head, *refs),
+        in_specs=[ANY] * len(args),
+        out_specs=ANY,
         out_shape=jax.ShapeDtypeStruct(fw_query.shape, BF16),
-        scratch_shapes=[pltpu.VMEM((FD, SPAN), BF16), pltpu.SemaphoreType.DMA((len(parts),))],
+        scratch_shapes=[
+            by_token,
+            pltpu.VMEM((FD, SPAN), BF16),
+            by_token,
+            pltpu.SemaphoreType.DMA((1 + 3 * len(parts) + pl.cdiv(tokens, 256),)),
+        ],
         input_output_aliases=aliases,
+        compiler_params=PARAMS,
         cost_estimate=cost(6 * tokens * FD * FD, 4e6, tokens * FD),
         name="head_query",
     )(*args)
@@ -375,33 +475,22 @@
     return lax.optimization_barrier((array,) + others)[0]
 
 
-class Lane:
-    def __init__(self):
-        self.ended = None
-
-    def cross(self, array):
-        if self.ended is not None:
-            array = after(array, self.ended)
-        self.ended = swapped(array, 2)
-        return self.ended
-
-
-def gather_rows(lane, shard, paired):
+def gather_rows(shard, paired):
     if not paired:
         return [(lax.all_gather(shard, "ctx", axis=0, tiled=True), None)]
-    across = lane.cross(shard)
+    across = swapped(shard, 2)
     beside = swapped(shard, 1)
     return [(shard, 0), (beside, 1), (across, 2), (swapped(across, 1), 3)]
 
 
-def sum_rows(lane, pieces, paired):
+def sum_rows(pieces, paired):
     if not paired:
         return [lax.psum_scatter(pieces[0], "ctx", scatter_dimension=0, tiled=True)]
     far, near, across, own = pieces
     far = swapped(far, 1)
     near = swapped(near, 1)
-    total = (across + far.astype(F32)).astype(BF16)
-    return [own, near, lane.cross(total)]
+    total = (across.astype(F32) + far.astype(F32)).astype(BF16)
+    return [own, near, swapped(total, 2)]
 
 
 def per_device(
@@ -410,24 +499,22 @@
     devices = lax.axis_size("ctx")
     head_local = fw_rate.shape[1]
     paired = devices == 4
-    lane = Lane()
     heads = range(head_local)
     all_heads = attn_query.shape[1] // HD
     moved = 2 * all_heads // 5
     stay = all_heads - moved
 
-    low = fast_weights[:, :SPAN].astype(BF16)
-    gathered = [gather_rows(lane, low, paired)]
-    started = gathered[0][2 if paired else 0][0]
-    source = after(fast_weights, low)
-    for head in heads[1:]:
-        low = source[:, head * SPAN : (head + 1) * SPAN].astype(BF16)
-        gathered.append(gather_rows(lane, low, paired))
-
+    gathered = []
+    source = fast_weights
+    for head in heads:
+        low = round_head(source, head)
+        gathered.append(gather_rows(low if head == 0 else after(low, started), paired))
+        if head == 0:
+            started = gathered[0][2 if paired else 0][0]
+            source = after(fast_weights, low)
+    queries, pairs = pack_travellers(after(attn_query, source[:1, :1]), attn_key, attn_value, moved)
     pair_key = swapped(attn_key, 1)
     pair_value = swapped(attn_value, 1)
-    queries = attn_query[:, moved * HD :]
-    pairs = jnp.concatenate([attn_key[:, : moved * HD], attn_value[:, : moved * HD]], axis=1)
     far_query = shifted(after(queries, started), -2)
     far_pairs = shifted(after(pairs, started), 2)
     far_pairs_other = swapped(far_pairs, 1)
@@ -440,7 +527,7 @@
     for head in heads:
         pieces = head_grads(after(fw_key, before), fw_value, fw_rate, gathered[head], head, paired)
         before = pieces[-1]
-        sums.append(sum_rows(lane, pieces, paired))
+        sums.append(sum_rows(pieces, paired))
     far_o, far_st, own_o, own_st = attention_call(
         group_kernel,
         stay,
@@ -449,24 +536,27 @@
         ["t", "s", "t", "s"],
         1.6,
     )
-    far_o = shifted(far_o, 2)
-    far_st = shifted(far_st, 2)
 
     new = None
     new_gathered = []
     for head in heads:
         new_weights, new_momentum, low = move_weights(fast_weights, momentum, sums[head], head, new)
         new = (new_weights, new_momentum)
-        new_gathered.append(gather_rows(lane, low, paired))
-    attn_out = attention_call(
-        whole_kernel,
-        moved,
-        [attn_query, attn_key, attn_value, pair_key, pair_value, far_pairs, far_pairs, far_pairs_other, far_pairs_other],
-        [0, 0, 0, 0, 0, 0, moved, 0, moved],
-        [0],
-        2.2,
-        (attn_query.shape, None),
-    )[0]
+        new_gathered.append(gather_rows(low, paired))
+        if head == 0:
+            far_o = shifted(after(far_o, low), 2)
+            far_st = shifted(after(far_st, low), 2)
+            attn_out = attention_call(
+                whole_kernel,
+                moved,
+                [after(attn_query, low), attn_key, attn_value, pair_key, pair_value, far_pairs, far_pairs, far_pairs_other, far_pairs_other],
+                [0, 0, 0, 0, 0, 0, moved, 0, moved],
+                [0],
+                2.2,
+                (attn_query.shape, None),
+                2,
+            )[0]
+            momentum = after(momentum, attn_out)
     fw_out = None
     for head in heads:
         fw_out = head_query(fw_query, new_gathered[head], head, fw_out)

time: 196 us -> 165 us (0.84)
  waiting for transfers between devices: 87.9 us -> 63.6 us
  local copies, waits for them, and re-layouts: 9.88 us -> 0.83 us
  starting transfers between devices: 25.3 us -> 29.3 us
    ppermute x21, waiting for transfers between devices: 57.4 us -> 34.5 us  [swapped(): return lax.ppermute(array, 'ctx', [(i, i ^ mask) for i in range(devices)])]
    ppermute x21, starting transfers between devices: 17.1 us -> 22.3 us  [swapped(): return lax.ppermute(array, 'ctx', [(i, i ^ mask) for i in range(devices)])]
    slice x7 -> x0, local copies, waits for them, and re-layouts: 4.78 us -> none  [the longest x1 2.18 us: per_device(): low = source[:, head * SPAN:(head + 1) * SPAN].astype(BF16)]
    unnamed x37 -> x6, local copies, waits for them, and re-layouts: 5.1 us -> 0.83 us
    pallas_call x2, Pallas kernels: 11.4 us -> 7.43 us  [move_weights(): pl.pallas_call(functools.partial(move_kernel, len(addends)), grid=(rows /...]
    pallas_call x4 -> x7, Pallas kernels: 29.4 us -> 32 us  [the longest x2 15.8 us: head_grads(): pl.pallas_call(functools.partial(grads_kernel, masks, split, head), in_sp...]
  transfers between devices with their start and end apart: 25 -> 25, of which waited for: 7 -> 7; matrix products, arithmetic and copies ran while one was open for 3% -> 1% of each run, Pallas kernels for 32% -> 37%
where the time goes in v3:
time: 165 us; the launch traced here: 164 us
  Pallas kernels  67.4 us (41%)
  waiting for transfers between devices  63.6 us (39%)
  starting transfers between devices  29.3 us (18%)
  other arithmetic  2.38 us (1%)
    ppermute x21, waiting for transfers between devices, swapped(): return lax.ppermute(array, 'ctx', [(i, i ^ mask) for i in range(devices)])  34.5 us
    ppermute x4, waiting for transfers between devices, shifted(): return lax.ppermute(array, 'ctx', pairs)  29.1 us
    pallas_call x4, Pallas kernels, attention_call(): pl.pallas_call(body, grid=(heads // per_step,), in_specs=in_specs, out_sp...  28 us
    ppermute x21, starting transfers between devices, swapped(): return lax.ppermute(array, 'ctx', [(i, i ^ mask) for i in range(devices)])  22.3 us
    pallas_call x2, Pallas kernels, head_grads(): pl.pallas_call(functools.partial(grads_kernel, masks, split, head), in_sp...  15.8 us
    pallas_call x2, Pallas kernels, head_query(): pl.pallas_call(lambda q_hbm, *refs: query_kernel(masks, q_hbm, head, *ref...  9.54 us
    pallas_call x2, Pallas kernels, move_weights(): pl.pallas_call(functools.partial(move_kernel, len(addends)), grid=(rows /...  7.43 us
    ppermute x4, starting transfers between devices, shifted(): return lax.ppermute(array, 'ctx', pairs)  6.97 us
  transfers between devices with their start and end apart: 25, of which 7 were waited for; matrix products, arithmetic and copies ran while one was open for 1% of the time, Pallas kernels for 37%

profile of v3, /device:TPU:7, one launch (start us, length us, event | category | flops | bytes accessed | tf_op | source)
XLA Modules:
  0.0 164.3 jit_solution(13979869430135258325)
XLA Ops:
  0.6 2.0 %round_head.2.refs_3_ = bf16[160,1920]{1,0:T(8,128)(2,1)} custom-call(f32[160,3840]{1,0:T(8,128)} %w_ref.6), custom_call_target="tpu_custom_call" | custom-call | flops 307200 | bytes 1843200 | tf_op jit(solution)/shard_map/round_head/pallas_call | solution.py:323
  2.7 0.3 collective-permute-start
  2.9 2.0 %round_head.3.refs_3_ = bf16[160,1920]{1,0:T(8,128)(2,1)} custom-call(f32[160,3840]{1,0:T(8,128)} %w_ref.6), custom_call_target="tpu_custom_call" | custom-call | flops 307200 | bytes 1843200 | tf_op jit(solution)/shard_map/round_head/pallas_call | solution.py:323
  4.9 12.8 %collective-permute-done.refs_5_ = bf16[160,1920]{1,0:T(8,128)(2,1)} collective-permute-done((bf16[160,1920]{1,0:T(8,128)(2,1)}, bf16[160,1920]{1,0:T(8,128)(2,1)}, u32[]{:S(2)}, u32[]{:S(2)}) %collective-permute-start) | collective-permute-done | bytes 614432 | tf_op jit(solution)/shard_map/ppermute | solution.py:465
  17.7 0.3 collective-permute-start.5
  18.0 1.8 %collective-permute-start.2 = (bf16[160,1920]{1,0:T(8,128)(2,1)}, bf16[160,1920]{1,0:T(8,128)(2,1)}, u32[]{:S(2)}, u32[]{:S(2)}) collective-permute-start(bf16[160,1920]{1,0:T(8,128)(2,1)} %round_head.2.refs_3_), channel_id=1, source_target_pairs={{0,8},{8,0},{16,24},{24,16},{1,9},{9,1},{17,25},{25,17},{2,10},{10... | collective-permute-start | bytes 1843208 | tf_op jit(solution)/shard_map/ppermute | solution.py:465
  19.8 0.0 collective-permute-start.3
  19.8 0.5 collective-permute-start.4
  20.3 11.6 %collective-permute-done.5.refs_5_ = bf16[160,1920]{1,0:T(8,128)(2,1)} collective-permute-done((bf16[160,1920]{1,0:T(8,128)(2,1)}, bf16[160,1920]{1,0:T(8,128)(2,1)}, u32[]{:S(2)}, u32[]{:S(2)}) %collective-permute-start.5) | collective-permute-done | bytes 614432 | tf_op jit(solution)/shard_map/ppermute | solution.py:465
  31.9 2.4 %collective-permute-start.6 = (bf16[160,1920]{1,0:T(8,128)(2,1)}, bf16[160,1920]{1,0:T(8,128)(2,1)}, u32[]{:S(2)}, u32[]{:S(2)}) collective-permute-start(bf16[160,1920]{1,0:T(8,128)(2,1)} %collective-permute-done.5.refs_5_), channel_id=1, source_target_pairs={{0,8},{8,0},{16,24},{24,16},{1,9},{9,1},{17,25},{25,17},{2,10},{10... | collective-permute-start | bytes 1843208 | tf_op jit(solution)/shard_map/ppermute | solution.py:465
  34.3 2.6 %pack_travellers.1 = (bf16[512,768]{1,0:T(8,128)(2,1)}, bf16[512,1024]{1,0:T(8,128)(2,1)}) custom-call(bf16[512,1280]{1,0:T(8,128)(2,1)} %q_ref.1, bf16[512,1280]{1,0:T(8,128)(2,1)} %k_ref.7, bf16[512,1280]{1,0:T(8,128)(2,1)} %v_ref.7), custom_call_target="tpu_custom_call" | custom-call | bytes 5242880 | tf_op jit(solution)/shard_map/pack_travellers/pallas_call | solution.py:350
  36.9 6.0 %shard_map.120 = (bf16[768,512]{1,0:T(8,128)(2,1)}, f32[24,512]{1,0:T(8,128)}) custom-call(bf16[512,768]{1,0:T(8,128)(2,1)} %get-tuple-element.38.q_ref, bf16[512,1280]{1,0:T(8,128)(2,1)} %k_ref.7, bf16[512,1280]{1,0:T(8,128)(2,1)} %v_ref.7), custom_call_target="tpu_custom_call" | custom-call | flops 483183808 | bytes 3932160 | tf_op jit(solution)/shard_map/pallas_call | solution.py:179
  42.8 0.0 collective-permute-done.2.refs_4_
  42.8 0.0 collective-permute-done.3.refs_6_
  42.9 7.9 %head_grads.2 = (bf16[160,1920]{1,0:T(8,128)(2,1)}, bf16[160,1920]{1,0:T(8,128)(2,1)}, bf16[160,1920]{1,0:T(8,128)(2,1)}, f32[160,1920]{1,0:T(8,128)}) custom-call(f32[2,512]{1,0:T(2,128)} %bitcast.1, bf16[512,1280]{1,0:T(8,128)(2,1)} %refs_1_.1, bf16[512,1280]{1,0:T(8,128)(2,1)} %refs_2_.3, bf16[160,1920]{1,0:T(8,128)(2,1)} %round_head.2.refs_3_, ...), custom_call_target="tpu_custom_call" | custom-call | flops 2516582400 | bytes 8000000 | tf_op jit(solution)/shard_map/head_grads/pallas_call | solution.py:289
  50.8 0.1 collective-permute-start.10
  50.9 1.3 collective-permute-start.14
  52.2 0.5 collective-permute-start.7
  52.7 0.0 collective-permute-done.4.refs_4_
  52.7 0.0 collective-permute-done.6.refs_6_
  52.7 7.9 %head_grads.3 = (bf16[160,1920]{1,0:T(8,128)(2,1)}, bf16[160,1920]{1,0:T(8,128)(2,1)}, bf16[160,1920]{1,0:T(8,128)(2,1)}, f32[160,1920]{1,0:T(8,128)}) custom-call(f32[2,512]{1,0:T(2,128)} %bitcast.2, bf16[512,1280]{1,0:T(8,128)(2,1)} %refs_1_.1, bf16[512,1280]{1,0:T(8,128)(2,1)} %refs_2_.3, bf16[160,1920]{1,0:T(8,128)(2,1)} %round_head.3.refs_3_, ...), custom_call_target="tpu_custom_call" | custom-call | flops 2516582400 | bytes 8000000 | tf_op jit(solution)/shard_map/head_grads/pallas_call | solution.py:289
  60.6 0.1 collective-permute-start.17
  60.7 0.5 collective-permute-start.8
  61.2 0.0 collective-permute-done.10
  61.2 0.1 collective-permute-start.9
  61.3 1.4 add_convert_fusion.1
  62.7 14.6 %collective-permute-done.14.fk_ref.fv_ref = bf16[512,1024]{1,0:T(8,128)(2,1)} collective-permute-done((bf16[512,1024]{1,0:T(8,128)(2,1)}, bf16[512,1024]{1,0:T(8,128)(2,1)}, u32[]{:S(2)}, u32[]{:S(2)}) %collective-permute-start.14) | collective-permute-done | bytes 1048608 | tf_op jit(solution)/shard_map/ppermute | solution.py:471
  77.3 0.0 collective-permute-start.11
  77.3 0.0 collective-permute-done.17
  77.3 1.3 collective-permute-start.15
  78.7 1.0 add_convert_fusion
  79.6 0.0 collective-permute-done.7.pk_ref
  79.6 0.0 collective-permute-start.16
  79.7 0.0 collective-permute-done.9.refs_1_
  79.7 1.8 %collective-permute-start.18 = (bf16[160,1920]{1,0:T(8,128)(2,1)}, bf16[160,1920]{1,0:T(8,128)(2,1)}, u32[]{:S(2)}, u32[]{:S(2)}) collective-permute-start(bf16[160,1920]{1,0:T(8,128)(2,1)} %add_convert_fusion), channel_id=1, source_target_pairs={{0,16},{8,24},{16,0},{24,8},{1,17},{9,25},{17,1},{25,9},{2,18},{10... | collective-permute-start | bytes 1843208 | tf_op jit(solution)/shard_map/ppermute | solution.py:465
  81.5 9.9 %collective-permute-done.11.refs_2_ = bf16[160,1920]{1,0:T(8,128)(2,1)S(1)} collective-permute-done((bf16[160,1920]{1,0:T(8,128)(2,1)S(1)}, bf16[160,1920]{1,0:T(8,128)(2,1)S(1)}, u32[]{:S(2)}, u32[]{:S(2)}) %collective-permute-start.11) | collective-permute-done | bytes 614432 | tf_op jit(solution)/shard_map/ppermute | solution.py:465
  91.4 0.8 copy-done.2
  92.2 3.1 %collective-permute-start.1 = (bf16[512,768]{1,0:T(8,128)(2,1)}, bf16[512,768]{1,0:T(8,128)(2,1)}, u32[]{:S(2)}, u32[]{:S(2)}) collective-permute-start(bf16[512,768]{1,0:T(8,128)(2,1)} %get-tuple-element.38.q_ref), channel_id=1, source_target_pairs={{16,0},{24,8},{17,1},{25,9},{18,2},{26,10},{19,3},{27,11},{20,4},{... | collective-permute-start | bytes 2359304 | tf_op jit(solution)/shard_map/ppermute | solution.py:471
  95.3 3.7 %move_weights.2 = (f32[160,3840]{1,0:T(8,128)}, f32[160,3840]{1,0:T(8,128)}, bf16[160,1920]{1,0:T(8,128)(2,1)}) custom-call(f32[160,3840]{1,0:T(8,128)} %w_ref.6, f32[160,3840]{1,0:T(8,128)} %m_ref.2, f32[160,1920]{1,0:T(8,128)} %get-tuple-element.41.refs_0_, bf16[160,1920]{1,0:T(8,128)(2,1)} %copy-done.1, bf16[160,1920]{1,0:T(8,128)(2,1)} %copy-done.2), custom_call_target="tpu_custom_call" | custom-call | flops 6144000 | bytes 7987200 | tf_op jit(solution)/shard_map/move_weights/pallas_call | solution.py:394
  99.0 0.0 collective-permute-done.8.pv_ref
  99.0 0.1 collective-permute-start.23
  99.1 0.0 collective-permute-done.15.fpk_ref.fpv_ref
  99.1 10.3 %shard_map.122.refs_4_ = bf16[512,1280]{1,0:T(8,128)(2,1)} custom-call(bf16[512,1280]{1,0:T(8,128)(2,1)} %q_ref.1, bf16[512,1280]{1,0:T(8,128)(2,1)} %k_ref.7, bf16[512,1280]{1,0:T(8,128)(2,1)} %v_ref.7, bf16[512,1280]{1,0:T(8,128)(2,1)} %collective-permute-done.7.pk_ref, bf16[512,1280]{1,0:T(8,128)(2,1)} %collective-permute-done.8.pv_ref, ...), custom_call_target="tpu_custom_call" | custom-call | flops 1181116032 | bytes 5242880 | tf_op jit(solution)/shard_map/pallas_call | solution.py:179
  109.4 0.0 collective-permute-done.16.refs_1_
  109.4 0.0 collective-permute-done.18.refs_2_
  109.5 3.7 %move_weights.3 = (f32[160,3840]{1,0:T(8,128)}, f32[160,3840]{1,0:T(8,128)}, bf16[160,1920]{1,0:T(8,128)(2,1)}) custom-call(f32[160,3840]{1,0:T(8,128)} %w_ref.6, f32[160,3840]{1,0:T(8,128)} %m_ref.2, f32[160,1920]{1,0:T(8,128)} %get-tuple-element.45.refs_0_, ...), custom_call_target="tpu_custom_call", output_to_operand_aliasing={{0}: (5, {}), {1}: (6, {})} | custom-call | flops 6144000 | bytes 7987200 | tf_op jit(solution)/shard_map/move_weights/pallas_call | solution.py:394
  113.2 1.4 collective-permute-start.20
  114.6 5.0 %collective-permute-done.1.far_ref = bf16[512,768]{1,0:T(8,128)(2,1)} collective-permute-done((bf16[512,768]{1,0:T(8,128)(2,1)}, bf16[512,768]{1,0:T(8,128)(2,1)}, u32[]{:S(2)}, u32[]{:S(2)}) %collective-permute-start.1) | collective-permute-done | bytes 786464 | tf_op jit(solution)/shard_map/ppermute | solution.py:471
  119.6 8.2 %shard_map.121 = (bf16[768,512]{1,0:T(8,128)(2,1)}, f32[24,512]{1,0:T(8,128)}, bf16[768,512]{1,0:T(8,128)(2,1)}, f32[24,512]{1,0:T(8,128)}) custom-call(bf16[512,768]{1,0:T(8,128)(2,1)} %get-tuple-element.38.q_ref, bf16[512,768]{1,0:T(8,128)(2,1)} %collective-permute-done.1.far_ref, bf16[512,1280]{1,0:T(8,128)(2,1)} %k_ref.7, bf16[512,1280]{1,0:T(8,128)(2,1)} %v_ref.7, ...), custom_call_target="tpu_custom_call" | custom-call | flops 1288490240 | bytes 9437184 | tf_op jit(solution)/shard_map/pallas_call | solution.py:179
  127.8 1.3 collective-permute-start.12
  129.1 3.5 %collective-permute-start.22 = (bf16[160,1920]{1,0:T(8,128)(2,1)}, bf16[160,1920]{1,0:T(8,128)(2,1)}, u32[]{:S(2)}, u32[]{:S(2)}) collective-permute-start(bf16[160,1920]{1,0:T(8,128)(2,1)} %get-tuple-element.54.refs_0_), channel_id=1, source_target_pairs={{0,8},{8,0},{16,24},{24,16},{1,9},{9,1},{17,25},{25,17},{2,10},{10... | collective-permute-start | bytes 1843208 | tf_op jit(solution)/shard_map/ppermute | solution.py:465
  132.6 0.1 collective-permute-done.23.refs_2_
  132.7 3.4 %collective-permute-start.24 = (bf16[160,1920]{1,0:T(8,128)(2,1)}, bf16[160,1920]{1,0:T(8,128)(2,1)}, u32[]{:S(2)}, u32[]{:S(2)}) collective-permute-start(bf16[160,1920]{1,0:T(8,128)(2,1)} %collective-permute-done.23.refs_2_), channel_id=1, source_target_pairs={{0,8},{8,0},{16,24},{24,16},{1,9},{9,1},{17,25},{25,17},{2,10},{10... | collective-permute-start | bytes 1843208 | tf_op jit(solution)/shard_map/ppermute | solution.py:465
  136.2 1.3 collective-permute-start.13
  137.5 9.5 %collective-permute-done.13.refs_3_ = f32[24,512]{1,0:T(8,128)} collective-permute-done((f32[24,512]{1,0:T(8,128)}, f32[24,512]{1,0:T(8,128)}, u32[]{:S(2)}, u32[]{:S(2)}) %collective-permute-start.13) | collective-permute-done | bytes 49184 | tf_op jit(solution)/shard_map/ppermute | solution.py:471
  147.0 4.2 %collective-permute-start.19 = (bf16[160,1920]{1,0:T(8,128)(2,1)}, bf16[160,1920]{1,0:T(8,128)(2,1)}, u32[]{:S(2)}, u32[]{:S(2)}) collective-permute-start(bf16[160,1920]{1,0:T(8,128)(2,1)} %get-tuple-element.67.refs_0_), channel_id=1, source_target_pairs={{0,8},{8,0},{16,24},{24,16},{1,9},{9,1},{17,25},{25,17},{2,10},{10... | collective-permute-start | bytes 1843208 | tf_op jit(solution)/shard_map/ppermute | solution.py:465
  151.2 0.0 collective-permute-done.20.refs_2_
  151.2 0.0 collective-permute-start.21
  151.2 0.0 collective-permute-done.12.refs_2_
  151.2 3.4 %shard_map.123 = bf16[512,1280]{1,0:T(8,128)(2,1)} custom-call(bf16[768,512]{1,0:T(8,128)(2,1)} %get-tuple-element.48.refs_0_, f32[24,512]{1,0:T(8,128)} %get-tuple-element.49.refs_1_, bf16[768,512]{1,0:T(8,128)(2,1)} %collective-permute-done.12.refs_2_, f32[24,512]{1,0:T(8,128)} %collective-permute-done.13.refs_3_, ...), custom_call_target="tpu_custom_call", output_to_operand_aliasing={{}: (4, {})} | custom-call | flops 8053063 | bytes 3932160 | tf_op jit(solution)/shard_map/pallas_call | solution.py:179
  154.6 4.8 %head_query.2.refs_4_ = bf16[512,1280]{1,0:T(8,128)(2,1)} custom-call(bf16[512,1280]{1,0:T(8,128)(2,1)} %q_hbm.3, bf16[160,1920]{1,0:T(8,128)(2,1)} %get-tuple-element.54.refs_0_, bf16[160,1920]{1,0:T(8,128)(2,1)} %collective-permute-done.22.refs_1_, bf16[160,1920]{1,0:T(8,128)(2,1)} %collective-permute-done.23.refs_2_, ...), custom_call_target="tpu_custom_call" | custom-call | flops 1258291200 | bytes 4000000 | tf_op jit(solution)/shard_map/head_query/pallas_call | solution.py:445
  159.4 0.0 collective-permute-done.19.refs_1_
  159.4 0.0 collective-permute-done.21.refs_3_
  159.4 4.8 %head_query.3 = bf16[512,1280]{1,0:T(8,128)(2,1)} custom-call(bf16[512,1280]{1,0:T(8,128)(2,1)} %q_hbm.3, bf16[160,1920]{1,0:T(8,128)(2,1)} %get-tuple-element.67.refs_0_, bf16[160,1920]{1,0:T(8,128)(2,1)} %collective-permute-done.19.refs_1_, bf16[160,1920]{1,0:T(8,128)(2,1)} %collective-permute-done.20.refs_2_, ...), custom_call_target="tpu_custom_call", output_to_operand_aliasing={{}: (5, {})} | custom-call | flops 1258291200 | bytes 4000000 | tf_op jit(solution)/shard_map/head_query/pallas_call | solution.py:445
  (7 shorter events, 0.0 us)
Async XLA Ops:
  2.7 15.1 %collective-permute-start = (bf16[160,1920]{1,0:T(8,128)(2,1)}, bf16[160,1920]{1,0:T(8,128)(2,1)}, u32[]{:S(2)}, u32[]{:S(2)}) collective-permute-start(bf16[160,1920]{1,0:T(8,128)(2,1)} %round_head.2.refs_3_), channel_id=1, source_target_pairs={{0,16},{8,24},{16,0},{24,8},{1,17},{9,25},{17,1},{25,9},{2,18},{10... | collective-permute-start | bytes 1843208 | tf_op jit(solution)/shard_map/ppermute | solution.py:465
  17.7 14.2 %collective-permute-start.5 = (bf16[160,1920]{1,0:T(8,128)(2,1)}, bf16[160,1920]{1,0:T(8,128)(2,1)}, u32[]{:S(2)}, u32[]{:S(2)}) collective-permute-start(bf16[160,1920]{1,0:T(8,128)(2,1)} %round_head.3.refs_3_), channel_id=1, source_target_pairs={{0,16},{8,24},{16,0},{24,8},{1,17},{9,25},{17,1},{25,9},{2,18},{10... | collective-permute-start | bytes 1843208 | tf_op jit(solution)/shard_map/ppermute | solution.py:465
  18.0 24.9 %collective-permute-start.2 = (bf16[160,1920]{1,0:T(8,128)(2,1)}, bf16[160,1920]{1,0:T(8,128)(2,1)}, u32[]{:S(2)}, u32[]{:S(2)}) collective-permute-start(bf16[160,1920]{1,0:T(8,128)(2,1)} %round_head.2.refs_3_), channel_id=1, source_target_pairs={{0,8},{8,0},{16,24},{24,16},{1,9},{9,1},{17,25},{25,17},{2,10},{10... | collective-permute-start | bytes 1843208 | tf_op jit(solution)/shard_map/ppermute | solution.py:465
  19.8 23.1 %collective-permute-start.3 = (bf16[160,1920]{1,0:T(8,128)(2,1)}, bf16[160,1920]{1,0:T(8,128)(2,1)}, u32[]{:S(2)}, u32[]{:S(2)}) collective-permute-start(bf16[160,1920]{1,0:T(8,128)(2,1)} %collective-permute-done.refs_5_), channel_id=1, source_target_pairs={{0,8},{8,0},{16,24},{24,16},{1,9},{9,1},{17,25},{25,17},{2,10},{10... | collective-permute-start | bytes 1843208 | tf_op jit(solution)/shard_map/ppermute | solution.py:465
  19.8 32.9 %collective-permute-start.4 = (bf16[160,1920]{1,0:T(8,128)(2,1)}, bf16[160,1920]{1,0:T(8,128)(2,1)}, u32[]{:S(2)}, u32[]{:S(2)}) collective-permute-start(bf16[160,1920]{1,0:T(8,128)(2,1)} %round_head.3.refs_3_), channel_id=1, source_target_pairs={{0,8},{8,0},{16,24},{24,16},{1,9},{9,1},{17,25},{25,17},{2,10},{10... | collective-permute-start | bytes 1843208 | tf_op jit(solution)/shard_map/ppermute | solution.py:465
  31.9 20.8 %collective-permute-start.6 = (bf16[160,1920]{1,0:T(8,128)(2,1)}, bf16[160,1920]{1,0:T(8,128)(2,1)}, u32[]{:S(2)}, u32[]{:S(2)}) collective-permute-start(bf16[160,1920]{1,0:T(8,128)(2,1)} %collective-permute-done.5.refs_5_), channel_id=1, source_target_pairs={{0,8},{8,0},{16,24},{24,16},{1,9},{9,1},{17,25},{25,17},{2,10},{10... | collective-permute-start | bytes 1843208 | tf_op jit(solution)/shard_map/ppermute | solution.py:465
  50.8 10.4 %collective-permute-start.10 = (bf16[160,1920]{1,0:T(8,128)(2,1)}, bf16[160,1920]{1,0:T(8,128)(2,1)}, u32[]{:S(2)}, u32[]{:S(2)}) collective-permute-start(bf16[160,1920]{1,0:T(8,128)(2,1)} %get-tuple-element.53), channel_id=1, source_target_pairs={{0,8},{8,0},{16,24},{24,16},{1,9},{9,1},{17,25},{25,17},{2,10},{10... | collective-permute-start | bytes 1843208 | tf_op jit(solution)/shard_map/ppermute | solution.py:465
  50.9 26.4 %collective-permute-start.14 = (bf16[512,1024]{1,0:T(8,128)(2,1)}, bf16[512,1024]{1,0:T(8,128)(2,1)}, u32[]{:S(2)}, u32[]{:S(2)}) collective-permute-start(bf16[512,1024]{1,0:T(8,128)(2,1)} %get-tuple-element.60), channel_id=1, source_target_pairs={{0,16},{8,24},{1,17},{9,25},{2,18},{10,26},{3,19},{11,27},{4,20},{... | collective-permute-start | bytes 3145736 | tf_op jit(solution)/shard_map/ppermute | solution.py:471
  52.2 27.5 %collective-permute-start.7 = (bf16[512,1280]{1,0:T(8,128)(2,1)}, bf16[512,1280]{1,0:T(8,128)(2,1)}, u32[]{:S(2)}, u32[]{:S(2)}) collective-permute-start(bf16[512,1280]{1,0:T(8,128)(2,1)} %k_ref.7), channel_id=1, source_target_pairs={{0,8},{8,0},{16,24},{24,16},{1,9},{9,1},{17,25},{25,17},{2,10},{10... | collective-permute-start | bytes 3932168 | tf_op jit(solution)/shard_map/ppermute | solution.py:465
  60.6 18.0 %copy-start = (bf16[160,1920]{1,0:T(8,128)(2,1)S(1)}, bf16[160,1920]{1,0:T(8,128)(2,1)}, u32[]{:S(2)}) copy-start(bf16[160,1920]{1,0:T(8,128)(2,1)} %get-tuple-element.63) | copy-start | bytes 1843204
  60.6 16.7 %collective-permute-start.17 = (bf16[160,1920]{1,0:T(8,128)(2,1)}, bf16[160,1920]{1,0:T(8,128)(2,1)S(1)}, u32[]{:S(2)}, u32[]{:S(2)}) collective-permute-start(bf16[160,1920]{1,0:T(8,128)(2,1)} %get-tuple-element.64), channel_id=1, source_target_pairs={{0,8},{8,0},{16,24},{24,16},{1,9},{9,1},{17,25},{25,17},{2,10},{10... | collective-permute-start | bytes 1843208 | tf_op jit(solution)/shard_map/ppermute | solution.py:465
  60.7 38.3 %collective-permute-start.8 = (bf16[512,1280]{1,0:T(8,128)(2,1)}, bf16[512,1280]{1,0:T(8,128)(2,1)}, u32[]{:S(2)}, u32[]{:S(2)}) collective-permute-start(bf16[512,1280]{1,0:T(8,128)(2,1)} %v_ref.7), channel_id=1, source_target_pairs={{0,8},{8,0},{16,24},{24,16},{1,9},{9,1},{17,25},{25,17},{2,10},{10... | collective-permute-start | bytes 3932168 | tf_op jit(solution)/shard_map/ppermute | solution.py:465
  61.2 18.4 %collective-permute-start.9 = (bf16[160,1920]{1,0:T(8,128)(2,1)}, bf16[160,1920]{1,0:T(8,128)(2,1)S(1)}, u32[]{:S(2)}, u32[]{:S(2)}) collective-permute-start(bf16[160,1920]{1,0:T(8,128)(2,1)} %get-tuple-element.51), channel_id=1, source_target_pairs={{0,8},{8,0},{16,24},{24,16},{1,9},{9,1},{17,25},{25,17},{2,10},{10... | collective-permute-start | bytes 1843208 | tf_op jit(solution)/shard_map/ppermute | solution.py:465
  77.3 14.1 %collective-permute-start.11 = (bf16[160,1920]{1,0:T(8,128)(2,1)S(1)}, bf16[160,1920]{1,0:T(8,128)(2,1)S(1)}, u32[]{:S(2)}, u32[]{:S(2)}) collective-permute-start(bf16[160,1920]{1,0:T(8,128)(2,1)S(1)} %add_convert_fusion.1), channel_id=1, source_target_pairs={{0,16},{8,24},{16,0},{24,8},{1,17},{9,25},{17,1},{25,9},{2,18},{10... | collective-permute-start | bytes 1843208 | tf_op jit(solution)/shard_map/ppermute | solution.py:465
  77.3 21.8 %collective-permute-start.15 = (bf16[512,1024]{1,0:T(8,128)(2,1)}, bf16[512,1024]{1,0:T(8,128)(2,1)}, u32[]{:S(2)}, u32[]{:S(2)}) collective-permute-start(bf16[512,1024]{1,0:T(8,128)(2,1)} %collective-permute-done.14.fk_ref.fv_ref), channel_id=1, source_target_pairs={{0,8},{8,0},{16,24},{24,16},{1,9},{9,1},{17,25},{25,17},{2,10},{10... | collective-permute-start | bytes 3145736 | tf_op jit(solution)/shard_map/ppermute | solution.py:465
  79.6 29.8 %collective-permute-start.16 = (bf16[160,1920]{1,0:T(8,128)(2,1)}, bf16[160,1920]{1,0:T(8,128)(2,1)}, u32[]{:S(2)}, u32[]{:S(2)}) collective-permute-start(bf16[160,1920]{1,0:T(8,128)(2,1)} %get-tuple-element.62), channel_id=1, source_target_pairs={{0,8},{8,0},{16,24},{24,16},{1,9},{9,1},{17,25},{25,17},{2,10},{10... | collective-permute-start | bytes 1843208 | tf_op jit(solution)/shard_map/ppermute | solution.py:465
  79.7 11.7 %copy-start.1 = (bf16[160,1920]{1,0:T(8,128)(2,1)}, bf16[160,1920]{1,0:T(8,128)(2,1)S(1)}, u32[]{:S(2)}) copy-start(bf16[160,1920]{1,0:T(8,128)(2,1)S(1)} %collective-permute-done.9.refs_1_) | copy-start | bytes 1843204
  79.7 29.8 %collective-permute-start.18 = (bf16[160,1920]{1,0:T(8,128)(2,1)}, bf16[160,1920]{1,0:T(8,128)(2,1)}, u32[]{:S(2)}, u32[]{:S(2)}) collective-permute-start(bf16[160,1920]{1,0:T(8,128)(2,1)} %add_convert_fusion), channel_id=1, source_target_pairs={{0,16},{8,24},{16,0},{24,8},{1,17},{9,25},{17,1},{25,9},{2,18},{10... | collective-permute-start | bytes 1843208 | tf_op jit(solution)/shard_map/ppermute | solution.py:465
  91.4 0.8 copy-start.2
  92.2 27.4 %collective-permute-start.1 = (bf16[512,768]{1,0:T(8,128)(2,1)}, bf16[512,768]{1,0:T(8,128)(2,1)}, u32[]{:S(2)}, u32[]{:S(2)}) collective-permute-start(bf16[512,768]{1,0:T(8,128)(2,1)} %get-tuple-element.38.q_ref), channel_id=1, source_target_pairs={{16,0},{24,8},{17,1},{25,9},{18,2},{26,10},{19,3},{27,11},{20,4},{... | collective-permute-start | bytes 2359304 | tf_op jit(solution)/shard_map/ppermute | solution.py:471
  99.0 33.7 %collective-permute-start.23 = (bf16[160,1920]{1,0:T(8,128)(2,1)}, bf16[160,1920]{1,0:T(8,128)(2,1)}, u32[]{:S(2)}, u32[]{:S(2)}) collective-permute-start(bf16[160,1920]{1,0:T(8,128)(2,1)} %get-tuple-element.54.refs_0_), channel_id=1, source_target_pairs={{0,16},{8,24},{16,0},{24,8},{1,17},{9,25},{17,1},{25,9},{2,18},{10... | collective-permute-start | bytes 1843208 | tf_op jit(solution)/shard_map/ppermute | solution.py:465
  113.2 38.0 %collective-permute-start.20 = (bf16[160,1920]{1,0:T(8,128)(2,1)}, bf16[160,1920]{1,0:T(8,128)(2,1)}, u32[]{:S(2)}, u32[]{:S(2)}) collective-permute-start(bf16[160,1920]{1,0:T(8,128)(2,1)} %get-tuple-element.67.refs_0_), channel_id=1, source_target_pairs={{0,16},{8,24},{16,0},{24,8},{1,17},{9,25},{17,1},{25,9},{2,18},{10... | collective-permute-start | bytes 1843208 | tf_op jit(solution)/shard_map/ppermute | solution.py:465
  127.8 23.4 %collective-permute-start.12 = (bf16[768,512]{1,0:T(8,128)(2,1)}, bf16[768,512]{1,0:T(8,128)(2,1)}, u32[]{:S(2)}, u32[]{:S(2)}) collective-permute-start(bf16[768,512]{1,0:T(8,128)(2,1)} %get-tuple-element.55), channel_id=1, source_target_pairs={{0,16},{8,24},{1,17},{9,25},{2,18},{10,26},{3,19},{11,27},{4,20},{... | collective-permute-start | bytes 2359304 | tf_op jit(solution)/shard_map/ppermute | solution.py:471
  129.1 25.5 %collective-permute-start.22 = (bf16[160,1920]{1,0:T(8,128)(2,1)}, bf16[160,1920]{1,0:T(8,128)(2,1)}, u32[]{:S(2)}, u32[]{:S(2)}) collective-permute-start(bf16[160,1920]{1,0:T(8,128)(2,1)} %get-tuple-element.54.refs_0_), channel_id=1, source_target_pairs={{0,8},{8,0},{16,24},{24,16},{1,9},{9,1},{17,25},{25,17},{2,10},{10... | collective-permute-start | bytes 1843208 | tf_op jit(solution)/shard_map/ppermute | solution.py:465
  132.7 21.9 %collective-permute-start.24 = (bf16[160,1920]{1,0:T(8,128)(2,1)}, bf16[160,1920]{1,0:T(8,128)(2,1)}, u32[]{:S(2)}, u32[]{:S(2)}) collective-permute-start(bf16[160,1920]{1,0:T(8,128)(2,1)} %collective-permute-done.23.refs_2_), channel_id=1, source_target_pairs={{0,8},{8,0},{16,24},{24,16},{1,9},{9,1},{17,25},{25,17},{2,10},{10... | collective-permute-start | bytes 1843208 | tf_op jit(solution)/shard_map/ppermute | solution.py:465
  136.2 10.8 %collective-permute-start.13 = (f32[24,512]{1,0:T(8,128)}, f32[24,512]{1,0:T(8,128)}, u32[]{:S(2)}, u32[]{:S(2)}) collective-permute-start(f32[24,512]{1,0:T(8,128)} %get-tuple-element.57), channel_id=1, source_target_pairs={{0,16},{8,24},{1,17},{9,25},{2,18},{10,26},{3,19},{11,27},{4,20},{... | collective-permute-start | bytes 147464 | tf_op jit(solution)/shard_map/ppermute | solution.py:471
  147.0 12.4 %collective-permute-start.19 = (bf16[160,1920]{1,0:T(8,128)(2,1)}, bf16[160,1920]{1,0:T(8,128)(2,1)}, u32[]{:S(2)}, u32[]{:S(2)}) collective-permute-start(bf16[160,1920]{1,0:T(8,128)(2,1)} %get-tuple-element.67.refs_0_), channel_id=1, source_target_pairs={{0,8},{8,0},{16,24},{24,16},{1,9},{9,1},{17,25},{25,17},{2,10},{10... | collective-permute-start | bytes 1843208 | tf_op jit(solution)/shard_map/ppermute | solution.py:465
  151.2 8.2 %collective-permute-start.21 = (bf16[160,1920]{1,0:T(8,128)(2,1)}, bf16[160,1920]{1,0:T(8,128)(2,1)}, u32[]{:S(2)}, u32[]{:S(2)}) collective-permute-start(bf16[160,1920]{1,0:T(8,128)(2,1)} %collective-permute-done.20.refs_2_), channel_id=1, source_target_pairs={{0,8},{8,0},{16,24},{24,16},{1,9},{9,1},{17,25},{25,17},{2,10},{10... | collective-permute-start | bytes 1843208 | tf_op jit(solution)/shard_map/ppermute | solution.py:465

commit v4 on v3

--- a/solution.py
+++ b/solution.py
@@ -143,31 +143,33 @@
 
 
 def attention_call(kernel, heads, arrays, firsts, outs, units, into=None, most=5):
-    rows = arrays[0].shape[0] if isinstance(firsts[0], int) else arrays[0].shape[1]
+    firsts, outs = [[f if isinstance(f, tuple) else ("c", f) for f in fs] for fs in (firsts, outs)]
+    rows = arrays[0].shape[firsts[0][0] != "c"]
     per_step = max(
         size
         for size in range(1, most + 1)
-        if heads % size == 0 and all(f % size == 0 for f in firsts + outs if isinstance(f, int))
+        if heads % size == 0 and all(f % size == 0 for _, f in firsts + outs)
     )
 
     stat_rows = 8 * pl.cdiv(2 * per_step, 8)
 
-    def spec(first):
-        if first == "t":
-            return pl.BlockSpec((per_step * HD, rows), lambda i: (i, 0))
-        if first == "s":
-            return pl.BlockSpec((stat_rows, rows), lambda i: (i, 0))
-        return pl.BlockSpec((rows, per_step * HD), lambda i: (0, i + first // per_step))
-
-    def shape(first):
-        if first == "t":
+    def spec(kind, first):
+        step = first // per_step
+        if kind == "t":
+            return pl.BlockSpec((per_step * HD, rows), lambda i: (i + step, 0))
+        if kind == "s":
+            return pl.BlockSpec((stat_rows, rows), lambda i: (i + step, 0))
+        return pl.BlockSpec((rows, per_step * HD), lambda i: (0, i + step))
+
+    def shape(kind):
+        if kind == "t":
             return jax.ShapeDtypeStruct((heads * HD, rows), BF16)
-        if first == "s":
+        if kind == "s":
             return jax.ShapeDtypeStruct((stat_rows * (heads // per_step), rows), F32)
         return jax.ShapeDtypeStruct(into[0], BF16)
 
     aliases = {}
-    in_specs = [spec(first) for first in firsts]
+    in_specs = [spec(*first) for first in firsts]
     body = functools.partial(kernel, per_step)
     if into is not None and into[1] is not None:
         aliases = {len(arrays): 0}
@@ -180,8 +182,8 @@
         body,
         grid=(heads // per_step,),
         in_specs=in_specs,
-        out_specs=[spec(first) for first in outs],
-        out_shape=[shape(first) for first in outs],
+        out_specs=[spec(*first) for first in outs],
+        out_shape=[shape(kind) for kind, _ in outs],
         input_output_aliases=aliases,
         compiler_params=PARAMS,
         cost_estimate=cost(
@@ -332,25 +334,26 @@
     )(fast_weights)
 
 
-def pack_kernel(moved, q_ref, k_ref, v_ref, queries_ref, pairs_ref):
-    width = moved * HD
-    queries_ref[...] = q_ref[:, width:]
+def pack_kernel(q_ref, k_ref, v_ref, queries_ref, pairs_ref):
+    width = k_ref.shape[1]
+    queries_ref[...] = q_ref[...]
     pairs_ref[:, :width] = k_ref[...]
     pairs_ref[:, width:] = v_ref[...]
 
 
-def pack_travellers(attn_query, attn_key, attn_value, moved):
+def pack_travellers(attn_query, attn_key, attn_value, stay):
     rows, width = attn_query.shape
     block = row_block(rows, 256)
-
-    def spec(cols):
-        return pl.BlockSpec((block, cols), lambda i: (i, 0))
-
-    widths = (width - moved * HD, 2 * moved * HD)
+    left, right = stay * HD, width - stay * HD
+
+    def spec(cols, first=0):
+        return pl.BlockSpec((block, cols), lambda i: (i, first // cols))
+
+    widths = (left, 2 * right)
     return pl.pallas_call(
-        functools.partial(pack_kernel, moved),
+        pack_kernel,
         grid=(rows // block,),
-        in_specs=[spec(width), spec(moved * HD), spec(moved * HD)],
+        in_specs=[spec(left), spec(right, left), spec(right, left)],
         out_specs=[spec(cols) for cols in widths],
         out_shape=[jax.ShapeDtypeStruct((rows, cols), BF16) for cols in widths],
         compiler_params=PARAMS,
@@ -485,12 +488,12 @@
 
 def sum_rows(pieces, paired):
     if not paired:
-        return [lax.psum_scatter(pieces[0], "ctx", scatter_dimension=0, tiled=True)]
+        return [lax.psum_scatter(pieces[0], "ctx", scatter_dimension=0, tiled=True)], pieces[0]
     far, near, across, own = pieces
     far = swapped(far, 1)
     near = swapped(near, 1)
     total = (across.astype(F32) + far.astype(F32)).astype(BF16)
-    return [own, near, swapped(total, 2)]
+    return [own, near, swapped(total, 2)], total
 
 
 def per_device(
@@ -501,74 +504,118 @@
     paired = devices == 4
     heads = range(head_local)
     all_heads = attn_query.shape[1] // HD
-    moved = 2 * all_heads // 5
+    moved = max(1, all_heads // 5)
+    while all_heads % moved:
+        moved -= 1
     stay = all_heads - moved
-
-    gathered = []
-    source = fast_weights
-    for head in heads:
-        low = round_head(source, head)
-        gathered.append(gather_rows(low if head == 0 else after(low, started), paired))
-        if head == 0:
-            started = gathered[0][2 if paired else 0][0]
-            source = after(fast_weights, low)
-    queries, pairs = pack_travellers(after(attn_query, source[:1, :1]), attn_key, attn_value, moved)
+    half = stay // 2 if stay % 2 == 0 else stay
+    halves = range(0, stay, half)
+
+    low = round_head(fast_weights, 0)
+    gathered = [gather_rows(low, paired)]
+    started = gathered[0][2 if paired else 0][0]
+    own = attention_call(
+        own_kernel,
+        stay,
+        [after(attn_query, low), attn_key, attn_value],
+        [0, 0, 0],
+        [("t", 0), ("s", 0)],
+        0.6,
+        most=half,
+    )
+    before = own[1]
+    for head in heads[1:]:
+        low = round_head(after(fast_weights, before), head)
+        before = low
+        gathered.append(gather_rows(after(low, started), paired))
+    queries, pairs = pack_travellers(after(attn_query, before), attn_key, attn_value, stay)
+    far_query = shifted(queries, -2)
+    far_pairs = shifted(pairs, 2)
+    far_pairs_other = swapped(far_pairs, 1)
     pair_key = swapped(attn_key, 1)
     pair_value = swapped(attn_value, 1)
-    far_query = shifted(after(queries, started), -2)
-    far_pairs = shifted(after(pairs, started), 2)
-    far_pairs_other = swapped(far_pairs, 1)
-
-    own = attention_call(
-        own_kernel, stay, [queries, attn_key, attn_value], [0, moved, moved], ["t", "s"], 0.6
-    )
-    before = own[1]
+
+    before = queries
     sums = []
+    totals = []
     for head in heads:
         pieces = head_grads(after(fw_key, before), fw_value, fw_rate, gathered[head], head, paired)
         before = pieces[-1]
-        sums.append(sum_rows(pieces, paired))
-    far_o, far_st, own_o, own_st = attention_call(
-        group_kernel,
-        stay,
-        [queries, after(far_query, before), attn_key, attn_value, pair_key, pair_value, *own],
-        [0, 0, moved, moved, moved, moved, "t", "s"],
-        ["t", "s", "t", "s"],
-        1.6,
-    )
-
-    new = None
+        addends, total = sum_rows(pieces, paired)
+        sums.append(addends)
+        totals.append(total)
+    found = []
+    for first in halves:
+        found.append(
+            attention_call(
+                group_kernel,
+                half,
+                [
+                    attn_query,
+                    after(far_query, before),
+                    attn_key,
+                    attn_value,
+                    pair_key,
+                    pair_value,
+                    *own,
+                ],
+                [first] * 6 + [("t", first), ("s", first)],
+                [("t", 0), ("s", 0), ("t", 0), ("s", 0)],
+                1.6,
+                most=half,
+            )
+        )
+        before = after(found[-1][1], totals[-1])
+
+    fw_new = None
     new_gathered = []
     for head in heads:
-        new_weights, new_momentum, low = move_weights(fast_weights, momentum, sums[head], head, new)
-        new = (new_weights, new_momentum)
+        new_weights, new_momentum, low = move_weights(
+            fast_weights, momentum, sums[head], head, fw_new
+        )
+        fw_new = (new_weights, new_momentum)
         new_gathered.append(gather_rows(low, paired))
         if head == 0:
-            far_o = shifted(after(far_o, low), 2)
-            far_st = shifted(after(far_st, low), 2)
             attn_out = attention_call(
                 whole_kernel,
                 moved,
-                [after(attn_query, low), attn_key, attn_value, pair_key, pair_value, far_pairs, far_pairs, far_pairs_other, far_pairs_other],
-                [0, 0, 0, 0, 0, 0, moved, 0, moved],
-                [0],
+                [
+                    after(attn_query, low),
+                    attn_key,
+                    attn_value,
+                    pair_key,
+                    pair_value,
+                    far_pairs,
+                    far_pairs,
+                    far_pairs_other,
+                    far_pairs_other,
+                ],
+                [stay] * 5 + [0, moved, 0, moved],
+                [stay],
                 2.2,
                 (attn_query.shape, None),
-                2,
+                most=2,
             )[0]
             momentum = after(momentum, attn_out)
+    returned = []
+    for number, (far_o, far_st, own_o, own_st) in enumerate(found):
+        if number > 0:
+            far_o, far_st = after(far_o, low), after(far_st, low)
+        returned.append((own_o, own_st, shifted(far_o, 2), shifted(far_st, 2)))
     fw_out = None
     for head in heads:
         fw_out = head_query(fw_query, new_gathered[head], head, fw_out)
-    attn_out = attention_call(
-        merge_kernel,
-        stay,
-        [own_o, own_st, far_o, far_st],
-        ["t", "s", "t", "s"],
-        [moved],
-        0.01,
-        (attn_query.shape, attn_out),
-    )[0]
+    for number, states in enumerate(returned):
+        attn_out = attention_call(
+            merge_kernel,
+            half,
+            states,
+            [("t", 0), ("s", 0), ("t", 0), ("s", 0)],
+            [number * half],
+            0.01,
+            (attn_query.shape, attn_out),
+            most=half,
+        )[0]
     return (attn_out, fw_out, new_weights, new_momentum)
 
 

time: 165 us -> 174 us (1.055)
  waiting for transfers between devices: 63.6 us -> 69.3 us
  Pallas kernels: 67.4 us -> 70 us
    ppermute x4 -> x6, waiting for transfers between devices: 29.1 us -> 38.3 us  [shifted(): return lax.ppermute(array, 'ctx', pairs)]
    ppermute x4 -> x6, starting transfers between devices: 6.97 us -> 11.2 us  [shifted(): return lax.ppermute(array, 'ctx', pairs)]
    ppermute x21, waiting for transfers between devices: 34.5 us -> 31 us  [swapped(): return lax.ppermute(array, 'ctx', [(i, i ^ mask) for i in range(devices)])]
    ppermute x21, starting transfers between devices: 22.3 us -> 19 us  [swapped(): return lax.ppermute(array, 'ctx', [(i, i ^ mask) for i in range(devices)])]
    pallas_call x4 -> x6, Pallas kernels: 28 us -> 30.8 us  [attention_call(): pl.pallas_call(body, grid=(heads // per_step,), in_specs=in_specs, out_sp...]
  transfers between devices with their start and end apart: 25 -> 27, of which waited for: 7 -> 8; matrix products, arithmetic and copies ran while one was open for 1% -> 1% of each run, Pallas kernels for 37% -> 36%
where the time goes in v4:
time: 174 us
  Pallas kernels  70 us (40%)
  waiting for transfers between devices  69.3 us (40%)
  starting transfers between devices  30.1 us (17%)
  other arithmetic  2.37 us (1%)
    ppermute x6, waiting for transfers between devices, shifted(): return lax.ppermute(array, 'ctx', pairs)  38.3 us
    ppermute x21, waiting for transfers between devices, swapped(): return lax.ppermute(array, 'ctx', [(i, i ^ mask) for i in range(devices)])  31 us
    pallas_call x6, Pallas kernels, attention_call(): pl.pallas_call(body, grid=(heads // per_step,), in_specs=in_specs, out_sp...  30.8 us
    ppermute x21, starting transfers between devices, swapped(): return lax.ppermute(array, 'ctx', [(i, i ^ mask) for i in range(devices)])  19 us
    pallas_call x2, Pallas kernels, head_grads(): pl.pallas_call(functools.partial(grads_kernel, masks, split, head), in_sp...  15.8 us
    ppermute x6, starting transfers between devices, shifted(): return lax.ppermute(array, 'ctx', pairs)  11.2 us
    pallas_call x2, Pallas kernels, head_query(): pl.pallas_call(lambda q_hbm, *refs: query_kernel(masks, q_hbm, head, *ref...  9.54 us
    pallas_call x2, Pallas kernels, move_weights(): pl.pallas_call(functools.partial(move_kernel, len(addends)), grid=(rows /...  7.4 us
  transfers between devices with their start and end apart: 27, of which 8 were waited for; matrix products, arithmetic and copies ran while one was open for 1% of the time, Pallas kernels for 36%

profile of v4, /device:TPU:7, one launch (start us, length us, event | category | flops | bytes accessed | tf_op | source)
XLA Modules:
  0.0 173.7 jit_solution(8383116802066329269)
XLA Ops:
  0.6 2.0 %round_head.2.refs_3_ = bf16[160,1920]{1,0:T(8,128)(2,1)} custom-call(f32[160,3840]{1,0:T(8,128)} %w_ref.6), custom_call_target="tpu_custom_call" | custom-call | flops 307200 | bytes 1843200 | tf_op jit(solution)/shard_map/round_head/pallas_call | solution.py:325
  2.7 0.3 collective-permute-start.4
  2.9 6.6 %shard_map.120 = (bf16[1024,512]{1,0:T(8,128)(2,1)}, f32[16,512]{1,0:T(8,128)}) custom-call(bf16[512,1280]{1,0:T(8,128)(2,1)} %q_ref.6, bf16[512,1280]{1,0:T(8,128)(2,1)} %k_ref.9, bf16[512,1280]{1,0:T(8,128)(2,1)} %v_ref.9), custom_call_target="tpu_custom_call" | custom-call | flops 644245120 | bytes 5242880 | tf_op jit(solution)/shard_map/pallas_call | solution.py:181
  9.5 2.0 %round_head.3.refs_3_ = bf16[160,1920]{1,0:T(8,128)(2,1)} custom-call(f32[160,3840]{1,0:T(8,128)} %w_ref.6), custom_call_target="tpu_custom_call" | custom-call | flops 307200 | bytes 1843200 | tf_op jit(solution)/shard_map/round_head/pallas_call | solution.py:325
  11.5 6.2 %collective-permute-done.4.refs_5_ = bf16[160,1920]{1,0:T(8,128)(2,1)} collective-permute-done((bf16[160,1920]{1,0:T(8,128)(2,1)}, bf16[160,1920]{1,0:T(8,128)(2,1)}, u32[]{:S(2)}, u32[]{:S(2)}) %collective-permute-start.4) | collective-permute-done | bytes 614432 | tf_op jit(solution)/shard_map/ppermute | solution.py:468
  17.7 0.3 collective-permute-start.12
  18.0 1.8 %collective-permute-start.3 = (bf16[160,1920]{1,0:T(8,128)(2,1)}, bf16[160,1920]{1,0:T(8,128)(2,1)}, u32[]{:S(2)}, u32[]{:S(2)}) collective-permute-start(bf16[160,1920]{1,0:T(8,128)(2,1)} %round_head.2.refs_3_), channel_id=1, source_target_pairs={{0,8},{8,0},{16,24},{24,16},{1,9},{9,1},{17,25},{25,17},{2,10},{10... | collective-permute-start | bytes 1843208 | tf_op jit(solution)/shard_map/ppermute | solution.py:468
  19.8 0.0 collective-permute-start.5
  19.8 0.5 collective-permute-start.11
  20.3 11.6 %collective-permute-done.12.refs_5_ = bf16[160,1920]{1,0:T(8,128)(2,1)} collective-permute-done((bf16[160,1920]{1,0:T(8,128)(2,1)}, bf16[160,1920]{1,0:T(8,128)(2,1)}, u32[]{:S(2)}, u32[]{:S(2)}) %collective-permute-start.12) | collective-permute-done | bytes 614432 | tf_op jit(solution)/shard_map/ppermute | solution.py:468
  31.9 2.4 %collective-permute-start.13 = (bf16[160,1920]{1,0:T(8,128)(2,1)}, bf16[160,1920]{1,0:T(8,128)(2,1)}, u32[]{:S(2)}, u32[]{:S(2)}) collective-permute-start(bf16[160,1920]{1,0:T(8,128)(2,1)} %collective-permute-done.12.refs_5_), channel_id=1, source_target_pairs={{0,8},{8,0},{16,24},{24,16},{1,9},{9,1},{17,25},{25,17},{2,10},{10... | collective-permute-start | bytes 1843208 | tf_op jit(solution)/shard_map/ppermute | solution.py:468
  34.3 2.4 %pack_travellers.1 = (bf16[512,1024]{1,0:T(8,128)(2,1)}, bf16[512,512]{1,0:T(8,128)(2,1)}) custom-call(bf16[512,1280]{1,0:T(8,128)(2,1)} %q_ref.6, bf16[512,1280]{1,0:T(8,128)(2,1)} %k_ref.9, bf16[512,1280]{1,0:T(8,128)(2,1)} %v_ref.9), custom_call_target="tpu_custom_call" | custom-call | bytes 5242880 | tf_op jit(solution)/shard_map/pack_travellers/pallas_call | solution.py:353
  36.7 0.0 collective-permute-done.3.refs_4_
  36.7 0.0 collective-permute-done.5.refs_6_
  36.7 7.9 %head_grads.2 = (bf16[160,1920]{1,0:T(8,128)(2,1)}, bf16[160,1920]{1,0:T(8,128)(2,1)}, bf16[160,1920]{1,0:T(8,128)(2,1)}, f32[160,1920]{1,0:T(8,128)}) custom-call(f32[2,512]{1,0:T(2,128)} %bitcast.1, bf16[512,1280]{1,0:T(8,128)(2,1)} %refs_1_.1, bf16[512,1280]{1,0:T(8,128)(2,1)} %refs_2_.3, bf16[160,1920]{1,0:T(8,128)(2,1)} %round_head.2.refs_3_, ...), custom_call_target="tpu_custom_call" | custom-call | flops 2516582400 | bytes 8000000 | tf_op jit(solution)/shard_map/head_grads/pallas_call | solution.py:291
  44.6 0.1 collective-permute-start.7
  44.7 1.5 collective-permute-start.9
  46.1 0.0 collective-permute-done.11.refs_4_
  46.2 0.0 collective-permute-done.13.refs_6_
  46.2 7.9 %head_grads.3 = (bf16[160,1920]{1,0:T(8,128)(2,1)}, bf16[160,1920]{1,0:T(8,128)(2,1)}, bf16[160,1920]{1,0:T(8,128)(2,1)}, f32[160,1920]{1,0:T(8,128)}) custom-call(f32[2,512]{1,0:T(2,128)} %bitcast.2, bf16[512,1280]{1,0:T(8,128)(2,1)} %refs_1_.1, bf16[512,1280]{1,0:T(8,128)(2,1)} %refs_2_.3, bf16[160,1920]{1,0:T(8,128)(2,1)} %round_head.3.refs_3_, ...), custom_call_target="tpu_custom_call" | custom-call | flops 2516582400 | bytes 8000000 | tf_op jit(solution)/shard_map/head_grads/pallas_call | solution.py:291
  54.1 0.6 collective-permute-start.15
  54.7 5.2 %collective-permute-done.9.fk_ref.fv_ref = bf16[512,512]{1,0:T(8,128)(2,1)} collective-permute-done((bf16[512,512]{1,0:T(8,128)(2,1)}, bf16[512,512]{1,0:T(8,128)(2,1)}, u32[]{:S(2)}, u32[]{:S(2)}) %collective-permute-start.9) | collective-permute-done | bytes 524320 | tf_op jit(solution)/shard_map/ppermute | solution.py:474
  59.9 1.3 collective-permute-start.10
  61.2 0.0 collective-permute-start.1
  61.2 0.5 collective-permute-start.2
  61.7 0.0 collective-permute-done.7
  61.7 0.0 collective-permute-start.6
  61.7 1.4 add_convert_fusion.1
  63.1 0.0 collective-permute-done.10.fpk_ref.fpv_ref
  63.2 0.1 collective-permute-start.8
  63.2 0.0 collective-permute-done.15
  63.2 4.3 %collective-permute-start = (bf16[512,1024]{1,0:T(8,128)(2,1)}, bf16[512,1024]{1,0:T(8,128)(2,1)}, u32[]{:S(2)}, u32[]{:S(2)}) collective-permute-start(bf16[512,1024]{1,0:T(8,128)(2,1)} %get-tuple-element.45), channel_id=1, source_target_pairs={{16,0},{24,8},{17,1},{25,9},{18,2},{26,10},{19,3},{27,11},{20,4},{... | collective-permute-start | bytes 3145736 | tf_op jit(solution)/shard_map/ppermute | solution.py:474
  67.6 1.0 add_convert_fusion
  68.5 1.1 collective-permute-start.14
  69.6 8.5 %collective-permute-done.8.refs_2_ = bf16[160,1920]{1,0:T(8,128)(2,1)S(1)} collective-permute-done((bf16[160,1920]{1,0:T(8,128)(2,1)S(1)}, bf16[160,1920]{1,0:T(8,128)(2,1)S(1)}, u32[]{:S(2)}, u32[]{:S(2)}) %collective-permute-start.8) | collective-permute-done | bytes 614432 | tf_op jit(solution)/shard_map/ppermute | solution.py:468
  78.1 0.8 copy-done.2
  78.9 0.3 collective-permute-start.16
  79.2 3.7 %move_weights.2 = (f32[160,3840]{1,0:T(8,128)}, f32[160,3840]{1,0:T(8,128)}, bf16[160,1920]{1,0:T(8,128)(2,1)}) custom-call(f32[160,3840]{1,0:T(8,128)} %w_ref.6, f32[160,3840]{1,0:T(8,128)} %m_ref.2, f32[160,1920]{1,0:T(8,128)} %get-tuple-element.51.refs_0_, bf16[160,1920]{1,0:T(8,128)(2,1)} %copy-done.1, bf16[160,1920]{1,0:T(8,128)(2,1)} %copy-done.2), custom_call_target="tpu_custom_call" | custom-call | flops 6144000 | bytes 7987200 | tf_op jit(solution)/shard_map/move_weights/pallas_call | solution.py:397
  82.9 15.8 %collective-permute-done.far_ref = bf16[512,1024]{1,0:T(8,128)(2,1)} collective-permute-done((bf16[512,1024]{1,0:T(8,128)(2,1)}, bf16[512,1024]{1,0:T(8,128)(2,1)}, u32[]{:S(2)}, u32[]{:S(2)}) %collective-permute-start) | collective-permute-done | bytes 1048608 | tf_op jit(solution)/shard_map/ppermute | solution.py:474
  98.8 2.2 %collective-permute-start.25 = (bf16[160,1920]{1,0:T(8,128)(2,1)}, bf16[160,1920]{1,0:T(8,128)(2,1)}, u32[]{:S(2)}, u32[]{:S(2)}) collective-permute-start(bf16[160,1920]{1,0:T(8,128)(2,1)} %get-tuple-element.55.refs_0_), channel_id=1, source_target_pairs={{0,16},{8,24},{16,0},{24,8},{1,17},{9,25},{17,1},{25,9},{2,18},{10... | collective-permute-start | bytes 1843208 | tf_op jit(solution)/shard_map/ppermute | solution.py:468
  101.0 0.0 collective-permute-done.1.pk_ref
  101.0 0.0 collective-permute-done.2.pv_ref
  101.0 6.3 %shard_map.122.refs_4_ = bf16[512,1280]{1,0:T(8,128)(2,1)} custom-call(bf16[512,1280]{1,0:T(8,128)(2,1)} %q_ref.6, bf16[512,1280]{1,0:T(8,128)(2,1)} %k_ref.9, bf16[512,1280]{1,0:T(8,128)(2,1)} %v_ref.9, bf16[512,1280]{1,0:T(8,128)(2,1)} %collective-permute-done.1.pk_ref, bf16[512,1280]{1,0:T(8,128)(2,1)} %collective-permute-done.2.pv_ref, ...), custom_call_target="tpu_custom_call" | custom-call | flops 590558016 | bytes 2621440 | tf_op jit(solution)/shard_map/pallas_call | solution.py:181
  107.3 4.7 %collective-permute-done.16.refs_2_ = bf16[160,1920]{1,0:T(8,128)(2,1)} collective-permute-done((bf16[160,1920]{1,0:T(8,128)(2,1)}, bf16[160,1920]{1,0:T(8,128)(2,1)}, u32[]{:S(2)}, u32[]{:S(2)}) %collective-permute-start.16) | collective-permute-done | bytes 614432 | tf_op jit(solution)/shard_map/ppermute | solution.py:468
  111.9 3.7 %move_weights.3 = (f32[160,3840]{1,0:T(8,128)}, f32[160,3840]{1,0:T(8,128)}, bf16[160,1920]{1,0:T(8,128)(2,1)}) custom-call(f32[160,3840]{1,0:T(8,128)} %w_ref.6, f32[160,3840]{1,0:T(8,128)} %m_ref.2, f32[160,1920]{1,0:T(8,128)} %get-tuple-element.61.refs_0_, ...), custom_call_target="tpu_custom_call", output_to_operand_aliasing={{0}: (5, {}), {1}: (6, {})} | custom-call | flops 6144000 | bytes 7987200 | tf_op jit(solution)/shard_map/move_weights/pallas_call | solution.py:397
  115.7 2.2 %collective-permute-start.22 = (bf16[160,1920]{1,0:T(8,128)(2,1)}, bf16[160,1920]{1,0:T(8,128)(2,1)}, u32[]{:S(2)}, u32[]{:S(2)}) collective-permute-start(bf16[160,1920]{1,0:T(8,128)(2,1)} %get-tuple-element.67.refs_0_), channel_id=1, source_target_pairs={{0,16},{8,24},{16,0},{24,8},{1,17},{9,25},{17,1},{25,9},{2,18},{10... | collective-permute-start | bytes 1843208 | tf_op jit(solution)/shard_map/ppermute | solution.py:468
  117.9 6.6 %shard_map.123 = (bf16[512,512]{1,0:T(8,128)(2,1)}, f32[8,512]{1,0:T(8,128)}, bf16[512,512]{1,0:T(8,128)(2,1)}, f32[8,512]{1,0:T(8,128)}) custom-call(bf16[512,1280]{1,0:T(8,128)(2,1)} %q_ref.6, bf16[512,1024]{1,0:T(8,128)(2,1)} %collective-permute-done.far_ref, bf16[512,1280]{1,0:T(8,128)(2,1)} %k_ref.9, bf16[512,1280]{1,0:T(8,128)(2,1)} %v_ref.9, ...), custom_call_target="tpu_custom_call" | custom-call | flops 858993472 | bytes 6291456 | tf_op jit(solution)/shard_map/pallas_call | solution.py:181
  124.4 1.3 collective-permute-start.19
  125.7 2.1 %collective-permute-start.24 = (bf16[160,1920]{1,0:T(8,128)(2,1)}, bf16[160,1920]{1,0:T(8,128)(2,1)}, u32[]{:S(2)}, u32[]{:S(2)}) collective-permute-start(bf16[160,1920]{1,0:T(8,128)(2,1)} %get-tuple-element.55.refs_0_), channel_id=1, source_target_pairs={{0,8},{8,0},{16,24},{24,16},{1,9},{9,1},{17,25},{25,17},{2,10},{10... | collective-permute-start | bytes 1843208 | tf_op jit(solution)/shard_map/ppermute | solution.py:468
  127.8 0.1 collective-permute-start.26
  127.9 1.3 collective-permute-start.20
  129.2 6.7 %shard_map.121 = (bf16[512,512]{1,0:T(8,128)(2,1)}, f32[8,512]{1,0:T(8,128)}, bf16[512,512]{1,0:T(8,128)(2,1)}, f32[8,512]{1,0:T(8,128)}) custom-call(bf16[512,1280]{1,0:T(8,128)(2,1)} %q_ref.6, bf16[512,1024]{1,0:T(8,128)(2,1)} %collective-permute-done.far_ref, bf16[512,1280]{1,0:T(8,128)(2,1)} %k_ref.9, bf16[512,1280]{1,0:T(8,128)(2,1)} %v_ref.9, ...), custom_call_target="tpu_custom_call" | custom-call | flops 858993472 | bytes 6291456 | tf_op jit(solution)/shard_map/pallas_call | solution.py:181
  135.9 6.4 %collective-permute-done.20.refs_3_ = f32[8,512]{1,0:T(8,128)} collective-permute-done((f32[8,512]{1,0:T(8,128)}, f32[8,512]{1,0:T(8,128)}, u32[]{:S(2)}, u32[]{:S(2)}) %collective-permute-start.20) | collective-permute-done | bytes 16416 | tf_op jit(solution)/shard_map/ppermute | solution.py:474
  142.2 1.3 collective-permute-start.17
  143.5 1.6 collective-permute-start.18
  145.1 10.8 %collective-permute-done.18.refs_3_ = f32[8,512]{1,0:T(8,128)} collective-permute-done((f32[8,512]{1,0:T(8,128)}, f32[8,512]{1,0:T(8,128)}, u32[]{:S(2)}, u32[]{:S(2)}) %collective-permute-start.18) | collective-permute-done | bytes 16416 | tf_op jit(solution)/shard_map/ppermute | solution.py:474
  155.9 3.2 %collective-permute-start.21 = (bf16[160,1920]{1,0:T(8,128)(2,1)}, bf16[160,1920]{1,0:T(8,128)(2,1)}, u32[]{:S(2)}, u32[]{:S(2)}) collective-permute-start(bf16[160,1920]{1,0:T(8,128)(2,1)} %get-tuple-element.67.refs_0_), channel_id=1, source_target_pairs={{0,8},{8,0},{16,24},{24,16},{1,9},{9,1},{17,25},{25,17},{2,10},{10... | collective-permute-start | bytes 1843208 | tf_op jit(solution)/shard_map/ppermute | solution.py:468
  159.1 0.0 collective-permute-start.23
  159.1 2.4 %shard_map.124.refs_4_ = bf16[512,1280]{1,0:T(8,128)(2,1)} custom-call(bf16[512,512]{1,0:T(8,128)(2,1)} %get-tuple-element.72.refs_0_, f32[8,512]{1,0:T(8,128)} %get-tuple-element.73.refs_1_, bf16[512,512]{1,0:T(8,128)(2,1)} %collective-permute-done.19.refs_2_, f32[8,512]{1,0:T(8,128)} %collective-permute-done.20.refs_3_, ...), custom_call_target="tpu_custom_call", output_to_operand_aliasing={{}: (4, {})} | custom-call | flops 5368709 | bytes 2621440 | tf_op jit(solution)/shard_map/pallas_call | solution.py:181
  161.5 0.0 collective-permute-done.17.refs_2_
  161.5 2.4 %shard_map.125 = bf16[512,1280]{1,0:T(8,128)(2,1)} custom-call(bf16[512,512]{1,0:T(8,128)(2,1)} %get-tuple-element.47.refs_0_, f32[8,512]{1,0:T(8,128)} %get-tuple-element.48.refs_1_, bf16[512,512]{1,0:T(8,128)(2,1)} %collective-permute-done.17.refs_2_, f32[8,512]{1,0:T(8,128)} %collective-permute-done.18.refs_3_, ...), custom_call_target="tpu_custom_call", output_to_operand_aliasing={{}: (4, {})} | custom-call | flops 5368709 | bytes 2621440 | tf_op jit(solution)/shard_map/pallas_call | solution.py:181
  163.9 4.8 %head_query.2.refs_4_ = bf16[512,1280]{1,0:T(8,128)(2,1)} custom-call(bf16[512,1280]{1,0:T(8,128)(2,1)} %q_hbm.3, bf16[160,1920]{1,0:T(8,128)(2,1)} %get-tuple-element.55.refs_0_, bf16[160,1920]{1,0:T(8,128)(2,1)} %collective-permute-done.24.refs_1_, bf16[160,1920]{1,0:T(8,128)(2,1)} %collective-permute-done.25.refs_2_, ...), custom_call_target="tpu_custom_call" | custom-call | flops 1258291200 | bytes 4000000 | tf_op jit(solution)/shard_map/head_query/pallas_call | solution.py:448
  168.7 0.0 collective-permute-done.21.refs_1_
  168.7 4.8 %head_query.3 = bf16[512,1280]{1,0:T(8,128)(2,1)} custom-call(bf16[512,1280]{1,0:T(8,128)(2,1)} %q_hbm.3, bf16[160,1920]{1,0:T(8,128)(2,1)} %get-tuple-element.67.refs_0_, bf16[160,1920]{1,0:T(8,128)(2,1)} %collective-permute-done.21.refs_1_, bf16[160,1920]{1,0:T(8,128)(2,1)} %collective-permute-done.22.refs_2_, ...), custom_call_target="tpu_custom_call", output_to_operand_aliasing={{}: (5, {})} | custom-call | flops 1258291200 | bytes 4000000 | tf_op jit(solution)/shard_map/head_query/pallas_call | solution.py:448
  (13 shorter events, 0.0 us)
Async XLA Ops:
  2.7 15.1 %collective-permute-start.4 = (bf16[160,1920]{1,0:T(8,128)(2,1)}, bf16[160,1920]{1,0:T(8,128)(2,1)}, u32[]{:S(2)}, u32[]{:S(2)}) collective-permute-start(bf16[160,1920]{1,0:T(8,128)(2,1)} %round_head.2.refs_3_), channel_id=1, source_target_pairs={{0,16},{8,24},{16,0},{24,8},{1,17},{9,25},{17,1},{25,9},{2,18},{10... | collective-permute-start | bytes 1843208 | tf_op jit(solution)/shard_map/ppermute | solution.py:468
  17.7 14.2 %collective-permute-start.12 = (bf16[160,1920]{1,0:T(8,128)(2,1)}, bf16[160,1920]{1,0:T(8,128)(2,1)}, u32[]{:S(2)}, u32[]{:S(2)}) collective-permute-start(bf16[160,1920]{1,0:T(8,128)(2,1)} %round_head.3.refs_3_), channel_id=1, source_target_pairs={{0,16},{8,24},{16,0},{24,8},{1,17},{9,25},{17,1},{25,9},{2,18},{10... | collective-permute-start | bytes 1843208 | tf_op jit(solution)/shard_map/ppermute | solution.py:468
  18.0 18.7 %collective-permute-start.3 = (bf16[160,1920]{1,0:T(8,128)(2,1)}, bf16[160,1920]{1,0:T(8,128)(2,1)}, u32[]{:S(2)}, u32[]{:S(2)}) collective-permute-start(bf16[160,1920]{1,0:T(8,128)(2,1)} %round_head.2.refs_3_), channel_id=1, source_target_pairs={{0,8},{8,0},{16,24},{24,16},{1,9},{9,1},{17,25},{25,17},{2,10},{10... | collective-permute-start | bytes 1843208 | tf_op jit(solution)/shard_map/ppermute | solution.py:468
  19.8 16.9 %collective-permute-start.5 = (bf16[160,1920]{1,0:T(8,128)(2,1)}, bf16[160,1920]{1,0:T(8,128)(2,1)}, u32[]{:S(2)}, u32[]{:S(2)}) collective-permute-start(bf16[160,1920]{1,0:T(8,128)(2,1)} %collective-permute-done.4.refs_5_), channel_id=1, source_target_pairs={{0,8},{8,0},{16,24},{24,16},{1,9},{9,1},{17,25},{25,17},{2,10},{10... | collective-permute-start | bytes 1843208 | tf_op jit(solution)/shard_map/ppermute | solution.py:468
  19.8 26.4 %collective-permute-start.11 = (bf16[160,1920]{1,0:T(8,128)(2,1)}, bf16[160,1920]{1,0:T(8,128)(2,1)}, u32[]{:S(2)}, u32[]{:S(2)}) collective-permute-start(bf16[160,1920]{1,0:T(8,128)(2,1)} %round_head.3.refs_3_), channel_id=1, source_target_pairs={{0,8},{8,0},{16,24},{24,16},{1,9},{9,1},{17,25},{25,17},{2,10},{10... | collective-permute-start | bytes 1843208 | tf_op jit(solution)/shard_map/ppermute | solution.py:468
  31.9 14.3 %collective-permute-start.13 = (bf16[160,1920]{1,0:T(8,128)(2,1)}, bf16[160,1920]{1,0:T(8,128)(2,1)}, u32[]{:S(2)}, u32[]{:S(2)}) collective-permute-start(bf16[160,1920]{1,0:T(8,128)(2,1)} %collective-permute-done.12.refs_5_), channel_id=1, source_target_pairs={{0,8},{8,0},{16,24},{24,16},{1,9},{9,1},{17,25},{25,17},{2,10},{10... | collective-permute-start | bytes 1843208 | tf_op jit(solution)/shard_map/ppermute | solution.py:468
  44.6 17.1 %collective-permute-start.7 = (bf16[160,1920]{1,0:T(8,128)(2,1)}, bf16[160,1920]{1,0:T(8,128)(2,1)}, u32[]{:S(2)}, u32[]{:S(2)}) collective-permute-start(bf16[160,1920]{1,0:T(8,128)(2,1)} %get-tuple-element.54), channel_id=1, source_target_pairs={{0,8},{8,0},{16,24},{24,16},{1,9},{9,1},{17,25},{25,17},{2,10},{10... | collective-permute-start | bytes 1843208 | tf_op jit(solution)/shard_map/ppermute | solution.py:468
  44.7 15.2 %collective-permute-start.9 = (bf16[512,512]{1,0:T(8,128)(2,1)}, bf16[512,512]{1,0:T(8,128)(2,1)}, u32[]{:S(2)}, u32[]{:S(2)}) collective-permute-start(bf16[512,512]{1,0:T(8,128)(2,1)} %get-tuple-element.57), channel_id=1, source_target_pairs={{0,16},{8,24},{1,17},{9,25},{2,18},{10,26},{3,19},{11,27},{4,20},{... | collective-permute-start | bytes 1572872 | tf_op jit(solution)/shard_map/ppermute | solution.py:474
  54.1 13.5 %copy-start = (bf16[160,1920]{1,0:T(8,128)(2,1)S(1)}, bf16[160,1920]{1,0:T(8,128)(2,1)}, u32[]{:S(2)}) copy-start(bf16[160,1920]{1,0:T(8,128)(2,1)} %get-tuple-element.63) | copy-start | bytes 1843204
  54.1 9.1 %collective-permute-start.15 = (bf16[160,1920]{1,0:T(8,128)(2,1)}, bf16[160,1920]{1,0:T(8,128)(2,1)S(1)}, u32[]{:S(2)}, u32[]{:S(2)}) collective-permute-start(bf16[160,1920]{1,0:T(8,128)(2,1)} %get-tuple-element.64), channel_id=1, source_target_pairs={{0,8},{8,0},{16,24},{24,16},{1,9},{9,1},{17,25},{25,17},{2,10},{10... | collective-permute-start | bytes 1843208 | tf_op jit(solution)/shard_map/ppermute | solution.py:468
  59.9 3.3 %collective-permute-start.10 = (bf16[512,512]{1,0:T(8,128)(2,1)}, bf16[512,512]{1,0:T(8,128)(2,1)}, u32[]{:S(2)}, u32[]{:S(2)}) collective-permute-start(bf16[512,512]{1,0:T(8,128)(2,1)} %collective-permute-done.9.fk_ref.fv_ref), channel_id=1, source_target_pairs={{0,8},{8,0},{16,24},{24,16},{1,9},{9,1},{17,25},{25,17},{2,10},{10... | collective-permute-start | bytes 1572872 | tf_op jit(solution)/shard_map/ppermute | solution.py:468
  61.2 39.8 %collective-permute-start.1 = (bf16[512,1280]{1,0:T(8,128)(2,1)}, bf16[512,1280]{1,0:T(8,128)(2,1)}, u32[]{:S(2)}, u32[]{:S(2)}) collective-permute-start(bf16[512,1280]{1,0:T(8,128)(2,1)} %k_ref.9), channel_id=1, source_target_pairs={{0,8},{8,0},{16,24},{24,16},{1,9},{9,1},{17,25},{25,17},{2,10},{10... | collective-permute-start | bytes 3932168 | tf_op jit(solution)/shard_map/ppermute | solution.py:468
  61.2 39.8 %collective-permute-start.2 = (bf16[512,1280]{1,0:T(8,128)(2,1)}, bf16[512,1280]{1,0:T(8,128)(2,1)}, u32[]{:S(2)}, u32[]{:S(2)}) collective-permute-start(bf16[512,1280]{1,0:T(8,128)(2,1)} %v_ref.9), channel_id=1, source_target_pairs={{0,8},{8,0},{16,24},{24,16},{1,9},{9,1},{17,25},{25,17},{2,10},{10... | collective-permute-start | bytes 3932168 | tf_op jit(solution)/shard_map/ppermute | solution.py:468
  61.7 6.8 %collective-permute-start.6 = (bf16[160,1920]{1,0:T(8,128)(2,1)}, bf16[160,1920]{1,0:T(8,128)(2,1)S(1)}, u32[]{:S(2)}, u32[]{:S(2)}) collective-permute-start(bf16[160,1920]{1,0:T(8,128)(2,1)} %get-tuple-element.52), channel_id=1, source_target_pairs={{0,8},{8,0},{16,24},{24,16},{1,9},{9,1},{17,25},{25,17},{2,10},{10... | collective-permute-start | bytes 1843208 | tf_op jit(solution)/shard_map/ppermute | solution.py:468
  63.2 15.0 %collective-permute-start.8 = (bf16[160,1920]{1,0:T(8,128)(2,1)S(1)}, bf16[160,1920]{1,0:T(8,128)(2,1)S(1)}, u32[]{:S(2)}, u32[]{:S(2)}) collective-permute-start(bf16[160,1920]{1,0:T(8,128)(2,1)S(1)} %add_convert_fusion.1), channel_id=1, source_target_pairs={{0,16},{8,24},{16,0},{24,8},{1,17},{9,25},{17,1},{25,9},{2,18},{10... | collective-permute-start | bytes 1843208 | tf_op jit(solution)/shard_map/ppermute | solution.py:468
  63.2 35.5 %collective-permute-start = (bf16[512,1024]{1,0:T(8,128)(2,1)}, bf16[512,1024]{1,0:T(8,128)(2,1)}, u32[]{:S(2)}, u32[]{:S(2)}) collective-permute-start(bf16[512,1024]{1,0:T(8,128)(2,1)} %get-tuple-element.45), channel_id=1, source_target_pairs={{16,0},{24,8},{17,1},{25,9},{18,2},{26,10},{19,3},{27,11},{20,4},{... | collective-permute-start | bytes 3145736 | tf_op jit(solution)/shard_map/ppermute | solution.py:474
  68.5 9.6 %copy-start.1 = (bf16[160,1920]{1,0:T(8,128)(2,1)}, bf16[160,1920]{1,0:T(8,128)(2,1)S(1)}, u32[]{:S(2)}) copy-start(bf16[160,1920]{1,0:T(8,128)(2,1)S(1)} %collective-permute-done.6.refs_1_) | copy-start | bytes 1843204
  68.5 38.7 %collective-permute-start.14 = (bf16[160,1920]{1,0:T(8,128)(2,1)}, bf16[160,1920]{1,0:T(8,128)(2,1)}, u32[]{:S(2)}, u32[]{:S(2)}) collective-permute-start(bf16[160,1920]{1,0:T(8,128)(2,1)} %get-tuple-element.62), channel_id=1, source_target_pairs={{0,8},{8,0},{16,24},{24,16},{1,9},{9,1},{17,25},{25,17},{2,10},{10... | collective-permute-start | bytes 1843208 | tf_op jit(solution)/shard_map/ppermute | solution.py:468
  78.1 0.8 copy-start.2
  78.9 33.0 %collective-permute-start.16 = (bf16[160,1920]{1,0:T(8,128)(2,1)}, bf16[160,1920]{1,0:T(8,128)(2,1)}, u32[]{:S(2)}, u32[]{:S(2)}) collective-permute-start(bf16[160,1920]{1,0:T(8,128)(2,1)} %add_convert_fusion), channel_id=1, source_target_pairs={{0,16},{8,24},{16,0},{24,8},{1,17},{9,25},{17,1},{25,9},{2,18},{10... | collective-permute-start | bytes 1843208 | tf_op jit(solution)/shard_map/ppermute | solution.py:468
  98.8 29.0 %collective-permute-start.25 = (bf16[160,1920]{1,0:T(8,128)(2,1)}, bf16[160,1920]{1,0:T(8,128)(2,1)}, u32[]{:S(2)}, u32[]{:S(2)}) collective-permute-start(bf16[160,1920]{1,0:T(8,128)(2,1)} %get-tuple-element.55.refs_0_), channel_id=1, source_target_pairs={{0,16},{8,24},{16,0},{24,8},{1,17},{9,25},{17,1},{25,9},{2,18},{10... | collective-permute-start | bytes 1843208 | tf_op jit(solution)/shard_map/ppermute | solution.py:468
  115.7 43.5 %collective-permute-start.22 = (bf16[160,1920]{1,0:T(8,128)(2,1)}, bf16[160,1920]{1,0:T(8,128)(2,1)}, u32[]{:S(2)}, u32[]{:S(2)}) collective-permute-start(bf16[160,1920]{1,0:T(8,128)(2,1)} %get-tuple-element.67.refs_0_), channel_id=1, source_target_pairs={{0,16},{8,24},{16,0},{24,8},{1,17},{9,25},{17,1},{25,9},{2,18},{10... | collective-permute-start | bytes 1843208 | tf_op jit(solution)/shard_map/ppermute | solution.py:468
  124.4 19.1 %collective-permute-start.19 = (bf16[512,512]{1,0:T(8,128)(2,1)}, bf16[512,512]{1,0:T(8,128)(2,1)}, u32[]{:S(2)}, u32[]{:S(2)}) collective-permute-start(bf16[512,512]{1,0:T(8,128)(2,1)} %get-tuple-element.74), channel_id=1, source_target_pairs={{0,16},{8,24},{1,17},{9,25},{2,18},{10,26},{3,19},{11,27},{4,20},{... | collective-permute-start | bytes 1572872 | tf_op jit(solution)/shard_map/ppermute | solution.py:474
  125.7 38.2 %collective-permute-start.24 = (bf16[160,1920]{1,0:T(8,128)(2,1)}, bf16[160,1920]{1,0:T(8,128)(2,1)}, u32[]{:S(2)}, u32[]{:S(2)}) collective-permute-start(bf16[160,1920]{1,0:T(8,128)(2,1)} %get-tuple-element.55.refs_0_), channel_id=1, source_target_pairs={{0,8},{8,0},{16,24},{24,16},{1,9},{9,1},{17,25},{25,17},{2,10},{10... | collective-permute-start | bytes 1843208 | tf_op jit(solution)/shard_map/ppermute | solution.py:468
  127.8 36.1 %collective-permute-start.26 = (bf16[160,1920]{1,0:T(8,128)(2,1)}, bf16[160,1920]{1,0:T(8,128)(2,1)}, u32[]{:S(2)}, u32[]{:S(2)}) collective-permute-start(bf16[160,1920]{1,0:T(8,128)(2,1)} %collective-permute-done.25.refs_2_), channel_id=1, source_target_pairs={{0,8},{8,0},{16,24},{24,16},{1,9},{9,1},{17,25},{25,17},{2,10},{10... | collective-permute-start | bytes 1843208 | tf_op jit(solution)/shard_map/ppermute | solution.py:468
  127.9 14.3 %collective-permute-start.20 = (f32[8,512]{1,0:T(8,128)}, f32[8,512]{1,0:T(8,128)}, u32[]{:S(2)}, u32[]{:S(2)}) collective-permute-start(f32[8,512]{1,0:T(8,128)} %get-tuple-element.75), channel_id=1, source_target_pairs={{0,16},{8,24},{1,17},{9,25},{2,18},{10,26},{3,19},{11,27},{4,20},{... | collective-permute-start | bytes 49160 | tf_op jit(solution)/shard_map/ppermute | solution.py:474
  142.2 19.3 %collective-permute-start.17 = (bf16[512,512]{1,0:T(8,128)(2,1)}, bf16[512,512]{1,0:T(8,128)(2,1)}, u32[]{:S(2)}, u32[]{:S(2)}) collective-permute-start(bf16[512,512]{1,0:T(8,128)(2,1)} %get-tuple-element.68), channel_id=1, source_target_pairs={{0,16},{8,24},{1,17},{9,25},{2,18},{10,26},{3,19},{11,27},{4,20},{... | collective-permute-start | bytes 1572872 | tf_op jit(solution)/shard_map/ppermute | solution.py:474
  143.5 12.4 %collective-permute-start.18 = (f32[8,512]{1,0:T(8,128)}, f32[8,512]{1,0:T(8,128)}, u32[]{:S(2)}, u32[]{:S(2)}) collective-permute-start(f32[8,512]{1,0:T(8,128)} %get-tuple-element.70), channel_id=1, source_target_pairs={{0,16},{8,24},{1,17},{9,25},{2,18},{10,26},{3,19},{11,27},{4,20},{... | collective-permute-start | bytes 49160 | tf_op jit(solution)/shard_map/ppermute | solution.py:474
  155.9 12.8 %collective-permute-start.21 = (bf16[160,1920]{1,0:T(8,128)(2,1)}, bf16[160,1920]{1,0:T(8,128)(2,1)}, u32[]{:S(2)}, u32[]{:S(2)}) collective-permute-start(bf16[160,1920]{1,0:T(8,128)(2,1)} %get-tuple-element.67.refs_0_), channel_id=1, source_target_pairs={{0,8},{8,0},{16,24},{24,16},{1,9},{9,1},{17,25},{25,17},{2,10},{10... | collective-permute-start | bytes 1843208 | tf_op jit(solution)/shard_map/ppermute | solution.py:468
  159.1 9.6 %collective-permute-start.23 = (bf16[160,1920]{1,0:T(8,128)(2,1)}, bf16[160,1920]{1,0:T(8,128)(2,1)}, u32[]{:S(2)}, u32[]{:S(2)}) collective-permute-start(bf16[160,1920]{1,0:T(8,128)(2,1)} %collective-permute-done.22.refs_2_), channel_id=1, source_target_pairs={{0,8},{8,0},{16,24},{24,16},{1,9},{9,1},{17,25},{25,17},{2,10},{10... | collective-permute-start | bytes 1843208 | tf_op jit(solution)/shard_map/ppermute | solution.py:468

commit v5 on v4

--- a/solution.py
+++ b/solution.py
@@ -67,15 +67,29 @@
             st_ref[per_step + g : per_step + g + 1, rows] = total
 
 
+def pieces_of(value, count):
+    rows = []
+    for _ in range(count):
+        rows.append(value.astype(BF16).astype(F32))
+        value = value - rows[-1]
+    return rows
+
+
+def stat_places(per_step):
+    return 16 * pl.cdiv(5 * per_step, 16)
+
+
 def group_kernel(
-    per_step, q_ref, far_ref, k_ref, v_ref, pk_ref, pv_ref, o_ref, st_ref, fo_ref, fst_ref, lo_ref, lst_ref
+    per_step, q_ref, far_ref, k_ref, v_ref, pk_ref, pv_ref, o_ref, st_ref, fo_ref, lo_ref, lst_ref
 ):
     leading = lax.axis_index("ctx") % 2 == 0
-    for g in range(per_step):
-        cols = slice(g * HD, (g + 1) * HD)
-        top, bottom = slice(g, g + 1), slice(per_step + g, per_step + g + 1)
-        for first in range(0, q_ref.shape[0], CHUNK):
-            rows = slice(first, first + CHUNK)
+    places = stat_places(per_step)
+    for first in range(0, q_ref.shape[0], CHUNK):
+        rows = slice(first, first + CHUNK)
+        stats = []
+        for g in range(per_step):
+            cols = slice(g * HD, (g + 1) * HD)
+            top, bottom = slice(g, g + 1), slice(per_step + g, per_step + g + 1)
             far = far_ref[rows, cols]
             scores = masked(dot(k_ref[first:, cols], far, 1, 1), False, first, first)
             far_o, far_m, far_l = soft(scores, v_ref[first:, cols])
@@ -85,8 +99,7 @@
             far_keep = scaled_to(far_m, far_top)
             far_add = jnp.where(leading, scaled_to(highest, far_top), 0.0)
             fo_ref[cols, rows] = (far_o * far_keep + mixed * far_add).astype(BF16)
-            fst_ref[top, rows] = far_top
-            fst_ref[bottom, rows] = far_l * far_keep + total * far_add
+            stats += pieces_of(far_top, 3) + pieces_of(far_l * far_keep + total * far_add, 2)
             own_m = st_ref[top, rows]
             own_top = jnp.where(leading, own_m, jnp.maximum(own_m, highest))
             own_keep = scaled_to(own_m, own_top)
@@ -94,19 +107,23 @@
             lo_ref[cols, rows] = (o_ref[cols, rows].astype(F32) * own_keep + mixed * own_add).astype(BF16)
             lst_ref[top, rows] = own_top
             lst_ref[bottom, rows] = st_ref[bottom, rows] * own_keep + total * own_add
-
-
-def merge_kernel(per_step, o_ref, st_ref, fo_ref, fst_ref, out_ref):
+        stats += [jnp.zeros_like(stats[0])] * (places - len(stats))
+        fo_ref[per_step * HD :, rows] = jnp.concatenate(stats, axis=0).astype(BF16)
+
+
+def merge_kernel(per_step, o_ref, st_ref, fo_ref, out_ref):
     valid = lax.axis_index("ctx") >= 2
+    stats = fo_ref[per_step * HD :, :].astype(F32)
     for g in range(per_step):
         cols = slice(g * HD, (g + 1) * HD)
         top, bottom = slice(g, g + 1), slice(per_step + g, per_step + g + 1)
+        m0, m1, m2, l0, l1 = [stats[5 * g + i : 5 * g + i + 1, :] for i in range(5)]
         own_m = st_ref[top, :]
-        far_m = jnp.where(valid, fst_ref[top, :], LOWEST)
+        far_m = jnp.where(valid, m0 + m1 + m2, LOWEST)
         highest = jnp.maximum(own_m, far_m)
         own_keep = scaled_to(own_m, highest)
         far_keep = scaled_to(far_m, highest)
-        total = st_ref[bottom, :] * own_keep + fst_ref[bottom, :] * far_keep
+        total = st_ref[bottom, :] * own_keep + (l0 + l1) * far_keep
         mixed = o_ref[cols, :].astype(F32) * own_keep + fo_ref[cols, :].astype(F32) * far_keep
         out_ref[:, cols] = (mixed / total).T.astype(BF16)
 
@@ -152,6 +169,7 @@
     )
 
     stat_rows = 8 * pl.cdiv(2 * per_step, 8)
+    far_rows = per_step * HD + stat_places(per_step)
 
     def spec(kind, first):
         step = first // per_step
@@ -159,11 +177,15 @@
             return pl.BlockSpec((per_step * HD, rows), lambda i: (i + step, 0))
         if kind == "s":
             return pl.BlockSpec((stat_rows, rows), lambda i: (i + step, 0))
+        if kind == "f":
+            return pl.BlockSpec((far_rows, rows), lambda i: (i + step, 0))
         return pl.BlockSpec((rows, per_step * HD), lambda i: (0, i + step))
 
     def shape(kind):
         if kind == "t":
             return jax.ShapeDtypeStruct((heads * HD, rows), BF16)
+        if kind == "f":
+            return jax.ShapeDtypeStruct((far_rows * (heads // per_step), rows), BF16)
         if kind == "s":
             return jax.ShapeDtypeStruct((stat_rows * (heads // per_step), rows), F32)
         return jax.ShapeDtypeStruct(into[0], BF16)
@@ -311,6 +333,26 @@
     )(fw_rate.T, fw_key, fw_value, *parts)
 
 
+def add_kernel(left_ref, right_ref, sum_ref):
+    sum_ref[...] = (left_ref[...].astype(F32) + right_ref[...].astype(F32)).astype(BF16)
+
+
+def add_rows(left, right):
+    rows, width = left.shape
+    block = row_block(rows, 80)
+    spec = pl.BlockSpec((block, width), lambda i: (i, 0))
+    return pl.pallas_call(
+        add_kernel,
+        grid=(rows // block,),
+        in_specs=[spec, spec],
+        out_specs=spec,
+        out_shape=jax.ShapeDtypeStruct((rows, width), BF16),
+        compiler_params=PARAMS,
+        cost_estimate=cost(rows * width, 6 * rows * width),
+        name="add_rows",
+    )(left, right)
+
+
 def round_kernel(w_ref, low_ref):
     low_ref[...] = w_ref[...].astype(BF16)
 
@@ -335,10 +377,10 @@
 
 
 def pack_kernel(q_ref, k_ref, v_ref, queries_ref, pairs_ref):
-    width = k_ref.shape[1]
+    first, width = queries_ref.shape[1], pairs_ref.shape[1] // 2
     queries_ref[...] = q_ref[...]
-    pairs_ref[:, :width] = k_ref[...]
-    pairs_ref[:, width:] = v_ref[...]
+    pairs_ref[:, :width] = k_ref[:, first:]
+    pairs_ref[:, width:] = v_ref[:, first:]
 
 
 def pack_travellers(attn_query, attn_key, attn_value, stay):
@@ -346,14 +388,14 @@
     block = row_block(rows, 256)
     left, right = stay * HD, width - stay * HD
 
-    def spec(cols, first=0):
-        return pl.BlockSpec((block, cols), lambda i: (i, first // cols))
+    def spec(cols):
+        return pl.BlockSpec((block, cols), lambda i: (i, 0))
 
     widths = (left, 2 * right)
     return pl.pallas_call(
         pack_kernel,
         grid=(rows // block,),
-        in_specs=[spec(left), spec(right, left), spec(right, left)],
+        in_specs=[spec(left), spec(width), spec(width)],
         out_specs=[spec(cols) for cols in widths],
         out_shape=[jax.ShapeDtypeStruct((rows, cols), BF16) for cols in widths],
         compiler_params=PARAMS,
@@ -492,7 +534,7 @@
     far, near, across, own = pieces
     far = swapped(far, 1)
     near = swapped(near, 1)
-    total = (across.astype(F32) + far.astype(F32)).astype(BF16)
+    total = add_rows(across, far)
     return [own, near, swapped(total, 2)], total
 
 
@@ -504,9 +546,7 @@
     paired = devices == 4
     heads = range(head_local)
     all_heads = attn_query.shape[1] // HD
-    moved = max(1, all_heads // 5)
-    while all_heads % moved:
-        moved -= 1
+    moved = 2 * all_heads // 5
     stay = all_heads - moved
     half = stay // 2 if stay % 2 == 0 else stay
     halves = range(0, stay, half)
@@ -529,8 +569,8 @@
         before = low
         gathered.append(gather_rows(after(low, started), paired))
     queries, pairs = pack_travellers(after(attn_query, before), attn_key, attn_value, stay)
-    far_query = shifted(queries, -2)
-    far_pairs = shifted(pairs, 2)
+    far_query = shifted(after(queries, started), -2)
+    far_pairs = shifted(after(pairs, started), 2)
     far_pairs_other = swapped(far_pairs, 1)
     pair_key = swapped(attn_key, 1)
     pair_value = swapped(attn_value, 1)
@@ -560,12 +600,12 @@
                     *own,
                 ],
                 [first] * 6 + [("t", first), ("s", first)],
-                [("t", 0), ("s", 0), ("t", 0), ("s", 0)],
+                [("f", 0), ("t", 0), ("s", 0)],
                 1.6,
                 most=half,
             )
         )
-        before = after(found[-1][1], totals[-1])
+        before = after(found[-1][2], totals[-1])
 
     fw_new = None
     new_gathered = []
@@ -598,10 +638,10 @@
             )[0]
             momentum = after(momentum, attn_out)
     returned = []
-    for number, (far_o, far_st, own_o, own_st) in enumerate(found):
+    for number, (far_o, own_o, own_st) in enumerate(found):
         if number > 0:
-            far_o, far_st = after(far_o, low), after(far_st, low)
-        returned.append((own_o, own_st, shifted(far_o, 2), shifted(far_st, 2)))
+            far_o = after(far_o, low)
+        returned.append((own_o, own_st, shifted(far_o, 2)))
     fw_out = None
     for head in heads:
         fw_out = head_query(fw_query, new_gathered[head], head, fw_out)
@@ -610,7 +650,7 @@
             merge_kernel,
             half,
             states,
-            [("t", 0), ("s", 0), ("t", 0), ("s", 0)],
+            [("t", 0), ("s", 0), ("f", 0)],
             [number * half],
             0.01,
             (attn_query.shape, attn_out),

time: 174 us -> 166 us (0.954)
  waiting for transfers between devices: 69.3 us -> 61.6 us
  Pallas kernels: 70 us -> 75.3 us
  starting transfers between devices: 30.1 us -> 27.5 us
  other arithmetic: 2.37 us -> 0 us
    ppermute x6 -> x4, waiting for transfers between devices: 38.3 us -> 21.2 us  [shifted(): return lax.ppermute(array, 'ctx', pairs)]
    ppermute x21, waiting for transfers between devices: 31 us -> 40.4 us  [swapped(): return lax.ppermute(array, 'ctx', [(i, i ^ mask) for i in range(devices)])]
    pallas_call x0 -> x2, Pallas kernels: none -> 4.12 us  [add_rows(): pl.pallas_call(add_kernel, grid=(rows // block,), in_specs=[spec, spec],...]
    ppermute x6 -> x4, starting transfers between devices: 11.2 us -> 7.39 us  [shifted(): return lax.ppermute(array, 'ctx', pairs)]
    convert_element_type x2 -> x0, other arithmetic: 2.37 us -> none  [sum_rows(): total = (across.astype(F32) + far.astype(F32)).astype(BF16)]
  transfers between devices with their start and end apart: 27 -> 25, of which waited for: 8 -> 8; matrix products, arithmetic and copies ran while one was open for 1% -> 0% of each run, Pallas kernels for 36% -> 41%
where the time goes in v5:
time: 166 us; the launch traced here: 165 us
  Pallas kernels  75.3 us (45%)
  waiting for transfers between devices  61.6 us (37%)
  starting transfers between devices  27.5 us (17%)
    ppermute x21, waiting for transfers between devices, swapped(): return lax.ppermute(array, 'ctx', [(i, i ^ mask) for i in range(devices)])  40.4 us
    pallas_call x6, Pallas kernels, attention_call(): pl.pallas_call(body, grid=(heads // per_step,), in_specs=in_specs, out_sp...  31.4 us
    ppermute x4, waiting for transfers between devices, shifted(): return lax.ppermute(array, 'ctx', pairs)  21.2 us
    ppermute x21, starting transfers between devices, swapped(): return lax.ppermute(array, 'ctx', [(i, i ^ mask) for i in range(devices)])  20.1 us
    pallas_call x2, Pallas kernels, head_grads(): pl.pallas_call(functools.partial(grads_kernel, masks, split, head), in_sp...  15.8 us
    pallas_call x2, Pallas kernels, head_query(): pl.pallas_call(lambda q_hbm, *refs: query_kernel(masks, q_hbm, head, *ref...  9.53 us
    pallas_call x2, Pallas kernels, move_weights(): pl.pallas_call(functools.partial(move_kernel, len(addends)), grid=(rows /...  7.43 us
    ppermute x4, starting transfers between devices, shifted(): return lax.ppermute(array, 'ctx', pairs)  7.39 us
  transfers between devices with their start and end apart: 25, of which 8 were waited for; matrix products, arithmetic and copies ran while one was open for 0% of the time, Pallas kernels for 41%

profile of v5, /device:TPU:7, one launch (start us, length us, event | category | flops | bytes accessed | tf_op | source)
XLA Modules:
  0.0 165.3 jit_solution(8605136998886952869)
XLA Ops:
  0.6 2.0 %round_head.2.refs_3_ = bf16[160,1920]{1,0:T(8,128)(2,1)} custom-call(f32[160,3840]{1,0:T(8,128)} %w_ref.6), custom_call_target="tpu_custom_call" | custom-call | flops 307200 | bytes 1843200 | tf_op jit(solution)/shard_map/round_head/pallas_call | solution.py:367
  2.7 0.3 collective-permute-start
  2.9 5.6 %shard_map.120 = (bf16[768,512]{1,0:T(8,128)(2,1)}, f32[16,512]{1,0:T(8,128)}) custom-call(bf16[512,1280]{1,0:T(8,128)(2,1)} %q_ref.6, bf16[512,1280]{1,0:T(8,128)(2,1)} %k_ref.9, bf16[512,1280]{1,0:T(8,128)(2,1)} %v_ref.9), custom_call_target="tpu_custom_call" | custom-call | flops 483183808 | bytes 3932160 | tf_op jit(solution)/shard_map/pallas_call | solution.py:203
  8.5 2.0 %round_head.3.refs_3_ = bf16[160,1920]{1,0:T(8,128)(2,1)} custom-call(f32[160,3840]{1,0:T(8,128)} %w_ref.6), custom_call_target="tpu_custom_call" | custom-call | flops 307200 | bytes 1843200 | tf_op jit(solution)/shard_map/round_head/pallas_call | solution.py:367
  10.5 7.2 %collective-permute-done.refs_5_ = bf16[160,1920]{1,0:T(8,128)(2,1)} collective-permute-done((bf16[160,1920]{1,0:T(8,128)(2,1)}, bf16[160,1920]{1,0:T(8,128)(2,1)}, u32[]{:S(2)}, u32[]{:S(2)}) %collective-permute-start) | collective-permute-done | bytes 614432 | tf_op jit(solution)/shard_map/ppermute | solution.py:510
  17.7 0.3 collective-permute-start.12
  18.0 1.8 %collective-permute-start.4 = (bf16[160,1920]{1,0:T(8,128)(2,1)}, bf16[160,1920]{1,0:T(8,128)(2,1)}, u32[]{:S(2)}, u32[]{:S(2)}) collective-permute-start(bf16[160,1920]{1,0:T(8,128)(2,1)} %round_head.2.refs_3_), channel_id=1, source_target_pairs={{0,8},{8,0},{16,24},{24,16},{1,9},{9,1},{17,25},{25,17},{2,10},{10... | collective-permute-start | bytes 1843208 | tf_op jit(solution)/shard_map/ppermute | solution.py:510
  19.8 0.0 collective-permute-start.5
  19.8 0.5 collective-permute-start.11
  20.3 11.6 %collective-permute-done.12.refs_5_ = bf16[160,1920]{1,0:T(8,128)(2,1)} collective-permute-done((bf16[160,1920]{1,0:T(8,128)(2,1)}, bf16[160,1920]{1,0:T(8,128)(2,1)}, u32[]{:S(2)}, u32[]{:S(2)}) %collective-permute-start.12) | collective-permute-done | bytes 614432 | tf_op jit(solution)/shard_map/ppermute | solution.py:510
  31.9 2.4 %collective-permute-start.13 = (bf16[160,1920]{1,0:T(8,128)(2,1)}, bf16[160,1920]{1,0:T(8,128)(2,1)}, u32[]{:S(2)}, u32[]{:S(2)}) collective-permute-start(bf16[160,1920]{1,0:T(8,128)(2,1)} %collective-permute-done.12.refs_5_), channel_id=1, source_target_pairs={{0,8},{8,0},{16,24},{24,16},{1,9},{9,1},{17,25},{25,17},{2,10},{10... | collective-permute-start | bytes 1843208 | tf_op jit(solution)/shard_map/ppermute | solution.py:510
  34.3 0.0 collective-permute-start.2
  34.3 2.9 %pack_travellers.1 = (bf16[512,768]{1,0:T(8,128)(2,1)}, bf16[512,1024]{1,0:T(8,128)(2,1)}) custom-call(bf16[512,1280]{1,0:T(8,128)(2,1)} %q_ref.6, bf16[512,1280]{1,0:T(8,128)(2,1)} %k_ref.9, bf16[512,1280]{1,0:T(8,128)(2,1)} %v_ref.9), custom_call_target="tpu_custom_call" | custom-call | bytes 5242880 | tf_op jit(solution)/shard_map/pack_travellers/pallas_call | solution.py:395
  37.2 0.0 collective-permute-done.4.refs_4_
  37.2 1.5 collective-permute-start.9
  38.7 0.0 collective-permute-done.5.refs_6_
  38.7 7.9 %head_grads.2 = (bf16[160,1920]{1,0:T(8,128)(2,1)}, bf16[160,1920]{1,0:T(8,128)(2,1)}, bf16[160,1920]{1,0:T(8,128)(2,1)}, f32[160,1920]{1,0:T(8,128)}) custom-call(f32[2,512]{1,0:T(2,128)} %bitcast.1, bf16[512,1280]{1,0:T(8,128)(2,1)} %refs_1_.1, bf16[512,1280]{1,0:T(8,128)(2,1)} %refs_2_.3, bf16[160,1920]{1,0:T(8,128)(2,1)} %round_head.2.refs_3_, ...), custom_call_target="tpu_custom_call" | custom-call | flops 2516582400 | bytes 8000000 | tf_op jit(solution)/shard_map/head_grads/pallas_call | solution.py:313
  46.6 0.6 collective-permute-start.7
  47.2 0.0 collective-permute-done.11.refs_4_
  47.2 0.0 collective-permute-done.13.refs_6_
  47.2 7.9 %head_grads.3 = (bf16[160,1920]{1,0:T(8,128)(2,1)}, bf16[160,1920]{1,0:T(8,128)(2,1)}, bf16[160,1920]{1,0:T(8,128)(2,1)}, f32[160,1920]{1,0:T(8,128)}) custom-call(f32[2,512]{1,0:T(2,128)} %bitcast.2, bf16[512,1280]{1,0:T(8,128)(2,1)} %refs_1_.1, bf16[512,1280]{1,0:T(8,128)(2,1)} %refs_2_.3, bf16[160,1920]{1,0:T(8,128)(2,1)} %round_head.3.refs_3_, ...), custom_call_target="tpu_custom_call" | custom-call | flops 2516582400 | bytes 8000000 | tf_op jit(solution)/shard_map/head_grads/pallas_call | solution.py:313
  55.1 0.1 collective-permute-start.15
  55.2 0.5 collective-permute-start.3
  55.7 0.0 collective-permute-done.7.right_ref
  55.7 0.1 collective-permute-start.6
  55.8 2.0 %add_rows.2 = bf16[160,1920]{1,0:T(8,128)(2,1)} custom-call(bf16[160,1920]{1,0:T(8,128)(2,1)} %get-tuple-element.53.left_ref, bf16[160,1920]{1,0:T(8,128)(2,1)} %collective-permute-done.7.right_ref), custom_call_target="tpu_custom_call" | custom-call | flops 307200 | bytes 1843200 | tf_op jit(solution)/shard_map/add_rows/pallas_call | solution.py:344
  57.8 5.8 %collective-permute-done.9.fk_ref.fv_ref = bf16[512,1024]{1,0:T(8,128)(2,1)} collective-permute-done((bf16[512,1024]{1,0:T(8,128)(2,1)}, bf16[512,1024]{1,0:T(8,128)(2,1)}, u32[]{:S(2)}, u32[]{:S(2)}) %collective-permute-start.9) | collective-permute-done | bytes 1048608 | tf_op jit(solution)/shard_map/ppermute | solution.py:516
  63.6 0.0 collective-permute-start.8
  63.6 0.0 collective-permute-done.15.right_ref
  63.6 1.4 collective-permute-start.10
  65.0 2.1 %add_rows.3 = bf16[160,1920]{1,0:T(8,128)(2,1)} custom-call(bf16[160,1920]{1,0:T(8,128)(2,1)} %get-tuple-element.64.left_ref, bf16[160,1920]{1,0:T(8,128)(2,1)} %collective-permute-done.15.right_ref), custom_call_target="tpu_custom_call" | custom-call | flops 307200 | bytes 1843200 | tf_op jit(solution)/shard_map/add_rows/pallas_call | solution.py:344
  67.1 0.0 collective-permute-done.2.pk_ref
  67.1 0.0 collective-permute-start.14
  67.1 0.0 collective-permute-done.6.refs_1_
  67.1 1.8 %collective-permute-start.16 = (bf16[160,1920]{1,0:T(8,128)(2,1)}, bf16[160,1920]{1,0:T(8,128)(2,1)}, u32[]{:S(2)}, u32[]{:S(2)}) collective-permute-start(bf16[160,1920]{1,0:T(8,128)(2,1)} %add_rows.3), channel_id=1, source_target_pairs={{0,16},{8,24},{16,0},{24,8},{1,17},{9,25},{17,1},{25,9},{2,18},{10... | collective-permute-start | bytes 1843208 | tf_op jit(solution)/shard_map/ppermute | solution.py:510
  68.9 9.1 %collective-permute-done.8.refs_2_ = bf16[160,1920]{1,0:T(8,128)(2,1)} collective-permute-done((bf16[160,1920]{1,0:T(8,128)(2,1)}, bf16[160,1920]{1,0:T(8,128)(2,1)}, u32[]{:S(2)}, u32[]{:S(2)}) %collective-permute-start.8) | collective-permute-done | bytes 614432 | tf_op jit(solution)/shard_map/ppermute | solution.py:510
  78.0 3.1 %collective-permute-start.1 = (bf16[512,768]{1,0:T(8,128)(2,1)}, bf16[512,768]{1,0:T(8,128)(2,1)}, u32[]{:S(2)}, u32[]{:S(2)}) collective-permute-start(bf16[512,768]{1,0:T(8,128)(2,1)} %get-tuple-element.45), channel_id=1, source_target_pairs={{16,0},{24,8},{17,1},{25,9},{18,2},{26,10},{19,3},{27,11},{20,4},{... | collective-permute-start | bytes 2359304 | tf_op jit(solution)/shard_map/ppermute | solution.py:516
  81.1 3.7 %move_weights.2 = (f32[160,3840]{1,0:T(8,128)}, f32[160,3840]{1,0:T(8,128)}, bf16[160,1920]{1,0:T(8,128)(2,1)}) custom-call(f32[160,3840]{1,0:T(8,128)} %w_ref.6, f32[160,3840]{1,0:T(8,128)} %m_ref.2, f32[160,1920]{1,0:T(8,128)} %get-tuple-element.51.refs_0_, bf16[160,1920]{1,0:T(8,128)(2,1)} %collective-permute-done.6.refs_1_, ...), custom_call_target="tpu_custom_call" | custom-call | flops 6144000 | bytes 7987200 | tf_op jit(solution)/shard_map/move_weights/pallas_call | solution.py:439
  84.8 0.0 collective-permute-done.3.pv_ref
  84.8 0.1 collective-permute-start.23
  84.9 0.0 collective-permute-done.10.fpk_ref.fpv_ref
  84.9 10.4 %shard_map.122.refs_3_ = bf16[512,1280]{1,0:T(8,128)(2,1)} custom-call(bf16[512,1280]{1,0:T(8,128)(2,1)} %q_ref.6, bf16[512,1280]{1,0:T(8,128)(2,1)} %k_ref.9, bf16[512,1280]{1,0:T(8,128)(2,1)} %v_ref.9, bf16[512,1280]{1,0:T(8,128)(2,1)} %collective-permute-done.2.pk_ref, bf16[512,1280]{1,0:T(8,128)(2,1)} %collective-permute-done.3.pv_ref, ...), custom_call_target="tpu_custom_call" | custom-call | flops 1181116032 | bytes 5242880 | tf_op jit(solution)/shard_map/pallas_call | solution.py:203
  95.3 0.0 collective-permute-done.16.refs_2_
  95.3 3.7 %move_weights.3 = (f32[160,3840]{1,0:T(8,128)}, f32[160,3840]{1,0:T(8,128)}, bf16[160,1920]{1,0:T(8,128)(2,1)}) custom-call(f32[160,3840]{1,0:T(8,128)} %w_ref.6, f32[160,3840]{1,0:T(8,128)} %m_ref.2, f32[160,1920]{1,0:T(8,128)} %get-tuple-element.62.refs_0_, ...), custom_call_target="tpu_custom_call", output_to_operand_aliasing={{0}: (5, {}), {1}: (6, {})} | custom-call | flops 6144000 | bytes 7987200 | tf_op jit(solution)/shard_map/move_weights/pallas_call | solution.py:439
  99.0 1.4 collective-permute-start.20
  100.4 5.7 %collective-permute-done.1.far_ref = bf16[512,768]{1,0:T(8,128)(2,1)} collective-permute-done((bf16[512,768]{1,0:T(8,128)(2,1)}, bf16[512,768]{1,0:T(8,128)(2,1)}, u32[]{:S(2)}, u32[]{:S(2)}) %collective-permute-start.1) | collective-permute-done | bytes 786464 | tf_op jit(solution)/shard_map/ppermute | solution.py:516
  106.1 5.6 %shard_map.123 = (bf16[400,512]{1,0:T(8,128)(2,1)}, bf16[384,512]{1,0:T(8,128)(2,1)}, f32[8,512]{1,0:T(8,128)}) custom-call(bf16[512,1280]{1,0:T(8,128)(2,1)} %q_ref.6, bf16[512,768]{1,0:T(8,128)(2,1)} %collective-permute-done.1.far_ref, bf16[512,1280]{1,0:T(8,128)(2,1)} %k_ref.9, bf16[512,1280]{1,0:T(8,128)(2,1)} %v_ref.9, ...), custom_call_target="tpu_custom_call" | custom-call | flops 644245120 | bytes 4325376 | tf_op jit(solution)/shard_map/pallas_call | solution.py:203
  111.7 1.3 collective-permute-start.18
  113.0 3.5 %collective-permute-start.22 = (bf16[160,1920]{1,0:T(8,128)(2,1)}, bf16[160,1920]{1,0:T(8,128)(2,1)}, u32[]{:S(2)}, u32[]{:S(2)}) collective-permute-start(bf16[160,1920]{1,0:T(8,128)(2,1)} %get-tuple-element.55.refs_0_), channel_id=1, source_target_pairs={{0,8},{8,0},{16,24},{24,16},{1,9},{9,1},{17,25},{25,17},{2,10},{10... | collective-permute-start | bytes 1843208 | tf_op jit(solution)/shard_map/ppermute | solution.py:510
  116.5 2.8 %collective-permute-done.23.refs_2_ = bf16[160,1920]{1,0:T(8,128)(2,1)} collective-permute-done((bf16[160,1920]{1,0:T(8,128)(2,1)}, bf16[160,1920]{1,0:T(8,128)(2,1)}, u32[]{:S(2)}, u32[]{:S(2)}) %collective-permute-start.23) | collective-permute-done | bytes 614432 | tf_op jit(solution)/shard_map/ppermute | solution.py:510
  119.3 3.5 %collective-permute-start.24 = (bf16[160,1920]{1,0:T(8,128)(2,1)}, bf16[160,1920]{1,0:T(8,128)(2,1)}, u32[]{:S(2)}, u32[]{:S(2)}) collective-permute-start(bf16[160,1920]{1,0:T(8,128)(2,1)} %collective-permute-done.23.refs_2_), channel_id=1, source_target_pairs={{0,8},{8,0},{16,24},{24,16},{1,9},{9,1},{17,25},{25,17},{2,10},{10... | collective-permute-start | bytes 1843208 | tf_op jit(solution)/shard_map/ppermute | solution.py:510
  122.7 9.7 %collective-permute-done.20.refs_2_ = bf16[160,1920]{1,0:T(8,128)(2,1)} collective-permute-done((bf16[160,1920]{1,0:T(8,128)(2,1)}, bf16[160,1920]{1,0:T(8,128)(2,1)}, u32[]{:S(2)}, u32[]{:S(2)}) %collective-permute-start.20) | collective-permute-done | bytes 614432 | tf_op jit(solution)/shard_map/ppermute | solution.py:510
  132.4 1.9 %collective-permute-start.21 = (bf16[160,1920]{1,0:T(8,128)(2,1)}, bf16[160,1920]{1,0:T(8,128)(2,1)}, u32[]{:S(2)}, u32[]{:S(2)}) collective-permute-start(bf16[160,1920]{1,0:T(8,128)(2,1)} %collective-permute-done.20.refs_2_), channel_id=1, source_target_pairs={{0,8},{8,0},{16,24},{24,16},{1,9},{9,1},{17,25},{25,17},{2,10},{10... | collective-permute-start | bytes 1843208 | tf_op jit(solution)/shard_map/ppermute | solution.py:510
  134.4 5.5 %shard_map.121 = (bf16[400,512]{1,0:T(8,128)(2,1)}, bf16[384,512]{1,0:T(8,128)(2,1)}, f32[8,512]{1,0:T(8,128)}) custom-call(bf16[512,1280]{1,0:T(8,128)(2,1)} %q_ref.6, bf16[512,768]{1,0:T(8,128)(2,1)} %collective-permute-done.1.far_ref, bf16[512,1280]{1,0:T(8,128)(2,1)} %k_ref.9, bf16[512,1280]{1,0:T(8,128)(2,1)} %v_ref.9, ...), custom_call_target="tpu_custom_call" | custom-call | flops 644245120 | bytes 4325376 | tf_op jit(solution)/shard_map/pallas_call | solution.py:203
  139.9 0.0 collective-permute-done.18.refs_2_
  139.9 1.5 collective-permute-start.17
  141.4 2.2 %shard_map.124.refs_3_ = bf16[512,1280]{1,0:T(8,128)(2,1)} custom-call(bf16[384,512]{1,0:T(8,128)(2,1)} %get-tuple-element.71.refs_0_, f32[8,512]{1,0:T(8,128)} %get-tuple-element.72.refs_1_, bf16[400,512]{1,0:T(8,128)(2,1)} %collective-permute-done.18.refs_2_, bf16[512,1280]{1,0:T(8,128)(2,1)} %shard_map.122.refs_3_), custom_call_target="tpu_custom_call", output_to_operand_aliasing={{}: (3, {})} | custom-call | flops 4026531 | bytes 1572864 | tf_op jit(solution)/shard_map/pallas_call | solution.py:203
  143.6 9.7 %collective-permute-done.17.refs_2_ = bf16[400,512]{1,0:T(8,128)(2,1)} collective-permute-done((bf16[400,512]{1,0:T(8,128)(2,1)}, bf16[400,512]{1,0:T(8,128)(2,1)}, u32[]{:S(2)}, u32[]{:S(2)}) %collective-permute-start.17) | collective-permute-done | bytes 409632 | tf_op jit(solution)/shard_map/ppermute | solution.py:516
  153.4 2.2 %shard_map.125 = bf16[512,1280]{1,0:T(8,128)(2,1)} custom-call(bf16[384,512]{1,0:T(8,128)(2,1)} %get-tuple-element.47.refs_0_, f32[8,512]{1,0:T(8,128)} %get-tuple-element.48.refs_1_, bf16[400,512]{1,0:T(8,128)(2,1)} %collective-permute-done.17.refs_2_, bf16[512,1280]{1,0:T(8,128)(2,1)} %shard_map.124.refs_3_), custom_call_target="tpu_custom_call", output_to_operand_aliasing={{}: (3, {})} | custom-call | flops 4026531 | bytes 1572864 | tf_op jit(solution)/shard_map/pallas_call | solution.py:203
  155.5 0.0 collective-permute-done.22.refs_1_
  155.6 0.0 collective-permute-done.24.refs_3_
  155.6 4.8 %head_query.2.refs_4_ = bf16[512,1280]{1,0:T(8,128)(2,1)} custom-call(bf16[512,1280]{1,0:T(8,128)(2,1)} %q_hbm.3, bf16[160,1920]{1,0:T(8,128)(2,1)} %get-tuple-element.55.refs_0_, bf16[160,1920]{1,0:T(8,128)(2,1)} %collective-permute-done.22.refs_1_, bf16[160,1920]{1,0:T(8,128)(2,1)} %collective-permute-done.23.refs_2_, ...), custom_call_target="tpu_custom_call" | custom-call | flops 1258291200 | bytes 4000000 | tf_op jit(solution)/shard_map/head_query/pallas_call | solution.py:490
  160.3 0.0 collective-permute-done.21.refs_3_
  160.3 4.8 %head_query.3 = bf16[512,1280]{1,0:T(8,128)(2,1)} custom-call(bf16[512,1280]{1,0:T(8,128)(2,1)} %q_hbm.3, bf16[160,1920]{1,0:T(8,128)(2,1)} %get-tuple-element.68.refs_0_, bf16[160,1920]{1,0:T(8,128)(2,1)} %collective-permute-done.19.refs_1_, bf16[160,1920]{1,0:T(8,128)(2,1)} %collective-permute-done.20.refs_2_, ...), custom_call_target="tpu_custom_call", output_to_operand_aliasing={{}: (5, {})} | custom-call | flops 1258291200 | bytes 4000000 | tf_op jit(solution)/shard_map/head_query/pallas_call | solution.py:490
  (3 shorter events, 0.0 us)
Async XLA Ops:
  2.7 15.1 %collective-permute-start = (bf16[160,1920]{1,0:T(8,128)(2,1)}, bf16[160,1920]{1,0:T(8,128)(2,1)}, u32[]{:S(2)}, u32[]{:S(2)}) collective-permute-start(bf16[160,1920]{1,0:T(8,128)(2,1)} %round_head.2.refs_3_), channel_id=1, source_target_pairs={{0,16},{8,24},{16,0},{24,8},{1,17},{9,25},{17,1},{25,9},{2,18},{10... | collective-permute-start | bytes 1843208 | tf_op jit(solution)/shard_map/ppermute | solution.py:510
  17.7 14.2 %collective-permute-start.12 = (bf16[160,1920]{1,0:T(8,128)(2,1)}, bf16[160,1920]{1,0:T(8,128)(2,1)}, u32[]{:S(2)}, u32[]{:S(2)}) collective-permute-start(bf16[160,1920]{1,0:T(8,128)(2,1)} %round_head.3.refs_3_), channel_id=1, source_target_pairs={{0,16},{8,24},{16,0},{24,8},{1,17},{9,25},{17,1},{25,9},{2,18},{10... | collective-permute-start | bytes 1843208 | tf_op jit(solution)/shard_map/ppermute | solution.py:510
  18.0 19.2 %collective-permute-start.4 = (bf16[160,1920]{1,0:T(8,128)(2,1)}, bf16[160,1920]{1,0:T(8,128)(2,1)}, u32[]{:S(2)}, u32[]{:S(2)}) collective-permute-start(bf16[160,1920]{1,0:T(8,128)(2,1)} %round_head.2.refs_3_), channel_id=1, source_target_pairs={{0,8},{8,0},{16,24},{24,16},{1,9},{9,1},{17,25},{25,17},{2,10},{10... | collective-permute-start | bytes 1843208 | tf_op jit(solution)/shard_map/ppermute | solution.py:510
  19.8 18.9 %collective-permute-start.5 = (bf16[160,1920]{1,0:T(8,128)(2,1)}, bf16[160,1920]{1,0:T(8,128)(2,1)}, u32[]{:S(2)}, u32[]{:S(2)}) collective-permute-start(bf16[160,1920]{1,0:T(8,128)(2,1)} %collective-permute-done.refs_5_), channel_id=1, source_target_pairs={{0,8},{8,0},{16,24},{24,16},{1,9},{9,1},{17,25},{25,17},{2,10},{10... | collective-permute-start | bytes 1843208 | tf_op jit(solution)/shard_map/ppermute | solution.py:510
  19.8 27.4 %collective-permute-start.11 = (bf16[160,1920]{1,0:T(8,128)(2,1)}, bf16[160,1920]{1,0:T(8,128)(2,1)}, u32[]{:S(2)}, u32[]{:S(2)}) collective-permute-start(bf16[160,1920]{1,0:T(8,128)(2,1)} %round_head.3.refs_3_), channel_id=1, source_target_pairs={{0,8},{8,0},{16,24},{24,16},{1,9},{9,1},{17,25},{25,17},{2,10},{10... | collective-permute-start | bytes 1843208 | tf_op jit(solution)/shard_map/ppermute | solution.py:510
  31.9 15.3 %collective-permute-start.13 = (bf16[160,1920]{1,0:T(8,128)(2,1)}, bf16[160,1920]{1,0:T(8,128)(2,1)}, u32[]{:S(2)}, u32[]{:S(2)}) collective-permute-start(bf16[160,1920]{1,0:T(8,128)(2,1)} %collective-permute-done.12.refs_5_), channel_id=1, source_target_pairs={{0,8},{8,0},{16,24},{24,16},{1,9},{9,1},{17,25},{25,17},{2,10},{10... | collective-permute-start | bytes 1843208 | tf_op jit(solution)/shard_map/ppermute | solution.py:510
  34.3 32.8 %collective-permute-start.2 = (bf16[512,1280]{1,0:T(8,128)(2,1)}, bf16[512,1280]{1,0:T(8,128)(2,1)}, u32[]{:S(2)}, u32[]{:S(2)}) collective-permute-start(bf16[512,1280]{1,0:T(8,128)(2,1)} %k_ref.9), channel_id=1, source_target_pairs={{0,8},{8,0},{16,24},{24,16},{1,9},{9,1},{17,25},{25,17},{2,10},{10... | collective-permute-start | bytes 3932168 | tf_op jit(solution)/shard_map/ppermute | solution.py:510
  37.2 26.4 %collective-permute-start.9 = (bf16[512,1024]{1,0:T(8,128)(2,1)}, bf16[512,1024]{1,0:T(8,128)(2,1)}, u32[]{:S(2)}, u32[]{:S(2)}) collective-permute-start(bf16[512,1024]{1,0:T(8,128)(2,1)} %get-tuple-element.58), channel_id=1, source_target_pairs={{0,16},{8,24},{1,17},{9,25},{2,18},{10,26},{3,19},{11,27},{4,20},{... | collective-permute-start | bytes 3145736 | tf_op jit(solution)/shard_map/ppermute | solution.py:516
  46.6 9.1 %collective-permute-start.7 = (bf16[160,1920]{1,0:T(8,128)(2,1)}, bf16[160,1920]{1,0:T(8,128)(2,1)}, u32[]{:S(2)}, u32[]{:S(2)}) collective-permute-start(bf16[160,1920]{1,0:T(8,128)(2,1)} %get-tuple-element.54), channel_id=1, source_target_pairs={{0,8},{8,0},{16,24},{24,16},{1,9},{9,1},{17,25},{25,17},{2,10},{10... | collective-permute-start | bytes 1843208 | tf_op jit(solution)/shard_map/ppermute | solution.py:510
  55.1 8.5 %collective-permute-start.15 = (bf16[160,1920]{1,0:T(8,128)(2,1)}, bf16[160,1920]{1,0:T(8,128)(2,1)}, u32[]{:S(2)}, u32[]{:S(2)}) collective-permute-start(bf16[160,1920]{1,0:T(8,128)(2,1)} %get-tuple-element.65), channel_id=1, source_target_pairs={{0,8},{8,0},{16,24},{24,16},{1,9},{9,1},{17,25},{25,17},{2,10},{10... | collective-permute-start | bytes 1843208 | tf_op jit(solution)/shard_map/ppermute | solution.py:510
  55.2 29.6 %collective-permute-start.3 = (bf16[512,1280]{1,0:T(8,128)(2,1)}, bf16[512,1280]{1,0:T(8,128)(2,1)}, u32[]{:S(2)}, u32[]{:S(2)}) collective-permute-start(bf16[512,1280]{1,0:T(8,128)(2,1)} %v_ref.9), channel_id=1, source_target_pairs={{0,8},{8,0},{16,24},{24,16},{1,9},{9,1},{17,25},{25,17},{2,10},{10... | collective-permute-start | bytes 3932168 | tf_op jit(solution)/shard_map/ppermute | solution.py:510
  55.7 11.4 %collective-permute-start.6 = (bf16[160,1920]{1,0:T(8,128)(2,1)}, bf16[160,1920]{1,0:T(8,128)(2,1)}, u32[]{:S(2)}, u32[]{:S(2)}) collective-permute-start(bf16[160,1920]{1,0:T(8,128)(2,1)} %get-tuple-element.52), channel_id=1, source_target_pairs={{0,8},{8,0},{16,24},{24,16},{1,9},{9,1},{17,25},{25,17},{2,10},{10... | collective-permute-start | bytes 1843208 | tf_op jit(solution)/shard_map/ppermute | solution.py:510
  63.6 14.4 %collective-permute-start.8 = (bf16[160,1920]{1,0:T(8,128)(2,1)}, bf16[160,1920]{1,0:T(8,128)(2,1)}, u32[]{:S(2)}, u32[]{:S(2)}) collective-permute-start(bf16[160,1920]{1,0:T(8,128)(2,1)} %add_rows.2), channel_id=1, source_target_pairs={{0,16},{8,24},{16,0},{24,8},{1,17},{9,25},{17,1},{25,9},{2,18},{10... | collective-permute-start | bytes 1843208 | tf_op jit(solution)/shard_map/ppermute | solution.py:510
  63.6 21.2 %collective-permute-start.10 = (bf16[512,1024]{1,0:T(8,128)(2,1)}, bf16[512,1024]{1,0:T(8,128)(2,1)}, u32[]{:S(2)}, u32[]{:S(2)}) collective-permute-start(bf16[512,1024]{1,0:T(8,128)(2,1)} %collective-permute-done.9.fk_ref.fv_ref), channel_id=1, source_target_pairs={{0,8},{8,0},{16,24},{24,16},{1,9},{9,1},{17,25},{25,17},{2,10},{10... | collective-permute-start | bytes 3145736 | tf_op jit(solution)/shard_map/ppermute | solution.py:510
  67.1 28.2 %collective-permute-start.14 = (bf16[160,1920]{1,0:T(8,128)(2,1)}, bf16[160,1920]{1,0:T(8,128)(2,1)}, u32[]{:S(2)}, u32[]{:S(2)}) collective-permute-start(bf16[160,1920]{1,0:T(8,128)(2,1)} %get-tuple-element.63), channel_id=1, source_target_pairs={{0,8},{8,0},{16,24},{24,16},{1,9},{9,1},{17,25},{25,17},{2,10},{10... | collective-permute-start | bytes 1843208 | tf_op jit(solution)/shard_map/ppermute | solution.py:510
  67.1 28.1 %collective-permute-start.16 = (bf16[160,1920]{1,0:T(8,128)(2,1)}, bf16[160,1920]{1,0:T(8,128)(2,1)}, u32[]{:S(2)}, u32[]{:S(2)}) collective-permute-start(bf16[160,1920]{1,0:T(8,128)(2,1)} %add_rows.3), channel_id=1, source_target_pairs={{0,16},{8,24},{16,0},{24,8},{1,17},{9,25},{17,1},{25,9},{2,18},{10... | collective-permute-start | bytes 1843208 | tf_op jit(solution)/shard_map/ppermute | solution.py:510
  78.0 28.1 %collective-permute-start.1 = (bf16[512,768]{1,0:T(8,128)(2,1)}, bf16[512,768]{1,0:T(8,128)(2,1)}, u32[]{:S(2)}, u32[]{:S(2)}) collective-permute-start(bf16[512,768]{1,0:T(8,128)(2,1)} %get-tuple-element.45), channel_id=1, source_target_pairs={{16,0},{24,8},{17,1},{25,9},{18,2},{26,10},{19,3},{27,11},{20,4},{... | collective-permute-start | bytes 2359304 | tf_op jit(solution)/shard_map/ppermute | solution.py:516
  84.8 34.5 %collective-permute-start.23 = (bf16[160,1920]{1,0:T(8,128)(2,1)}, bf16[160,1920]{1,0:T(8,128)(2,1)}, u32[]{:S(2)}, u32[]{:S(2)}) collective-permute-start(bf16[160,1920]{1,0:T(8,128)(2,1)} %get-tuple-element.55.refs_0_), channel_id=1, source_target_pairs={{0,16},{8,24},{16,0},{24,8},{1,17},{9,25},{17,1},{25,9},{2,18},{10... | collective-permute-start | bytes 1843208 | tf_op jit(solution)/shard_map/ppermute | solution.py:510
  99.0 33.4 %collective-permute-start.20 = (bf16[160,1920]{1,0:T(8,128)(2,1)}, bf16[160,1920]{1,0:T(8,128)(2,1)}, u32[]{:S(2)}, u32[]{:S(2)}) collective-permute-start(bf16[160,1920]{1,0:T(8,128)(2,1)} %get-tuple-element.68.refs_0_), channel_id=1, source_target_pairs={{0,16},{8,24},{16,0},{24,8},{1,17},{9,25},{17,1},{25,9},{2,18},{10... | collective-permute-start | bytes 1843208 | tf_op jit(solution)/shard_map/ppermute | solution.py:510
  111.7 28.2 %collective-permute-start.18 = (bf16[400,512]{1,0:T(8,128)(2,1)}, bf16[400,512]{1,0:T(8,128)(2,1)}, u32[]{:S(2)}, u32[]{:S(2)}) collective-permute-start(bf16[400,512]{1,0:T(8,128)(2,1)} %get-tuple-element.73), channel_id=1, source_target_pairs={{0,16},{8,24},{1,17},{9,25},{2,18},{10,26},{3,19},{11,27},{4,20},{... | collective-permute-start | bytes 1228808 | tf_op jit(solution)/shard_map/ppermute | solution.py:516
  113.0 42.6 %collective-permute-start.22 = (bf16[160,1920]{1,0:T(8,128)(2,1)}, bf16[160,1920]{1,0:T(8,128)(2,1)}, u32[]{:S(2)}, u32[]{:S(2)}) collective-permute-start(bf16[160,1920]{1,0:T(8,128)(2,1)} %get-tuple-element.55.refs_0_), channel_id=1, source_target_pairs={{0,8},{8,0},{16,24},{24,16},{1,9},{9,1},{17,25},{25,17},{2,10},{10... | collective-permute-start | bytes 1843208 | tf_op jit(solution)/shard_map/ppermute | solution.py:510
  119.3 36.3 %collective-permute-start.24 = (bf16[160,1920]{1,0:T(8,128)(2,1)}, bf16[160,1920]{1,0:T(8,128)(2,1)}, u32[]{:S(2)}, u32[]{:S(2)}) collective-permute-start(bf16[160,1920]{1,0:T(8,128)(2,1)} %collective-permute-done.23.refs_2_), channel_id=1, source_target_pairs={{0,8},{8,0},{16,24},{24,16},{1,9},{9,1},{17,25},{25,17},{2,10},{10... | collective-permute-start | bytes 1843208 | tf_op jit(solution)/shard_map/ppermute | solution.py:510
  122.7 37.6 %collective-permute-start.19 = (bf16[160,1920]{1,0:T(8,128)(2,1)}, bf16[160,1920]{1,0:T(8,128)(2,1)}, u32[]{:S(2)}, u32[]{:S(2)}) collective-permute-start(bf16[160,1920]{1,0:T(8,128)(2,1)} %get-tuple-element.68.refs_0_), channel_id=1, source_target_pairs={{0,8},{8,0},{16,24},{24,16},{1,9},{9,1},{17,25},{25,17},{2,10},{10... | collective-permute-start | bytes 1843208 | tf_op jit(solution)/shard_map/ppermute | solution.py:510
  132.4 27.9 %collective-permute-start.21 = (bf16[160,1920]{1,0:T(8,128)(2,1)}, bf16[160,1920]{1,0:T(8,128)(2,1)}, u32[]{:S(2)}, u32[]{:S(2)}) collective-permute-start(bf16[160,1920]{1,0:T(8,128)(2,1)} %collective-permute-done.20.refs_2_), channel_id=1, source_target_pairs={{0,8},{8,0},{16,24},{24,16},{1,9},{9,1},{17,25},{25,17},{2,10},{10... | collective-permute-start | bytes 1843208 | tf_op jit(solution)/shard_map/ppermute | solution.py:510
  139.9 13.5 %collective-permute-start.17 = (bf16[400,512]{1,0:T(8,128)(2,1)}, bf16[400,512]{1,0:T(8,128)(2,1)}, u32[]{:S(2)}, u32[]{:S(2)}) collective-permute-start(bf16[400,512]{1,0:T(8,128)(2,1)} %get-tuple-element.69), channel_id=1, source_target_pairs={{0,16},{8,24},{1,17},{9,25},{2,18},{10,26},{3,19},{11,27},{4,20},{... | collective-permute-start | bytes 1228808 | tf_op jit(solution)/shard_map/ppermute | solution.py:516

commit v6 on v5

--- a/solution.py
+++ b/solution.py
@@ -546,7 +546,7 @@
     paired = devices == 4
     heads = range(head_local)
     all_heads = attn_query.shape[1] // HD
-    moved = 2 * all_heads // 5
+    moved = all_heads // 5
     stay = all_heads - moved
     half = stay // 2 if stay % 2 == 0 else stay
     halves = range(0, stay, half)
@@ -584,10 +584,14 @@
         addends, total = sum_rows(pieces, paired)
         sums.append(addends)
         totals.append(total)
+    before = totals[-1]
+    fw_new = None
+    new_gathered = []
     found = []
-    for first in halves:
-        found.append(
-            attention_call(
+    for number in range(max(len(halves), head_local)):
+        if number < len(halves):
+            first = halves[number]
+            far_o, own_o, own_st = attention_call(
                 group_kernel,
                 half,
                 [
@@ -604,39 +608,35 @@
                 1.6,
                 most=half,
             )
-        )
-        before = after(found[-1][2], totals[-1])
-
-    fw_new = None
-    new_gathered = []
-    for head in heads:
-        new_weights, new_momentum, low = move_weights(
-            fast_weights, momentum, sums[head], head, fw_new
-        )
-        fw_new = (new_weights, new_momentum)
-        new_gathered.append(gather_rows(low, paired))
-        if head == 0:
-            attn_out = attention_call(
-                whole_kernel,
-                moved,
-                [
-                    after(attn_query, low),
-                    attn_key,
-                    attn_value,
-                    pair_key,
-                    pair_value,
-                    far_pairs,
-                    far_pairs,
-                    far_pairs_other,
-                    far_pairs_other,
-                ],
-                [stay] * 5 + [0, moved, 0, moved],
-                [stay],
-                2.2,
-                (attn_query.shape, None),
-                most=2,
-            )[0]
-            momentum = after(momentum, attn_out)
+            found.append((far_o, own_o, own_st))
+            before = own_st
+        if number < head_local:
+            new_weights, new_momentum, low = move_weights(
+                fast_weights, after(momentum, before), sums[number], number, fw_new
+            )
+            fw_new = (new_weights, new_momentum)
+            new_gathered.append(gather_rows(low, paired))
+            before = low
+    attn_out = attention_call(
+        whole_kernel,
+        moved,
+        [
+            after(attn_query, before),
+            attn_key,
+            attn_value,
+            pair_key,
+            pair_value,
+            far_pairs,
+            far_pairs,
+            far_pairs_other,
+            far_pairs_other,
+        ],
+        [stay] * 5 + [0, moved, 0, moved],
+        [stay],
+        2.2,
+        (attn_query.shape, None),
+        most=2,
+    )[0]
     returned = []
     for number, (far_o, own_o, own_st) in enumerate(found):
         if number > 0:

time: 166 us -> 164 us (0.988)
  starting transfers between devices: 27.5 us -> 25.8 us
    ppermute x21, waiting for transfers between devices: 40.4 us -> 31.9 us  [swapped(): return lax.ppermute(array, 'ctx', [(i, i ^ mask) for i in range(devices)])]
    ppermute x4, waiting for transfers between devices: 21.2 us -> 28 us  [shifted(): return lax.ppermute(array, 'ctx', pairs)]
    ppermute x21, starting transfers between devices: 20.1 us -> 18.3 us  [swapped(): return lax.ppermute(array, 'ctx', [(i, i ^ mask) for i in range(devices)])]
  transfers between devices with their start and end apart: 25 -> 25, of which waited for: 8 -> 8; matrix products, arithmetic and copies ran while one was open for 0% -> 0% of each run, Pallas kernels for 41% -> 42%
where the time goes in v6:
time: 164 us; the launch traced here: 162 us
  Pallas kernels  75.3 us (46%)
  waiting for transfers between devices  60 us (37%)
  starting transfers between devices  25.8 us (16%)
    ppermute x21, waiting for transfers between devices, swapped(): return lax.ppermute(array, 'ctx', [(i, i ^ mask) for i in range(devices)])  31.9 us
    pallas_call x6, Pallas kernels, attention_call(): pl.pallas_call(body, grid=(heads // per_step,), in_specs=in_specs, out_sp...  31.5 us
    ppermute x4, waiting for transfers between devices, shifted(): return lax.ppermute(array, 'ctx', pairs)  28 us
    ppermute x21, starting transfers between devices, swapped(): return lax.ppermute(array, 'ctx', [(i, i ^ mask) for i in range(devices)])  18.3 us
    pallas_call x2, Pallas kernels, head_grads(): pl.pallas_call(functools.partial(grads_kernel, masks, split, head), in_sp...  15.8 us
    pallas_call x2, Pallas kernels, head_query(): pl.pallas_call(lambda q_hbm, *refs: query_kernel(masks, q_hbm, head, *ref...  9.53 us
    ppermute x4, starting transfers between devices, shifted(): return lax.ppermute(array, 'ctx', pairs)  7.52 us
    pallas_call x2, Pallas kernels, move_weights(): pl.pallas_call(functools.partial(move_kernel, len(addends)), grid=(rows /...  7.38 us
  transfers between devices with their start and end apart: 25, of which 8 were waited for; matrix products, arithmetic and copies ran while one was open for 0% of the time, Pallas kernels for 42%

profile of v6, /device:TPU:7, one launch (start us, length us, event | category | flops | bytes accessed | tf_op | source)
XLA Modules:
  0.0 162.1 jit_solution(13790885705889499085)
XLA Ops:
  0.6 2.0 %round_head.2.refs_3_ = bf16[160,1920]{1,0:T(8,128)(2,1)} custom-call(f32[160,3840]{1,0:T(8,128)} %w_ref.6), custom_call_target="tpu_custom_call" | custom-call | flops 307200 | bytes 1843200 | tf_op jit(solution)/shard_map/round_head/pallas_call | solution.py:367
  2.7 0.3 collective-permute-start
  2.9 6.6 %shard_map.120 = (bf16[1024,512]{1,0:T(8,128)(2,1)}, f32[16,512]{1,0:T(8,128)}) custom-call(bf16[512,1280]{1,0:T(8,128)(2,1)} %q_ref.6, bf16[512,1280]{1,0:T(8,128)(2,1)} %k_ref.9, bf16[512,1280]{1,0:T(8,128)(2,1)} %v_ref.9), custom_call_target="tpu_custom_call" | custom-call | flops 644245120 | bytes 5242880 | tf_op jit(solution)/shard_map/pallas_call | solution.py:203
  9.5 2.0 %round_head.3.refs_3_ = bf16[160,1920]{1,0:T(8,128)(2,1)} custom-call(f32[160,3840]{1,0:T(8,128)} %w_ref.6), custom_call_target="tpu_custom_call" | custom-call | flops 307200 | bytes 1843200 | tf_op jit(solution)/shard_map/round_head/pallas_call | solution.py:367
  11.5 6.2 %collective-permute-done.refs_5_ = bf16[160,1920]{1,0:T(8,128)(2,1)} collective-permute-done((bf16[160,1920]{1,0:T(8,128)(2,1)}, bf16[160,1920]{1,0:T(8,128)(2,1)}, u32[]{:S(2)}, u32[]{:S(2)}) %collective-permute-start) | collective-permute-done | bytes 614432 | tf_op jit(solution)/shard_map/ppermute | solution.py:510
  17.7 0.3 collective-permute-start.5
  18.0 1.8 %collective-permute-start.2 = (bf16[160,1920]{1,0:T(8,128)(2,1)}, bf16[160,1920]{1,0:T(8,128)(2,1)}, u32[]{:S(2)}, u32[]{:S(2)}) collective-permute-start(bf16[160,1920]{1,0:T(8,128)(2,1)} %round_head.2.refs_3_), channel_id=1, source_target_pairs={{0,8},{8,0},{16,24},{24,16},{1,9},{9,1},{17,25},{25,17},{2,10},{10... | collective-permute-start | bytes 1843208 | tf_op jit(solution)/shard_map/ppermute | solution.py:510
  19.8 0.0 collective-permute-start.3
  19.8 0.5 collective-permute-start.4
  20.3 11.6 %collective-permute-done.5.refs_5_ = bf16[160,1920]{1,0:T(8,128)(2,1)} collective-permute-done((bf16[160,1920]{1,0:T(8,128)(2,1)}, bf16[160,1920]{1,0:T(8,128)(2,1)}, u32[]{:S(2)}, u32[]{:S(2)}) %collective-permute-start.5) | collective-permute-done | bytes 614432 | tf_op jit(solution)/shard_map/ppermute | solution.py:510
  31.9 2.4 %collective-permute-start.6 = (bf16[160,1920]{1,0:T(8,128)(2,1)}, bf16[160,1920]{1,0:T(8,128)(2,1)}, u32[]{:S(2)}, u32[]{:S(2)}) collective-permute-start(bf16[160,1920]{1,0:T(8,128)(2,1)} %collective-permute-done.5.refs_5_), channel_id=1, source_target_pairs={{0,8},{8,0},{16,24},{24,16},{1,9},{9,1},{17,25},{25,17},{2,10},{10... | collective-permute-start | bytes 1843208 | tf_op jit(solution)/shard_map/ppermute | solution.py:510
  34.3 0.0 collective-permute-start.8
  34.3 0.0 collective-permute-done.2.refs_4_
  34.3 0.5 collective-permute-start.9
  34.8 2.9 %pack_travellers.1 = (bf16[512,1024]{1,0:T(8,128)(2,1)}, bf16[512,512]{1,0:T(8,128)(2,1)}) custom-call(bf16[512,1280]{1,0:T(8,128)(2,1)} %q_ref.6, bf16[512,1280]{1,0:T(8,128)(2,1)} %k_ref.9, bf16[512,1280]{1,0:T(8,128)(2,1)} %v_ref.9), custom_call_target="tpu_custom_call" | custom-call | bytes 5242880 | tf_op jit(solution)/shard_map/pack_travellers/pallas_call | solution.py:395
  37.7 0.0 collective-permute-done.3.refs_6_
  37.7 3.2 %collective-permute-start.1 = (bf16[512,1024]{1,0:T(8,128)(2,1)}, bf16[512,1024]{1,0:T(8,128)(2,1)}, u32[]{:S(2)}, u32[]{:S(2)}) collective-permute-start(bf16[512,1024]{1,0:T(8,128)(2,1)} %get-tuple-element.47), channel_id=1, source_target_pairs={{16,0},{24,8},{17,1},{25,9},{18,2},{26,10},{19,3},{27,11},{20,4},{... | collective-permute-start | bytes 3145736 | tf_op jit(solution)/shard_map/ppermute | solution.py:516
  40.9 7.9 %head_grads.2 = (bf16[160,1920]{1,0:T(8,128)(2,1)}, bf16[160,1920]{1,0:T(8,128)(2,1)}, bf16[160,1920]{1,0:T(8,128)(2,1)}, f32[160,1920]{1,0:T(8,128)}) custom-call(f32[2,512]{1,0:T(2,128)} %bitcast.1, bf16[512,1280]{1,0:T(8,128)(2,1)} %refs_1_.1, bf16[512,1280]{1,0:T(8,128)(2,1)} %refs_2_.3, bf16[160,1920]{1,0:T(8,128)(2,1)} %round_head.2.refs_3_, ...), custom_call_target="tpu_custom_call" | custom-call | flops 2516582400 | bytes 8000000 | tf_op jit(solution)/shard_map/head_grads/pallas_call | solution.py:313
  48.9 0.0 collective-permute-done.4.refs_4_
  48.9 0.4 collective-permute-start.11
  49.2 0.0 collective-permute-done.6.refs_6_
  49.2 7.9 %head_grads.3 = (bf16[160,1920]{1,0:T(8,128)(2,1)}, bf16[160,1920]{1,0:T(8,128)(2,1)}, bf16[160,1920]{1,0:T(8,128)(2,1)}, f32[160,1920]{1,0:T(8,128)}) custom-call(f32[2,512]{1,0:T(2,128)} %bitcast.2, bf16[512,1280]{1,0:T(8,128)(2,1)} %refs_1_.1, bf16[512,1280]{1,0:T(8,128)(2,1)} %refs_2_.3, bf16[160,1920]{1,0:T(8,128)(2,1)} %round_head.3.refs_3_, ...), custom_call_target="tpu_custom_call" | custom-call | flops 2516582400 | bytes 8000000 | tf_op jit(solution)/shard_map/head_grads/pallas_call | solution.py:313
  57.2 0.3 collective-permute-start.7
  57.4 0.0 collective-permute-done.11.right_ref
  57.4 0.3 collective-permute-start.10
  57.7 2.0 %add_rows.3 = bf16[160,1920]{1,0:T(8,128)(2,1)} custom-call(bf16[160,1920]{1,0:T(8,128)(2,1)} %get-tuple-element.59.left_ref, bf16[160,1920]{1,0:T(8,128)(2,1)} %collective-permute-done.11.right_ref), custom_call_target="tpu_custom_call" | custom-call | flops 307200 | bytes 1843200 | tf_op jit(solution)/shard_map/add_rows/pallas_call | solution.py:344
  59.8 0.0 collective-permute-done.7.right_ref
  59.8 0.0 collective-permute-start.12
  59.8 2.1 %add_rows.2 = bf16[160,1920]{1,0:T(8,128)(2,1)} custom-call(bf16[160,1920]{1,0:T(8,128)(2,1)} %get-tuple-element.52.left_ref, bf16[160,1920]{1,0:T(8,128)(2,1)} %collective-permute-done.7.right_ref), custom_call_target="tpu_custom_call" | custom-call | flops 307200 | bytes 1843200 | tf_op jit(solution)/shard_map/add_rows/pallas_call | solution.py:344
  61.8 0.0 collective-permute-done.8.pk_ref
  61.9 0.2 collective-permute-start.13
  62.1 0.0 collective-permute-done.9.pv_ref
  62.1 1.7 %collective-permute-start.14 = (bf16[160,1920]{1,0:T(8,128)(2,1)}, bf16[160,1920]{1,0:T(8,128)(2,1)}, u32[]{:S(2)}, u32[]{:S(2)}) collective-permute-start(bf16[160,1920]{1,0:T(8,128)(2,1)} %add_rows.2), channel_id=1, source_target_pairs={{0,16},{8,24},{16,0},{24,8},{1,17},{9,25},{17,1},{25,9},{2,18},{10... | collective-permute-start | bytes 1843208 | tf_op jit(solution)/shard_map/ppermute | solution.py:510
  63.8 0.0 collective-permute-done.1.far_ref
  63.8 1.5 collective-permute-start.17
  65.3 6.9 %shard_map.121 = (bf16[544,512]{1,0:T(8,128)(2,1)}, bf16[512,512]{1,0:T(8,128)(2,1)}, f32[8,512]{1,0:T(8,128)}) custom-call(bf16[512,1280]{1,0:T(8,128)(2,1)} %q_ref.6, bf16[512,1024]{1,0:T(8,128)(2,1)} %collective-permute-done.1.far_ref, bf16[512,1280]{1,0:T(8,128)(2,1)} %k_ref.9, bf16[512,1280]{1,0:T(8,128)(2,1)} %v_ref.9, ...), custom_call_target="tpu_custom_call" | custom-call | flops 858993472 | bytes 5767168 | tf_op jit(solution)/shard_map/pallas_call | solution.py:203
  72.2 0.0 collective-permute-done.10.refs_1_
  72.2 3.7 %collective-permute-done.12.refs_2_ = bf16[160,1920]{1,0:T(8,128)(2,1)} collective-permute-done((bf16[160,1920]{1,0:T(8,128)(2,1)}, bf16[160,1920]{1,0:T(8,128)(2,1)}, u32[]{:S(2)}, u32[]{:S(2)}) %collective-permute-start.12) | collective-permute-done | bytes 614432 | tf_op jit(solution)/shard_map/ppermute | solution.py:510
  75.9 3.7 %move_weights.2 = (f32[160,3840]{1,0:T(8,128)}, f32[160,3840]{1,0:T(8,128)}, bf16[160,1920]{1,0:T(8,128)(2,1)}) custom-call(f32[160,3840]{1,0:T(8,128)} %w_ref.6, f32[160,3840]{1,0:T(8,128)} %m_ref.1, f32[160,1920]{1,0:T(8,128)} %get-tuple-element.49.refs_0_, bf16[160,1920]{1,0:T(8,128)(2,1)} %collective-permute-done.10.refs_1_, ...), custom_call_target="tpu_custom_call" | custom-call | flops 6144000 | bytes 7987200 | tf_op jit(solution)/shard_map/move_weights/pallas_call | solution.py:439
  79.5 2.2 %collective-permute-start.23 = (bf16[160,1920]{1,0:T(8,128)(2,1)}, bf16[160,1920]{1,0:T(8,128)(2,1)}, u32[]{:S(2)}, u32[]{:S(2)}) collective-permute-start(bf16[160,1920]{1,0:T(8,128)(2,1)} %get-tuple-element.61.refs_0_), channel_id=1, source_target_pairs={{0,16},{8,24},{16,0},{24,8},{1,17},{9,25},{17,1},{25,9},{2,18},{10... | collective-permute-start | bytes 1843208 | tf_op jit(solution)/shard_map/ppermute | solution.py:510
  81.7 6.9 %shard_map.122 = (bf16[544,512]{1,0:T(8,128)(2,1)}, bf16[512,512]{1,0:T(8,128)(2,1)}, f32[8,512]{1,0:T(8,128)}) custom-call(bf16[512,1280]{1,0:T(8,128)(2,1)} %q_ref.6, bf16[512,1024]{1,0:T(8,128)(2,1)} %collective-permute-done.1.far_ref, bf16[512,1280]{1,0:T(8,128)(2,1)} %k_ref.9, bf16[512,1280]{1,0:T(8,128)(2,1)} %v_ref.9, ...), custom_call_target="tpu_custom_call" | custom-call | flops 858993472 | bytes 5767168 | tf_op jit(solution)/shard_map/pallas_call | solution.py:203
  88.7 0.4 collective-permute-done.14.refs_2_
  89.0 3.7 %move_weights.3 = (f32[160,3840]{1,0:T(8,128)}, f32[160,3840]{1,0:T(8,128)}, bf16[160,1920]{1,0:T(8,128)(2,1)}) custom-call(f32[160,3840]{1,0:T(8,128)} %w_ref.6, f32[160,3840]{1,0:T(8,128)} %m_ref.1, f32[160,1920]{1,0:T(8,128)} %get-tuple-element.67.refs_0_, ...), custom_call_target="tpu_custom_call", output_to_operand_aliasing={{0}: (5, {}), {1}: (6, {})} | custom-call | flops 6144000 | bytes 7987200 | tf_op jit(solution)/shard_map/move_weights/pallas_call | solution.py:439
  92.7 2.2 %collective-permute-start.20 = (bf16[160,1920]{1,0:T(8,128)(2,1)}, bf16[160,1920]{1,0:T(8,128)(2,1)}, u32[]{:S(2)}, u32[]{:S(2)}) collective-permute-start(bf16[160,1920]{1,0:T(8,128)(2,1)} %get-tuple-element.71.refs_0_), channel_id=1, source_target_pairs={{0,16},{8,24},{16,0},{24,8},{1,17},{9,25},{17,1},{25,9},{2,18},{10... | collective-permute-start | bytes 1843208 | tf_op jit(solution)/shard_map/ppermute | solution.py:510
  94.9 4.8 %collective-permute-done.17.fk_ref.fv_ref = bf16[512,512]{1,0:T(8,128)(2,1)} collective-permute-done((bf16[512,512]{1,0:T(8,128)(2,1)}, bf16[512,512]{1,0:T(8,128)(2,1)}, u32[]{:S(2)}, u32[]{:S(2)}) %collective-permute-start.17) | collective-permute-done | bytes 524320 | tf_op jit(solution)/shard_map/ppermute | solution.py:516
  99.7 1.7 %collective-permute-start.18 = (bf16[512,512]{1,0:T(8,128)(2,1)}, bf16[512,512]{1,0:T(8,128)(2,1)}, u32[]{:S(2)}, u32[]{:S(2)}) collective-permute-start(bf16[512,512]{1,0:T(8,128)(2,1)} %collective-permute-done.17.fk_ref.fv_ref), channel_id=1, source_target_pairs={{0,8},{8,0},{16,24},{24,16},{1,9},{9,1},{17,25},{25,17},{2,10},{10... | collective-permute-start | bytes 1572872 | tf_op jit(solution)/shard_map/ppermute | solution.py:510
  101.4 1.3 collective-permute-start.16
  102.7 0.1 collective-permute-start.22
  102.8 10.1 %collective-permute-done.23.refs_2_ = bf16[160,1920]{1,0:T(8,128)(2,1)} collective-permute-done((bf16[160,1920]{1,0:T(8,128)(2,1)}, bf16[160,1920]{1,0:T(8,128)(2,1)}, u32[]{:S(2)}, u32[]{:S(2)}) %collective-permute-start.23) | collective-permute-done | bytes 614432 | tf_op jit(solution)/shard_map/ppermute | solution.py:510
  112.9 1.7 %collective-permute-start.24 = (bf16[160,1920]{1,0:T(8,128)(2,1)}, bf16[160,1920]{1,0:T(8,128)(2,1)}, u32[]{:S(2)}, u32[]{:S(2)}) collective-permute-start(bf16[160,1920]{1,0:T(8,128)(2,1)} %collective-permute-done.23.refs_2_), channel_id=1, source_target_pairs={{0,8},{8,0},{16,24},{24,16},{1,9},{9,1},{17,25},{25,17},{2,10},{10... | collective-permute-start | bytes 1843208 | tf_op jit(solution)/shard_map/ppermute | solution.py:510
  114.6 0.0 collective-permute-done.18.fpk_ref.fpv_ref
  114.6 1.5 collective-permute-start.15
  116.1 21.8 %collective-permute-done.16.refs_2_ = bf16[544,512]{1,0:T(8,128)(2,1)} collective-permute-done((bf16[544,512]{1,0:T(8,128)(2,1)}, bf16[544,512]{1,0:T(8,128)(2,1)}, u32[]{:S(2)}, u32[]{:S(2)}) %collective-permute-start.16) | collective-permute-done | bytes 557088 | tf_op jit(solution)/shard_map/ppermute | solution.py:516
  138.0 1.7 %collective-permute-start.19 = (bf16[160,1920]{1,0:T(8,128)(2,1)}, bf16[160,1920]{1,0:T(8,128)(2,1)}, u32[]{:S(2)}, u32[]{:S(2)}) collective-permute-start(bf16[160,1920]{1,0:T(8,128)(2,1)} %get-tuple-element.71.refs_0_), channel_id=1, source_target_pairs={{0,8},{8,0},{16,24},{24,16},{1,9},{9,1},{17,25},{25,17},{2,10},{10... | collective-permute-start | bytes 1843208 | tf_op jit(solution)/shard_map/ppermute | solution.py:510
  139.7 0.0 collective-permute-start.21
  139.7 6.3 %shard_map.123.refs_3_ = bf16[512,1280]{1,0:T(8,128)(2,1)} custom-call(bf16[512,1280]{1,0:T(8,128)(2,1)} %q_ref.6, bf16[512,1280]{1,0:T(8,128)(2,1)} %k_ref.9, bf16[512,1280]{1,0:T(8,128)(2,1)} %v_ref.9, bf16[512,1280]{1,0:T(8,128)(2,1)} %collective-permute-done.8.pk_ref, bf16[512,1280]{1,0:T(8,128)(2,1)} %collective-permute-done.9.pv_ref, ...), custom_call_target="tpu_custom_call" | custom-call | flops 590558016 | bytes 2621440 | tf_op jit(solution)/shard_map/pallas_call | solution.py:203
  146.0 2.4 %shard_map.124.refs_3_ = bf16[512,1280]{1,0:T(8,128)(2,1)} custom-call(bf16[512,512]{1,0:T(8,128)(2,1)} %get-tuple-element.73.refs_0_, f32[8,512]{1,0:T(8,128)} %get-tuple-element.56.refs_1_, bf16[544,512]{1,0:T(8,128)(2,1)} %collective-permute-done.16.refs_2_, bf16[512,1280]{1,0:T(8,128)(2,1)} %shard_map.123.refs_3_), custom_call_target="tpu_custom_call", output_to_operand_aliasing={{}: (3, {})} | custom-call | flops 5368709 | bytes 2097152 | tf_op jit(solution)/shard_map/pallas_call | solution.py:203
  148.4 1.5 collective-permute-done.15.refs_2_
  149.9 2.4 %shard_map.125 = bf16[512,1280]{1,0:T(8,128)(2,1)} custom-call(bf16[512,512]{1,0:T(8,128)(2,1)} %get-tuple-element.63.refs_0_, f32[8,512]{1,0:T(8,128)} %get-tuple-element.64.refs_1_, bf16[544,512]{1,0:T(8,128)(2,1)} %collective-permute-done.15.refs_2_, bf16[512,1280]{1,0:T(8,128)(2,1)} %shard_map.124.refs_3_), custom_call_target="tpu_custom_call", output_to_operand_aliasing={{}: (3, {})} | custom-call | flops 5368709 | bytes 2097152 | tf_op jit(solution)/shard_map/pallas_call | solution.py:203
  152.3 0.0 collective-permute-done.22.refs_1_
  152.3 0.0 collective-permute-done.24.refs_3_
  152.3 4.8 %head_query.2.refs_4_ = bf16[512,1280]{1,0:T(8,128)(2,1)} custom-call(bf16[512,1280]{1,0:T(8,128)(2,1)} %q_hbm.3, bf16[160,1920]{1,0:T(8,128)(2,1)} %get-tuple-element.61.refs_0_, bf16[160,1920]{1,0:T(8,128)(2,1)} %collective-permute-done.22.refs_1_, bf16[160,1920]{1,0:T(8,128)(2,1)} %collective-permute-done.23.refs_2_, ...), custom_call_target="tpu_custom_call" | custom-call | flops 1258291200 | bytes 4000000 | tf_op jit(solution)/shard_map/head_query/pallas_call | solution.py:490
  157.1 0.0 collective-permute-done.21.refs_3_
  157.1 4.8 %head_query.3 = bf16[512,1280]{1,0:T(8,128)(2,1)} custom-call(bf16[512,1280]{1,0:T(8,128)(2,1)} %q_hbm.3, bf16[160,1920]{1,0:T(8,128)(2,1)} %get-tuple-element.71.refs_0_, bf16[160,1920]{1,0:T(8,128)(2,1)} %collective-permute-done.19.refs_1_, bf16[160,1920]{1,0:T(8,128)(2,1)} %collective-permute-done.20.refs_2_, ...), custom_call_target="tpu_custom_call", output_to_operand_aliasing={{}: (5, {})} | custom-call | flops 1258291200 | bytes 4000000 | tf_op jit(solution)/shard_map/head_query/pallas_call | solution.py:490
  (3 shorter events, 0.0 us)
Async XLA Ops:
  2.7 15.1 %collective-permute-start = (bf16[160,1920]{1,0:T(8,128)(2,1)}, bf16[160,1920]{1,0:T(8,128)(2,1)}, u32[]{:S(2)}, u32[]{:S(2)}) collective-permute-start(bf16[160,1920]{1,0:T(8,128)(2,1)} %round_head.2.refs_3_), channel_id=1, source_target_pairs={{0,16},{8,24},{16,0},{24,8},{1,17},{9,25},{17,1},{25,9},{2,18},{10... | collective-permute-start | bytes 1843208 | tf_op jit(solution)/shard_map/ppermute | solution.py:510
  17.7 14.2 %collective-permute-start.5 = (bf16[160,1920]{1,0:T(8,128)(2,1)}, bf16[160,1920]{1,0:T(8,128)(2,1)}, u32[]{:S(2)}, u32[]{:S(2)}) collective-permute-start(bf16[160,1920]{1,0:T(8,128)(2,1)} %round_head.3.refs_3_), channel_id=1, source_target_pairs={{0,16},{8,24},{16,0},{24,8},{1,17},{9,25},{17,1},{25,9},{2,18},{10... | collective-permute-start | bytes 1843208 | tf_op jit(solution)/shard_map/ppermute | solution.py:510
  18.0 16.3 %collective-permute-start.2 = (bf16[160,1920]{1,0:T(8,128)(2,1)}, bf16[160,1920]{1,0:T(8,128)(2,1)}, u32[]{:S(2)}, u32[]{:S(2)}) collective-permute-start(bf16[160,1920]{1,0:T(8,128)(2,1)} %round_head.2.refs_3_), channel_id=1, source_target_pairs={{0,8},{8,0},{16,24},{24,16},{1,9},{9,1},{17,25},{25,17},{2,10},{10... | collective-permute-start | bytes 1843208 | tf_op jit(solution)/shard_map/ppermute | solution.py:510
  19.8 18.0 %collective-permute-start.3 = (bf16[160,1920]{1,0:T(8,128)(2,1)}, bf16[160,1920]{1,0:T(8,128)(2,1)}, u32[]{:S(2)}, u32[]{:S(2)}) collective-permute-start(bf16[160,1920]{1,0:T(8,128)(2,1)} %collective-permute-done.refs_5_), channel_id=1, source_target_pairs={{0,8},{8,0},{16,24},{24,16},{1,9},{9,1},{17,25},{25,17},{2,10},{10... | collective-permute-start | bytes 1843208 | tf_op jit(solution)/shard_map/ppermute | solution.py:510
  19.8 29.1 %collective-permute-start.4 = (bf16[160,1920]{1,0:T(8,128)(2,1)}, bf16[160,1920]{1,0:T(8,128)(2,1)}, u32[]{:S(2)}, u32[]{:S(2)}) collective-permute-start(bf16[160,1920]{1,0:T(8,128)(2,1)} %round_head.3.refs_3_), channel_id=1, source_target_pairs={{0,8},{8,0},{16,24},{24,16},{1,9},{9,1},{17,25},{25,17},{2,10},{10... | collective-permute-start | bytes 1843208 | tf_op jit(solution)/shard_map/ppermute | solution.py:510
  31.9 17.3 %collective-permute-start.6 = (bf16[160,1920]{1,0:T(8,128)(2,1)}, bf16[160,1920]{1,0:T(8,128)(2,1)}, u32[]{:S(2)}, u32[]{:S(2)}) collective-permute-start(bf16[160,1920]{1,0:T(8,128)(2,1)} %collective-permute-done.5.refs_5_), channel_id=1, source_target_pairs={{0,8},{8,0},{16,24},{24,16},{1,9},{9,1},{17,25},{25,17},{2,10},{10... | collective-permute-start | bytes 1843208 | tf_op jit(solution)/shard_map/ppermute | solution.py:510
  34.3 27.6 %collective-permute-start.8 = (bf16[512,1280]{1,0:T(8,128)(2,1)}, bf16[512,1280]{1,0:T(8,128)(2,1)}, u32[]{:S(2)}, u32[]{:S(2)}) collective-permute-start(bf16[512,1280]{1,0:T(8,128)(2,1)} %k_ref.9), channel_id=1, source_target_pairs={{0,8},{8,0},{16,24},{24,16},{1,9},{9,1},{17,25},{25,17},{2,10},{10... | collective-permute-start | bytes 3932168 | tf_op jit(solution)/shard_map/ppermute | solution.py:510
  34.3 27.8 %collective-permute-start.9 = (bf16[512,1280]{1,0:T(8,128)(2,1)}, bf16[512,1280]{1,0:T(8,128)(2,1)}, u32[]{:S(2)}, u32[]{:S(2)}) collective-permute-start(bf16[512,1280]{1,0:T(8,128)(2,1)} %v_ref.9), channel_id=1, source_target_pairs={{0,8},{8,0},{16,24},{24,16},{1,9},{9,1},{17,25},{25,17},{2,10},{10... | collective-permute-start | bytes 3932168 | tf_op jit(solution)/shard_map/ppermute | solution.py:510
  37.7 26.1 %collective-permute-start.1 = (bf16[512,1024]{1,0:T(8,128)(2,1)}, bf16[512,1024]{1,0:T(8,128)(2,1)}, u32[]{:S(2)}, u32[]{:S(2)}) collective-permute-start(bf16[512,1024]{1,0:T(8,128)(2,1)} %get-tuple-element.47), channel_id=1, source_target_pairs={{16,0},{24,8},{17,1},{25,9},{18,2},{26,10},{19,3},{27,11},{20,4},{... | collective-permute-start | bytes 3145736 | tf_op jit(solution)/shard_map/ppermute | solution.py:516
  48.9 8.6 %collective-permute-start.11 = (bf16[160,1920]{1,0:T(8,128)(2,1)}, bf16[160,1920]{1,0:T(8,128)(2,1)}, u32[]{:S(2)}, u32[]{:S(2)}) collective-permute-start(bf16[160,1920]{1,0:T(8,128)(2,1)} %get-tuple-element.60), channel_id=1, source_target_pairs={{0,8},{8,0},{16,24},{24,16},{1,9},{9,1},{17,25},{25,17},{2,10},{10... | collective-permute-start | bytes 1843208 | tf_op jit(solution)/shard_map/ppermute | solution.py:510
  57.2 2.6 %collective-permute-start.7 = (bf16[160,1920]{1,0:T(8,128)(2,1)}, bf16[160,1920]{1,0:T(8,128)(2,1)}, u32[]{:S(2)}, u32[]{:S(2)}) collective-permute-start(bf16[160,1920]{1,0:T(8,128)(2,1)} %get-tuple-element.53), channel_id=1, source_target_pairs={{0,8},{8,0},{16,24},{24,16},{1,9},{9,1},{17,25},{25,17},{2,10},{10... | collective-permute-start | bytes 1843208 | tf_op jit(solution)/shard_map/ppermute | solution.py:510
  57.4 14.7 %collective-permute-start.10 = (bf16[160,1920]{1,0:T(8,128)(2,1)}, bf16[160,1920]{1,0:T(8,128)(2,1)}, u32[]{:S(2)}, u32[]{:S(2)}) collective-permute-start(bf16[160,1920]{1,0:T(8,128)(2,1)} %get-tuple-element.58), channel_id=1, source_target_pairs={{0,8},{8,0},{16,24},{24,16},{1,9},{9,1},{17,25},{25,17},{2,10},{10... | collective-permute-start | bytes 1843208 | tf_op jit(solution)/shard_map/ppermute | solution.py:510
  59.8 16.1 %collective-permute-start.12 = (bf16[160,1920]{1,0:T(8,128)(2,1)}, bf16[160,1920]{1,0:T(8,128)(2,1)}, u32[]{:S(2)}, u32[]{:S(2)}) collective-permute-start(bf16[160,1920]{1,0:T(8,128)(2,1)} %add_rows.3), channel_id=1, source_target_pairs={{0,16},{8,24},{16,0},{24,8},{1,17},{9,25},{17,1},{25,9},{2,18},{10... | collective-permute-start | bytes 1843208 | tf_op jit(solution)/shard_map/ppermute | solution.py:510
  61.9 26.8 %collective-permute-start.13 = (bf16[160,1920]{1,0:T(8,128)(2,1)}, bf16[160,1920]{1,0:T(8,128)(2,1)}, u32[]{:S(2)}, u32[]{:S(2)}) collective-permute-start(bf16[160,1920]{1,0:T(8,128)(2,1)} %get-tuple-element.68), channel_id=1, source_target_pairs={{0,8},{8,0},{16,24},{24,16},{1,9},{9,1},{17,25},{25,17},{2,10},{10... | collective-permute-start | bytes 1843208 | tf_op jit(solution)/shard_map/ppermute | solution.py:510
  62.1 27.0 %collective-permute-start.14 = (bf16[160,1920]{1,0:T(8,128)(2,1)}, bf16[160,1920]{1,0:T(8,128)(2,1)}, u32[]{:S(2)}, u32[]{:S(2)}) collective-permute-start(bf16[160,1920]{1,0:T(8,128)(2,1)} %add_rows.2), channel_id=1, source_target_pairs={{0,16},{8,24},{16,0},{24,8},{1,17},{9,25},{17,1},{25,9},{2,18},{10... | collective-permute-start | bytes 1843208 | tf_op jit(solution)/shard_map/ppermute | solution.py:510
  63.8 35.9 %collective-permute-start.17 = (bf16[512,512]{1,0:T(8,128)(2,1)}, bf16[512,512]{1,0:T(8,128)(2,1)}, u32[]{:S(2)}, u32[]{:S(2)}) collective-permute-start(bf16[512,512]{1,0:T(8,128)(2,1)} %get-tuple-element.77), channel_id=1, source_target_pairs={{0,16},{8,24},{1,17},{9,25},{2,18},{10,26},{3,19},{11,27},{4,20},{... | collective-permute-start | bytes 1572872 | tf_op jit(solution)/shard_map/ppermute | solution.py:516
  79.5 33.3 %collective-permute-start.23 = (bf16[160,1920]{1,0:T(8,128)(2,1)}, bf16[160,1920]{1,0:T(8,128)(2,1)}, u32[]{:S(2)}, u32[]{:S(2)}) collective-permute-start(bf16[160,1920]{1,0:T(8,128)(2,1)} %get-tuple-element.61.refs_0_), channel_id=1, source_target_pairs={{0,16},{8,24},{16,0},{24,8},{1,17},{9,25},{17,1},{25,9},{2,18},{10... | collective-permute-start | bytes 1843208 | tf_op jit(solution)/shard_map/ppermute | solution.py:510
  92.7 47.0 %collective-permute-start.20 = (bf16[160,1920]{1,0:T(8,128)(2,1)}, bf16[160,1920]{1,0:T(8,128)(2,1)}, u32[]{:S(2)}, u32[]{:S(2)}) collective-permute-start(bf16[160,1920]{1,0:T(8,128)(2,1)} %get-tuple-element.71.refs_0_), channel_id=1, source_target_pairs={{0,16},{8,24},{16,0},{24,8},{1,17},{9,25},{17,1},{25,9},{2,18},{10... | collective-permute-start | bytes 1843208 | tf_op jit(solution)/shard_map/ppermute | solution.py:510
  99.7 14.9 %collective-permute-start.18 = (bf16[512,512]{1,0:T(8,128)(2,1)}, bf16[512,512]{1,0:T(8,128)(2,1)}, u32[]{:S(2)}, u32[]{:S(2)}) collective-permute-start(bf16[512,512]{1,0:T(8,128)(2,1)} %collective-permute-done.17.fk_ref.fv_ref), channel_id=1, source_target_pairs={{0,8},{8,0},{16,24},{24,16},{1,9},{9,1},{17,25},{25,17},{2,10},{10... | collective-permute-start | bytes 1572872 | tf_op jit(solution)/shard_map/ppermute | solution.py:510
  101.4 36.5 %collective-permute-start.16 = (bf16[544,512]{1,0:T(8,128)(2,1)}, bf16[544,512]{1,0:T(8,128)(2,1)}, u32[]{:S(2)}, u32[]{:S(2)}) collective-permute-start(bf16[544,512]{1,0:T(8,128)(2,1)} %get-tuple-element.74), channel_id=1, source_target_pairs={{0,16},{8,24},{1,17},{9,25},{2,18},{10,26},{3,19},{11,27},{4,20},{... | collective-permute-start | bytes 1671176 | tf_op jit(solution)/shard_map/ppermute | solution.py:516
  102.7 49.6 %collective-permute-start.22 = (bf16[160,1920]{1,0:T(8,128)(2,1)}, bf16[160,1920]{1,0:T(8,128)(2,1)}, u32[]{:S(2)}, u32[]{:S(2)}) collective-permute-start(bf16[160,1920]{1,0:T(8,128)(2,1)} %get-tuple-element.61.refs_0_), channel_id=1, source_target_pairs={{0,8},{8,0},{16,24},{24,16},{1,9},{9,1},{17,25},{25,17},{2,10},{10... | collective-permute-start | bytes 1843208 | tf_op jit(solution)/shard_map/ppermute | solution.py:510
  112.9 39.5 %collective-permute-start.24 = (bf16[160,1920]{1,0:T(8,128)(2,1)}, bf16[160,1920]{1,0:T(8,128)(2,1)}, u32[]{:S(2)}, u32[]{:S(2)}) collective-permute-start(bf16[160,1920]{1,0:T(8,128)(2,1)} %collective-permute-done.23.refs_2_), channel_id=1, source_target_pairs={{0,8},{8,0},{16,24},{24,16},{1,9},{9,1},{17,25},{25,17},{2,10},{10... | collective-permute-start | bytes 1843208 | tf_op jit(solution)/shard_map/ppermute | solution.py:510
  114.6 35.3 %collective-permute-start.15 = (bf16[544,512]{1,0:T(8,128)(2,1)}, bf16[544,512]{1,0:T(8,128)(2,1)}, u32[]{:S(2)}, u32[]{:S(2)}) collective-permute-start(bf16[544,512]{1,0:T(8,128)(2,1)} %get-tuple-element.72), channel_id=1, source_target_pairs={{0,16},{8,24},{1,17},{9,25},{2,18},{10,26},{3,19},{11,27},{4,20},{... | collective-permute-start | bytes 1671176 | tf_op jit(solution)/shard_map/ppermute | solution.py:516
  138.0 19.1 %collective-permute-start.19 = (bf16[160,1920]{1,0:T(8,128)(2,1)}, bf16[160,1920]{1,0:T(8,128)(2,1)}, u32[]{:S(2)}, u32[]{:S(2)}) collective-permute-start(bf16[160,1920]{1,0:T(8,128)(2,1)} %get-tuple-element.71.refs_0_), channel_id=1, source_target_pairs={{0,8},{8,0},{16,24},{24,16},{1,9},{9,1},{17,25},{25,17},{2,10},{10... | collective-permute-start | bytes 1843208 | tf_op jit(solution)/shard_map/ppermute | solution.py:510
  139.7 17.4 %collective-permute-start.21 = (bf16[160,1920]{1,0:T(8,128)(2,1)}, bf16[160,1920]{1,0:T(8,128)(2,1)}, u32[]{:S(2)}, u32[]{:S(2)}) collective-permute-start(bf16[160,1920]{1,0:T(8,128)(2,1)} %collective-permute-done.20.refs_2_), channel_id=1, source_target_pairs={{0,8},{8,0},{16,24},{24,16},{1,9},{9,1},{17,25},{25,17},{2,10},{10... | collective-permute-start | bytes 1843208 | tf_op jit(solution)/shard_map/ppermute | solution.py:510

commit v7 on v6

--- a/solution.py
+++ b/solution.py
@@ -16,7 +16,7 @@
 SPAN = 3 * FD
 INV_ROOT = FD ** (-0.5)
 EXP2_SCALE = HD ** (-0.5) * math.log2(math.e)
-LOWEST = -1e30
+LOWEST = -(2.0**100)
 F32 = jnp.float32
 BF16 = jnp.bfloat16
 ANY = pl.BlockSpec(memory_space=pltpu.HBM)
@@ -76,7 +76,7 @@
 
 
 def stat_places(per_step):
-    return 16 * pl.cdiv(5 * per_step, 16)
+    return 16 * pl.cdiv(4 * per_step, 16)
 
 
 def group_kernel(
@@ -96,10 +96,12 @@
             guest = jnp.where(leading, far, q_ref[rows, cols])
             mixed, highest, total = soft(dot(pk_ref[:, cols], guest, 1, 1), pv_ref[:, cols])
             far_top = jnp.where(leading, jnp.maximum(far_m, highest), far_m)
+            top_rows = pieces_of(far_top, 2)
+            far_top = top_rows[0] + top_rows[1]
             far_keep = scaled_to(far_m, far_top)
             far_add = jnp.where(leading, scaled_to(highest, far_top), 0.0)
             fo_ref[cols, rows] = (far_o * far_keep + mixed * far_add).astype(BF16)
-            stats += pieces_of(far_top, 3) + pieces_of(far_l * far_keep + total * far_add, 2)
+            stats += top_rows + pieces_of(far_l * far_keep + total * far_add, 2)
             own_m = st_ref[top, rows]
             own_top = jnp.where(leading, own_m, jnp.maximum(own_m, highest))
             own_keep = scaled_to(own_m, own_top)
@@ -117,9 +119,9 @@
     for g in range(per_step):
         cols = slice(g * HD, (g + 1) * HD)
         top, bottom = slice(g, g + 1), slice(per_step + g, per_step + g + 1)
-        m0, m1, m2, l0, l1 = [stats[5 * g + i : 5 * g + i + 1, :] for i in range(5)]
+        m0, m1, l0, l1 = [stats[4 * g + i : 4 * g + i + 1, :] for i in range(4)]
         own_m = st_ref[top, :]
-        far_m = jnp.where(valid, m0 + m1 + m2, LOWEST)
+        far_m = jnp.where(valid, m0 + m1, LOWEST)
         highest = jnp.maximum(own_m, far_m)
         own_keep = scaled_to(own_m, highest)
         far_keep = scaled_to(far_m, highest)
@@ -564,11 +566,14 @@
         most=half,
     )
     before = own[1]
+    lows = []
     for head in heads[1:]:
         low = round_head(after(fast_weights, before), head)
         before = low
-        gathered.append(gather_rows(after(low, started), paired))
+        lows.append(low)
     queries, pairs = pack_travellers(after(attn_query, before), attn_key, attn_value, stay)
+    for head in heads[1:]:
+        gathered.append(gather_rows(after(lows[head - 1], pairs), paired))
     far_query = shifted(after(queries, started), -2)
     far_pairs = shifted(after(pairs, started), 2)
     far_pairs_other = swapped(far_pairs, 1)

time: 164 us -> 158 us (0.963)
  waiting for transfers between devices: 60 us -> 52.8 us
  starting transfers between devices: 25.8 us -> 27.6 us
    ppermute x21, waiting for transfers between devices: 31.9 us -> 25.5 us  [swapped(): return lax.ppermute(array, 'ctx', [(i, i ^ mask) for i in range(devices)])]
    ppermute x21, starting transfers between devices: 18.3 us -> 20.1 us  [swapped(): return lax.ppermute(array, 'ctx', [(i, i ^ mask) for i in range(devices)])]
  transfers between devices with their start and end apart: 25 -> 25, of which waited for: 8 -> 8; matrix products, arithmetic and copies ran while one was open for 0% -> 0% of each run, Pallas kernels for 42% -> 44%
where the time goes in v7:
time: 158 us; the launch traced here: 157 us
  Pallas kernels  75.2 us (48%)
  waiting for transfers between devices  52.8 us (33%)
  starting transfers between devices  27.6 us (17%)
    pallas_call x6, Pallas kernels, attention_call(): pl.pallas_call(body, grid=(heads // per_step,), in_specs=in_specs, out_sp...  31.4 us
    ppermute x4, waiting for transfers between devices, shifted(): return lax.ppermute(array, 'ctx', pairs)  27.3 us
    ppermute x21, waiting for transfers between devices, swapped(): return lax.ppermute(array, 'ctx', [(i, i ^ mask) for i in range(devices)])  25.5 us
    ppermute x21, starting transfers between devices, swapped(): return lax.ppermute(array, 'ctx', [(i, i ^ mask) for i in range(devices)])  20.1 us
    pallas_call x2, Pallas kernels, head_grads(): pl.pallas_call(functools.partial(grads_kernel, masks, split, head), in_sp...  15.8 us
    pallas_call x2, Pallas kernels, head_query(): pl.pallas_call(lambda q_hbm, *refs: query_kernel(masks, q_hbm, head, *ref...  9.54 us
    ppermute x4, starting transfers between devices, shifted(): return lax.ppermute(array, 'ctx', pairs)  7.52 us
    pallas_call x2, Pallas kernels, move_weights(): pl.pallas_call(functools.partial(move_kernel, len(addends)), grid=(rows /...  7.37 us
  transfers between devices with their start and end apart: 25, of which 8 were waited for; matrix products, arithmetic and copies ran while one was open for 0% of the time, Pallas kernels for 44%

profile of v7, /device:TPU:7, one launch (start us, length us, event | category | flops | bytes accessed | tf_op | source)
XLA Modules:
  0.0 156.5 jit_solution(15946954984358319207)
XLA Ops:
  0.6 2.0 %round_head.2.refs_3_ = bf16[160,1920]{1,0:T(8,128)(2,1)} custom-call(f32[160,3840]{1,0:T(8,128)} %w_ref.6), custom_call_target="tpu_custom_call" | custom-call | flops 307200 | bytes 1843200 | tf_op jit(solution)/shard_map/round_head/pallas_call | solution.py:369
  2.7 0.3 collective-permute-start
  2.9 6.6 %shard_map.120 = (bf16[1024,512]{1,0:T(8,128)(2,1)}, f32[16,512]{1,0:T(8,128)}) custom-call(bf16[512,1280]{1,0:T(8,128)(2,1)} %q_ref.6, bf16[512,1280]{1,0:T(8,128)(2,1)} %k_ref.9, bf16[512,1280]{1,0:T(8,128)(2,1)} %v_ref.9), custom_call_target="tpu_custom_call" | custom-call | flops 644245120 | bytes 5242880 | tf_op jit(solution)/shard_map/pallas_call | solution.py:205
  9.5 2.0 %round_head.3.refs_3_ = bf16[160,1920]{1,0:T(8,128)(2,1)} custom-call(f32[160,3840]{1,0:T(8,128)} %w_ref.6), custom_call_target="tpu_custom_call" | custom-call | flops 307200 | bytes 1843200 | tf_op jit(solution)/shard_map/round_head/pallas_call | solution.py:369
  11.5 2.9 %pack_travellers.1 = (bf16[512,1024]{1,0:T(8,128)(2,1)}, bf16[512,512]{1,0:T(8,128)(2,1)}) custom-call(bf16[512,1280]{1,0:T(8,128)(2,1)} %q_ref.6, bf16[512,1280]{1,0:T(8,128)(2,1)} %k_ref.9, bf16[512,1280]{1,0:T(8,128)(2,1)} %v_ref.9), custom_call_target="tpu_custom_call" | custom-call | bytes 5242880 | tf_op jit(solution)/shard_map/pack_travellers/pallas_call | solution.py:397
  14.4 1.2 collective-permute-start.5
  15.6 1.2 collective-permute-start.2
  16.9 0.8 collective-permute-done.refs_5_
  17.7 2.7 %collective-permute-start.3 = (bf16[160,1920]{1,0:T(8,128)(2,1)}, bf16[160,1920]{1,0:T(8,128)(2,1)}, u32[]{:S(2)}, u32[]{:S(2)}) collective-permute-start(bf16[160,1920]{1,0:T(8,128)(2,1)} %collective-permute-done.refs_5_), channel_id=1, source_target_pairs={{0,8},{8,0},{16,24},{24,16},{1,9},{9,1},{17,25},{25,17},{2,10},{10... | collective-permute-start | bytes 1843208 | tf_op jit(solution)/shard_map/ppermute | solution.py:512
  20.4 0.0 collective-permute-start.4
  20.4 10.5 %collective-permute-done.5.refs_5_ = bf16[160,1920]{1,0:T(8,128)(2,1)} collective-permute-done((bf16[160,1920]{1,0:T(8,128)(2,1)}, bf16[160,1920]{1,0:T(8,128)(2,1)}, u32[]{:S(2)}, u32[]{:S(2)}) %collective-permute-start.5) | collective-permute-done | bytes 614432 | tf_op jit(solution)/shard_map/ppermute | solution.py:512
  30.9 1.5 collective-permute-start.6
  32.4 0.0 collective-permute-start.8
  32.4 0.0 collective-permute-done.2.refs_4_
  32.4 0.5 collective-permute-start.9
  32.9 0.0 collective-permute-done.3.refs_6_
  32.9 3.2 %collective-permute-start.1 = (bf16[512,1024]{1,0:T(8,128)(2,1)}, bf16[512,1024]{1,0:T(8,128)(2,1)}, u32[]{:S(2)}, u32[]{:S(2)}) collective-permute-start(bf16[512,1024]{1,0:T(8,128)(2,1)} %get-tuple-element.47), channel_id=1, source_target_pairs={{16,0},{24,8},{17,1},{25,9},{18,2},{26,10},{19,3},{27,11},{20,4},{... | collective-permute-start | bytes 3145736 | tf_op jit(solution)/shard_map/ppermute | solution.py:518
  36.1 7.9 %head_grads.2 = (bf16[160,1920]{1,0:T(8,128)(2,1)}, bf16[160,1920]{1,0:T(8,128)(2,1)}, bf16[160,1920]{1,0:T(8,128)(2,1)}, f32[160,1920]{1,0:T(8,128)}) custom-call(f32[2,512]{1,0:T(2,128)} %bitcast.1, bf16[512,1280]{1,0:T(8,128)(2,1)} %refs_1_.1, bf16[512,1280]{1,0:T(8,128)(2,1)} %refs_2_.3, bf16[160,1920]{1,0:T(8,128)(2,1)} %round_head.2.refs_3_, ...), custom_call_target="tpu_custom_call" | custom-call | flops 2516582400 | bytes 8000000 | tf_op jit(solution)/shard_map/head_grads/pallas_call | solution.py:315
  44.0 0.0 collective-permute-done.4.refs_4_
  44.1 0.4 collective-permute-start.11
  44.4 0.0 collective-permute-done.6.refs_6_
  44.4 7.9 %head_grads.3 = (bf16[160,1920]{1,0:T(8,128)(2,1)}, bf16[160,1920]{1,0:T(8,128)(2,1)}, bf16[160,1920]{1,0:T(8,128)(2,1)}, f32[160,1920]{1,0:T(8,128)}) custom-call(f32[2,512]{1,0:T(2,128)} %bitcast.2, bf16[512,1280]{1,0:T(8,128)(2,1)} %refs_1_.1, bf16[512,1280]{1,0:T(8,128)(2,1)} %refs_2_.3, bf16[160,1920]{1,0:T(8,128)(2,1)} %round_head.3.refs_3_, ...), custom_call_target="tpu_custom_call" | custom-call | flops 2516582400 | bytes 8000000 | tf_op jit(solution)/shard_map/head_grads/pallas_call | solution.py:315
  52.3 0.3 collective-permute-start.7
  52.6 0.3 collective-permute-start.10
  52.9 2.0 %add_rows.3 = bf16[160,1920]{1,0:T(8,128)(2,1)} custom-call(bf16[160,1920]{1,0:T(8,128)(2,1)} %get-tuple-element.60.left_ref, bf16[160,1920]{1,0:T(8,128)(2,1)} %collective-permute-done.11.right_ref), custom_call_target="tpu_custom_call" | custom-call | flops 307200 | bytes 1843200 | tf_op jit(solution)/shard_map/add_rows/pallas_call | solution.py:346
  55.0 0.0 collective-permute-done.7.right_ref
  55.0 2.1 %add_rows.2 = bf16[160,1920]{1,0:T(8,128)(2,1)} custom-call(bf16[160,1920]{1,0:T(8,128)(2,1)} %get-tuple-element.53.left_ref, bf16[160,1920]{1,0:T(8,128)(2,1)} %collective-permute-done.7.right_ref), custom_call_target="tpu_custom_call" | custom-call | flops 307200 | bytes 1843200 | tf_op jit(solution)/shard_map/add_rows/pallas_call | solution.py:346
  57.0 0.0 collective-permute-done.8.pk_ref
  57.1 0.2 collective-permute-start.13
  57.3 1.7 %collective-permute-start.14 = (bf16[160,1920]{1,0:T(8,128)(2,1)}, bf16[160,1920]{1,0:T(8,128)(2,1)}, u32[]{:S(2)}, u32[]{:S(2)}) collective-permute-start(bf16[160,1920]{1,0:T(8,128)(2,1)} %add_rows.2), channel_id=1, source_target_pairs={{0,16},{8,24},{16,0},{24,8},{1,17},{9,25},{17,1},{25,9},{2,18},{10... | collective-permute-start | bytes 1843208 | tf_op jit(solution)/shard_map/ppermute | solution.py:512
  59.0 0.0 collective-permute-done.1.far_ref
  59.0 1.5 collective-permute-start.17
  60.5 6.8 %shard_map.121 = (bf16[528,512]{1,0:T(8,128)(2,1)}, bf16[512,512]{1,0:T(8,128)(2,1)}, f32[8,512]{1,0:T(8,128)}) custom-call(bf16[512,1280]{1,0:T(8,128)(2,1)} %q_ref.6, bf16[512,1024]{1,0:T(8,128)(2,1)} %collective-permute-done.1.far_ref, bf16[512,1280]{1,0:T(8,128)(2,1)} %k_ref.9, bf16[512,1280]{1,0:T(8,128)(2,1)} %v_ref.9, ...), custom_call_target="tpu_custom_call" | custom-call | flops 858993472 | bytes 5767168 | tf_op jit(solution)/shard_map/pallas_call | solution.py:205
  67.3 0.0 collective-permute-done.10.refs_1_
  67.3 3.7 %collective-permute-done.12.refs_2_ = bf16[160,1920]{1,0:T(8,128)(2,1)} collective-permute-done((bf16[160,1920]{1,0:T(8,128)(2,1)}, bf16[160,1920]{1,0:T(8,128)(2,1)}, u32[]{:S(2)}, u32[]{:S(2)}) %collective-permute-start.12) | collective-permute-done | bytes 614432 | tf_op jit(solution)/shard_map/ppermute | solution.py:512
  71.0 3.7 %move_weights.2 = (f32[160,3840]{1,0:T(8,128)}, f32[160,3840]{1,0:T(8,128)}, bf16[160,1920]{1,0:T(8,128)(2,1)}) custom-call(f32[160,3840]{1,0:T(8,128)} %w_ref.6, f32[160,3840]{1,0:T(8,128)} %m_ref.1, f32[160,1920]{1,0:T(8,128)} %get-tuple-element.49.refs_0_, bf16[160,1920]{1,0:T(8,128)(2,1)} %collective-permute-done.10.refs_1_, ...), custom_call_target="tpu_custom_call" | custom-call | flops 6144000 | bytes 7987200 | tf_op jit(solution)/shard_map/move_weights/pallas_call | solution.py:441
  74.7 2.2 %collective-permute-start.23 = (bf16[160,1920]{1,0:T(8,128)(2,1)}, bf16[160,1920]{1,0:T(8,128)(2,1)}, u32[]{:S(2)}, u32[]{:S(2)}) collective-permute-start(bf16[160,1920]{1,0:T(8,128)(2,1)} %get-tuple-element.62.refs_0_), channel_id=1, source_target_pairs={{0,16},{8,24},{16,0},{24,8},{1,17},{9,25},{17,1},{25,9},{2,18},{10... | collective-permute-start | bytes 1843208 | tf_op jit(solution)/shard_map/ppermute | solution.py:512
  76.9 6.9 %shard_map.122 = (bf16[528,512]{1,0:T(8,128)(2,1)}, bf16[512,512]{1,0:T(8,128)(2,1)}, f32[8,512]{1,0:T(8,128)}) custom-call(bf16[512,1280]{1,0:T(8,128)(2,1)} %q_ref.6, bf16[512,1024]{1,0:T(8,128)(2,1)} %collective-permute-done.1.far_ref, bf16[512,1280]{1,0:T(8,128)(2,1)} %k_ref.9, bf16[512,1280]{1,0:T(8,128)(2,1)} %v_ref.9, ...), custom_call_target="tpu_custom_call" | custom-call | flops 858993472 | bytes 5767168 | tf_op jit(solution)/shard_map/pallas_call | solution.py:205
  83.9 0.0 collective-permute-done.13.refs_1_
  83.9 0.3 collective-permute-done.14.refs_2_
  84.2 3.7 %move_weights.3 = (f32[160,3840]{1,0:T(8,128)}, f32[160,3840]{1,0:T(8,128)}, bf16[160,1920]{1,0:T(8,128)(2,1)}) custom-call(f32[160,3840]{1,0:T(8,128)} %w_ref.6, f32[160,3840]{1,0:T(8,128)} %m_ref.1, f32[160,1920]{1,0:T(8,128)} %get-tuple-element.68.refs_0_, ...), custom_call_target="tpu_custom_call", output_to_operand_aliasing={{0}: (5, {}), {1}: (6, {})} | custom-call | flops 6144000 | bytes 7987200 | tf_op jit(solution)/shard_map/move_weights/pallas_call | solution.py:441
  87.9 2.2 %collective-permute-start.20 = (bf16[160,1920]{1,0:T(8,128)(2,1)}, bf16[160,1920]{1,0:T(8,128)(2,1)}, u32[]{:S(2)}, u32[]{:S(2)}) collective-permute-start(bf16[160,1920]{1,0:T(8,128)(2,1)} %get-tuple-element.72.refs_0_), channel_id=1, source_target_pairs={{0,16},{8,24},{16,0},{24,8},{1,17},{9,25},{17,1},{25,9},{2,18},{10... | collective-permute-start | bytes 1843208 | tf_op jit(solution)/shard_map/ppermute | solution.py:512
  90.1 4.8 %collective-permute-done.17.fk_ref.fv_ref = bf16[512,512]{1,0:T(8,128)(2,1)} collective-permute-done((bf16[512,512]{1,0:T(8,128)(2,1)}, bf16[512,512]{1,0:T(8,128)(2,1)}, u32[]{:S(2)}, u32[]{:S(2)}) %collective-permute-start.17) | collective-permute-done | bytes 524320 | tf_op jit(solution)/shard_map/ppermute | solution.py:518
  94.9 1.8 %collective-permute-start.18 = (bf16[512,512]{1,0:T(8,128)(2,1)}, bf16[512,512]{1,0:T(8,128)(2,1)}, u32[]{:S(2)}, u32[]{:S(2)}) collective-permute-start(bf16[512,512]{1,0:T(8,128)(2,1)} %collective-permute-done.17.fk_ref.fv_ref), channel_id=1, source_target_pairs={{0,8},{8,0},{16,24},{24,16},{1,9},{9,1},{17,25},{25,17},{2,10},{10... | collective-permute-start | bytes 1572872 | tf_op jit(solution)/shard_map/ppermute | solution.py:512
  96.6 1.3 collective-permute-start.16
  97.9 0.1 collective-permute-start.22
  98.0 10.0 %collective-permute-done.23.refs_2_ = bf16[160,1920]{1,0:T(8,128)(2,1)} collective-permute-done((bf16[160,1920]{1,0:T(8,128)(2,1)}, bf16[160,1920]{1,0:T(8,128)(2,1)}, u32[]{:S(2)}, u32[]{:S(2)}) %collective-permute-start.23) | collective-permute-done | bytes 614432 | tf_op jit(solution)/shard_map/ppermute | solution.py:512
  108.0 1.8 %collective-permute-start.24 = (bf16[160,1920]{1,0:T(8,128)(2,1)}, bf16[160,1920]{1,0:T(8,128)(2,1)}, u32[]{:S(2)}, u32[]{:S(2)}) collective-permute-start(bf16[160,1920]{1,0:T(8,128)(2,1)} %collective-permute-done.23.refs_2_), channel_id=1, source_target_pairs={{0,8},{8,0},{16,24},{24,16},{1,9},{9,1},{17,25},{25,17},{2,10},{10... | collective-permute-start | bytes 1843208 | tf_op jit(solution)/shard_map/ppermute | solution.py:512
  109.8 0.0 collective-permute-done.18.fpk_ref.fpv_ref
  109.8 1.5 collective-permute-start.15
  111.3 21.4 %collective-permute-done.16.refs_2_ = bf16[528,512]{1,0:T(8,128)(2,1)} collective-permute-done((bf16[528,512]{1,0:T(8,128)(2,1)}, bf16[528,512]{1,0:T(8,128)(2,1)}, u32[]{:S(2)}, u32[]{:S(2)}) %collective-permute-start.16) | collective-permute-done | bytes 540704 | tf_op jit(solution)/shard_map/ppermute | solution.py:518
  132.8 1.8 %collective-permute-start.19 = (bf16[160,1920]{1,0:T(8,128)(2,1)}, bf16[160,1920]{1,0:T(8,128)(2,1)}, u32[]{:S(2)}, u32[]{:S(2)}) collective-permute-start(bf16[160,1920]{1,0:T(8,128)(2,1)} %get-tuple-element.72.refs_0_), channel_id=1, source_target_pairs={{0,8},{8,0},{16,24},{24,16},{1,9},{9,1},{17,25},{25,17},{2,10},{10... | collective-permute-start | bytes 1843208 | tf_op jit(solution)/shard_map/ppermute | solution.py:512
  134.5 0.0 collective-permute-done.20.refs_2_
  134.5 0.0 collective-permute-start.21
  134.6 6.3 %shard_map.123.refs_3_ = bf16[512,1280]{1,0:T(8,128)(2,1)} custom-call(bf16[512,1280]{1,0:T(8,128)(2,1)} %q_ref.6, bf16[512,1280]{1,0:T(8,128)(2,1)} %k_ref.9, bf16[512,1280]{1,0:T(8,128)(2,1)} %v_ref.9, bf16[512,1280]{1,0:T(8,128)(2,1)} %collective-permute-done.8.pk_ref, bf16[512,1280]{1,0:T(8,128)(2,1)} %collective-permute-done.9.pv_ref, ...), custom_call_target="tpu_custom_call" | custom-call | flops 590558016 | bytes 2621440 | tf_op jit(solution)/shard_map/pallas_call | solution.py:205
  140.8 2.4 %shard_map.124.refs_3_ = bf16[512,1280]{1,0:T(8,128)(2,1)} custom-call(bf16[512,512]{1,0:T(8,128)(2,1)} %get-tuple-element.74.refs_0_, f32[8,512]{1,0:T(8,128)} %get-tuple-element.57.refs_1_, bf16[528,512]{1,0:T(8,128)(2,1)} %collective-permute-done.16.refs_2_, bf16[512,1280]{1,0:T(8,128)(2,1)} %shard_map.123.refs_3_), custom_call_target="tpu_custom_call", output_to_operand_aliasing={{}: (3, {})} | custom-call | flops 5368709 | bytes 2097152 | tf_op jit(solution)/shard_map/pallas_call | solution.py:205
  143.2 1.1 collective-permute-done.15.refs_2_
  144.4 2.4 %shard_map.125 = bf16[512,1280]{1,0:T(8,128)(2,1)} custom-call(bf16[512,512]{1,0:T(8,128)(2,1)} %get-tuple-element.64.refs_0_, f32[8,512]{1,0:T(8,128)} %get-tuple-element.65.refs_1_, bf16[528,512]{1,0:T(8,128)(2,1)} %collective-permute-done.15.refs_2_, bf16[512,1280]{1,0:T(8,128)(2,1)} %shard_map.124.refs_3_), custom_call_target="tpu_custom_call", output_to_operand_aliasing={{}: (3, {})} | custom-call | flops 5368709 | bytes 2097152 | tf_op jit(solution)/shard_map/pallas_call | solution.py:205
  146.8 0.0 collective-permute-done.22.refs_1_
  146.8 0.0 collective-permute-done.24.refs_3_
  146.8 4.8 %head_query.2.refs_4_ = bf16[512,1280]{1,0:T(8,128)(2,1)} custom-call(bf16[512,1280]{1,0:T(8,128)(2,1)} %q_hbm.3, bf16[160,1920]{1,0:T(8,128)(2,1)} %get-tuple-element.62.refs_0_, bf16[160,1920]{1,0:T(8,128)(2,1)} %collective-permute-done.22.refs_1_, bf16[160,1920]{1,0:T(8,128)(2,1)} %collective-permute-done.23.refs_2_, ...), custom_call_target="tpu_custom_call" | custom-call | flops 1258291200 | bytes 4000000 | tf_op jit(solution)/shard_map/head_query/pallas_call | solution.py:492
  151.6 0.0 collective-permute-done.19.refs_1_
  151.6 0.0 collective-permute-done.21.refs_3_
  151.6 4.8 %head_query.3 = bf16[512,1280]{1,0:T(8,128)(2,1)} custom-call(bf16[512,1280]{1,0:T(8,128)(2,1)} %q_hbm.3, bf16[160,1920]{1,0:T(8,128)(2,1)} %get-tuple-element.72.refs_0_, bf16[160,1920]{1,0:T(8,128)(2,1)} %collective-permute-done.19.refs_1_, bf16[160,1920]{1,0:T(8,128)(2,1)} %collective-permute-done.20.refs_2_, ...), custom_call_target="tpu_custom_call", output_to_operand_aliasing={{}: (5, {})} | custom-call | flops 1258291200 | bytes 4000000 | tf_op jit(solution)/shard_map/head_query/pallas_call | solution.py:492
  (3 shorter events, 0.0 us)
Async XLA Ops:
  2.7 15.1 %collective-permute-start = (bf16[160,1920]{1,0:T(8,128)(2,1)}, bf16[160,1920]{1,0:T(8,128)(2,1)}, u32[]{:S(2)}, u32[]{:S(2)}) collective-permute-start(bf16[160,1920]{1,0:T(8,128)(2,1)} %round_head.2.refs_3_), channel_id=1, source_target_pairs={{0,16},{8,24},{16,0},{24,8},{1,17},{9,25},{17,1},{25,9},{2,18},{10... | collective-permute-start | bytes 1843208 | tf_op jit(solution)/shard_map/ppermute | solution.py:512
  14.4 16.4 %collective-permute-start.5 = (bf16[160,1920]{1,0:T(8,128)(2,1)}, bf16[160,1920]{1,0:T(8,128)(2,1)}, u32[]{:S(2)}, u32[]{:S(2)}) collective-permute-start(bf16[160,1920]{1,0:T(8,128)(2,1)} %round_head.3.refs_3_), channel_id=1, source_target_pairs={{0,16},{8,24},{16,0},{24,8},{1,17},{9,25},{17,1},{25,9},{2,18},{10... | collective-permute-start | bytes 1843208 | tf_op jit(solution)/shard_map/ppermute | solution.py:512
  15.6 16.8 %collective-permute-start.2 = (bf16[160,1920]{1,0:T(8,128)(2,1)}, bf16[160,1920]{1,0:T(8,128)(2,1)}, u32[]{:S(2)}, u32[]{:S(2)}) collective-permute-start(bf16[160,1920]{1,0:T(8,128)(2,1)} %round_head.2.refs_3_), channel_id=1, source_target_pairs={{0,8},{8,0},{16,24},{24,16},{1,9},{9,1},{17,25},{25,17},{2,10},{10... | collective-permute-start | bytes 1843208 | tf_op jit(solution)/shard_map/ppermute | solution.py:512
  17.7 15.2 %collective-permute-start.3 = (bf16[160,1920]{1,0:T(8,128)(2,1)}, bf16[160,1920]{1,0:T(8,128)(2,1)}, u32[]{:S(2)}, u32[]{:S(2)}) collective-permute-start(bf16[160,1920]{1,0:T(8,128)(2,1)} %collective-permute-done.refs_5_), channel_id=1, source_target_pairs={{0,8},{8,0},{16,24},{24,16},{1,9},{9,1},{17,25},{25,17},{2,10},{10... | collective-permute-start | bytes 1843208 | tf_op jit(solution)/shard_map/ppermute | solution.py:512
  20.4 23.7 %collective-permute-start.4 = (bf16[160,1920]{1,0:T(8,128)(2,1)}, bf16[160,1920]{1,0:T(8,128)(2,1)}, u32[]{:S(2)}, u32[]{:S(2)}) collective-permute-start(bf16[160,1920]{1,0:T(8,128)(2,1)} %round_head.3.refs_3_), channel_id=1, source_target_pairs={{0,8},{8,0},{16,24},{24,16},{1,9},{9,1},{17,25},{25,17},{2,10},{10... | collective-permute-start | bytes 1843208 | tf_op jit(solution)/shard_map/ppermute | solution.py:512
  30.9 13.5 %collective-permute-start.6 = (bf16[160,1920]{1,0:T(8,128)(2,1)}, bf16[160,1920]{1,0:T(8,128)(2,1)}, u32[]{:S(2)}, u32[]{:S(2)}) collective-permute-start(bf16[160,1920]{1,0:T(8,128)(2,1)} %collective-permute-done.5.refs_5_), channel_id=1, source_target_pairs={{0,8},{8,0},{16,24},{24,16},{1,9},{9,1},{17,25},{25,17},{2,10},{10... | collective-permute-start | bytes 1843208 | tf_op jit(solution)/shard_map/ppermute | solution.py:512
  32.4 24.6 %collective-permute-start.8 = (bf16[512,1280]{1,0:T(8,128)(2,1)}, bf16[512,1280]{1,0:T(8,128)(2,1)}, u32[]{:S(2)}, u32[]{:S(2)}) collective-permute-start(bf16[512,1280]{1,0:T(8,128)(2,1)} %k_ref.9), channel_id=1, source_target_pairs={{0,8},{8,0},{16,24},{24,16},{1,9},{9,1},{17,25},{25,17},{2,10},{10... | collective-permute-start | bytes 3932168 | tf_op jit(solution)/shard_map/ppermute | solution.py:512
  32.4 24.9 %collective-permute-start.9 = (bf16[512,1280]{1,0:T(8,128)(2,1)}, bf16[512,1280]{1,0:T(8,128)(2,1)}, u32[]{:S(2)}, u32[]{:S(2)}) collective-permute-start(bf16[512,1280]{1,0:T(8,128)(2,1)} %v_ref.9), channel_id=1, source_target_pairs={{0,8},{8,0},{16,24},{24,16},{1,9},{9,1},{17,25},{25,17},{2,10},{10... | collective-permute-start | bytes 3932168 | tf_op jit(solution)/shard_map/ppermute | solution.py:512
  32.9 26.1 %collective-permute-start.1 = (bf16[512,1024]{1,0:T(8,128)(2,1)}, bf16[512,1024]{1,0:T(8,128)(2,1)}, u32[]{:S(2)}, u32[]{:S(2)}) collective-permute-start(bf16[512,1024]{1,0:T(8,128)(2,1)} %get-tuple-element.47), channel_id=1, source_target_pairs={{16,0},{24,8},{17,1},{25,9},{18,2},{26,10},{19,3},{27,11},{20,4},{... | collective-permute-start | bytes 3145736 | tf_op jit(solution)/shard_map/ppermute | solution.py:518
  44.1 8.6 %collective-permute-start.11 = (bf16[160,1920]{1,0:T(8,128)(2,1)}, bf16[160,1920]{1,0:T(8,128)(2,1)}, u32[]{:S(2)}, u32[]{:S(2)}) collective-permute-start(bf16[160,1920]{1,0:T(8,128)(2,1)} %get-tuple-element.61), channel_id=1, source_target_pairs={{0,8},{8,0},{16,24},{24,16},{1,9},{9,1},{17,25},{25,17},{2,10},{10... | collective-permute-start | bytes 1843208 | tf_op jit(solution)/shard_map/ppermute | solution.py:512
  52.3 2.6 %collective-permute-start.7 = (bf16[160,1920]{1,0:T(8,128)(2,1)}, bf16[160,1920]{1,0:T(8,128)(2,1)}, u32[]{:S(2)}, u32[]{:S(2)}) collective-permute-start(bf16[160,1920]{1,0:T(8,128)(2,1)} %get-tuple-element.54), channel_id=1, source_target_pairs={{0,8},{8,0},{16,24},{24,16},{1,9},{9,1},{17,25},{25,17},{2,10},{10... | collective-permute-start | bytes 1843208 | tf_op jit(solution)/shard_map/ppermute | solution.py:512
  52.6 14.7 %collective-permute-start.10 = (bf16[160,1920]{1,0:T(8,128)(2,1)}, bf16[160,1920]{1,0:T(8,128)(2,1)}, u32[]{:S(2)}, u32[]{:S(2)}) collective-permute-start(bf16[160,1920]{1,0:T(8,128)(2,1)} %get-tuple-element.59), channel_id=1, source_target_pairs={{0,8},{8,0},{16,24},{24,16},{1,9},{9,1},{17,25},{25,17},{2,10},{10... | collective-permute-start | bytes 1843208 | tf_op jit(solution)/shard_map/ppermute | solution.py:512
  55.0 16.1 %collective-permute-start.12 = (bf16[160,1920]{1,0:T(8,128)(2,1)}, bf16[160,1920]{1,0:T(8,128)(2,1)}, u32[]{:S(2)}, u32[]{:S(2)}) collective-permute-start(bf16[160,1920]{1,0:T(8,128)(2,1)} %add_rows.3), channel_id=1, source_target_pairs={{0,16},{8,24},{16,0},{24,8},{1,17},{9,25},{17,1},{25,9},{2,18},{10... | collective-permute-start | bytes 1843208 | tf_op jit(solution)/shard_map/ppermute | solution.py:512
  57.1 26.8 %collective-permute-start.13 = (bf16[160,1920]{1,0:T(8,128)(2,1)}, bf16[160,1920]{1,0:T(8,128)(2,1)}, u32[]{:S(2)}, u32[]{:S(2)}) collective-permute-start(bf16[160,1920]{1,0:T(8,128)(2,1)} %get-tuple-element.69), channel_id=1, source_target_pairs={{0,8},{8,0},{16,24},{24,16},{1,9},{9,1},{17,25},{25,17},{2,10},{10... | collective-permute-start | bytes 1843208 | tf_op jit(solution)/shard_map/ppermute | solution.py:512
  57.3 26.9 %collective-permute-start.14 = (bf16[160,1920]{1,0:T(8,128)(2,1)}, bf16[160,1920]{1,0:T(8,128)(2,1)}, u32[]{:S(2)}, u32[]{:S(2)}) collective-permute-start(bf16[160,1920]{1,0:T(8,128)(2,1)} %add_rows.2), channel_id=1, source_target_pairs={{0,16},{8,24},{16,0},{24,8},{1,17},{9,25},{17,1},{25,9},{2,18},{10... | collective-permute-start | bytes 1843208 | tf_op jit(solution)/shard_map/ppermute | solution.py:512
  59.0 35.9 %collective-permute-start.17 = (bf16[512,512]{1,0:T(8,128)(2,1)}, bf16[512,512]{1,0:T(8,128)(2,1)}, u32[]{:S(2)}, u32[]{:S(2)}) collective-permute-start(bf16[512,512]{1,0:T(8,128)(2,1)} %get-tuple-element.77), channel_id=1, source_target_pairs={{0,16},{8,24},{1,17},{9,25},{2,18},{10,26},{3,19},{11,27},{4,20},{... | collective-permute-start | bytes 1572872 | tf_op jit(solution)/shard_map/ppermute | solution.py:518
  74.7 33.3 %collective-permute-start.23 = (bf16[160,1920]{1,0:T(8,128)(2,1)}, bf16[160,1920]{1,0:T(8,128)(2,1)}, u32[]{:S(2)}, u32[]{:S(2)}) collective-permute-start(bf16[160,1920]{1,0:T(8,128)(2,1)} %get-tuple-element.62.refs_0_), channel_id=1, source_target_pairs={{0,16},{8,24},{16,0},{24,8},{1,17},{9,25},{17,1},{25,9},{2,18},{10... | collective-permute-start | bytes 1843208 | tf_op jit(solution)/shard_map/ppermute | solution.py:512
  87.9 46.6 %collective-permute-start.20 = (bf16[160,1920]{1,0:T(8,128)(2,1)}, bf16[160,1920]{1,0:T(8,128)(2,1)}, u32[]{:S(2)}, u32[]{:S(2)}) collective-permute-start(bf16[160,1920]{1,0:T(8,128)(2,1)} %get-tuple-element.72.refs_0_), channel_id=1, source_target_pairs={{0,16},{8,24},{16,0},{24,8},{1,17},{9,25},{17,1},{25,9},{2,18},{10... | collective-permute-start | bytes 1843208 | tf_op jit(solution)/shard_map/ppermute | solution.py:512
  94.9 14.9 %collective-permute-start.18 = (bf16[512,512]{1,0:T(8,128)(2,1)}, bf16[512,512]{1,0:T(8,128)(2,1)}, u32[]{:S(2)}, u32[]{:S(2)}) collective-permute-start(bf16[512,512]{1,0:T(8,128)(2,1)} %collective-permute-done.17.fk_ref.fv_ref), channel_id=1, source_target_pairs={{0,8},{8,0},{16,24},{24,16},{1,9},{9,1},{17,25},{25,17},{2,10},{10... | collective-permute-start | bytes 1572872 | tf_op jit(solution)/shard_map/ppermute | solution.py:512
  96.6 36.2 %collective-permute-start.16 = (bf16[528,512]{1,0:T(8,128)(2,1)}, bf16[528,512]{1,0:T(8,128)(2,1)}, u32[]{:S(2)}, u32[]{:S(2)}) collective-permute-start(bf16[528,512]{1,0:T(8,128)(2,1)} %get-tuple-element.75), channel_id=1, source_target_pairs={{0,16},{8,24},{1,17},{9,25},{2,18},{10,26},{3,19},{11,27},{4,20},{... | collective-permute-start | bytes 1622024 | tf_op jit(solution)/shard_map/ppermute | solution.py:518
  97.9 48.9 %collective-permute-start.22 = (bf16[160,1920]{1,0:T(8,128)(2,1)}, bf16[160,1920]{1,0:T(8,128)(2,1)}, u32[]{:S(2)}, u32[]{:S(2)}) collective-permute-start(bf16[160,1920]{1,0:T(8,128)(2,1)} %get-tuple-element.62.refs_0_), channel_id=1, source_target_pairs={{0,8},{8,0},{16,24},{24,16},{1,9},{9,1},{17,25},{25,17},{2,10},{10... | collective-permute-start | bytes 1843208 | tf_op jit(solution)/shard_map/ppermute | solution.py:512
  108.0 38.7 %collective-permute-start.24 = (bf16[160,1920]{1,0:T(8,128)(2,1)}, bf16[160,1920]{1,0:T(8,128)(2,1)}, u32[]{:S(2)}, u32[]{:S(2)}) collective-permute-start(bf16[160,1920]{1,0:T(8,128)(2,1)} %collective-permute-done.23.refs_2_), channel_id=1, source_target_pairs={{0,8},{8,0},{16,24},{24,16},{1,9},{9,1},{17,25},{25,17},{2,10},{10... | collective-permute-start | bytes 1843208 | tf_op jit(solution)/shard_map/ppermute | solution.py:512
  109.8 34.6 %collective-permute-start.15 = (bf16[528,512]{1,0:T(8,128)(2,1)}, bf16[528,512]{1,0:T(8,128)(2,1)}, u32[]{:S(2)}, u32[]{:S(2)}) collective-permute-start(bf16[528,512]{1,0:T(8,128)(2,1)} %get-tuple-element.73), channel_id=1, source_target_pairs={{0,16},{8,24},{1,17},{9,25},{2,18},{10,26},{3,19},{11,27},{4,20},{... | collective-permute-start | bytes 1622024 | tf_op jit(solution)/shard_map/ppermute | solution.py:518
  132.8 18.8 %collective-permute-start.19 = (bf16[160,1920]{1,0:T(8,128)(2,1)}, bf16[160,1920]{1,0:T(8,128)(2,1)}, u32[]{:S(2)}, u32[]{:S(2)}) collective-permute-start(bf16[160,1920]{1,0:T(8,128)(2,1)} %get-tuple-element.72.refs_0_), channel_id=1, source_target_pairs={{0,8},{8,0},{16,24},{24,16},{1,9},{9,1},{17,25},{25,17},{2,10},{10... | collective-permute-start | bytes 1843208 | tf_op jit(solution)/shard_map/ppermute | solution.py:512
  134.5 17.0 %collective-permute-start.21 = (bf16[160,1920]{1,0:T(8,128)(2,1)}, bf16[160,1920]{1,0:T(8,128)(2,1)}, u32[]{:S(2)}, u32[]{:S(2)}) collective-permute-start(bf16[160,1920]{1,0:T(8,128)(2,1)} %collective-permute-done.20.refs_2_), channel_id=1, source_target_pairs={{0,8},{8,0},{16,24},{24,16},{1,9},{9,1},{17,25},{25,17},{2,10},{10... | collective-permute-start | bytes 1843208 | tf_op jit(solution)/shard_map/ppermute | solution.py:512
